TPU v7x, 128 devices: a whole 4x4x4 slice. The times are simulated.
128 devices in a mesh: ctx: 8 (over x, core), tp: 16 (over z, y).
Axes of the slice: x: 4, y: 4, z: 4, core: 2. Of those that a mesh axis runs over, the one named last changes fastest.
Arguments:
- out_grad: bfloat16 [8192, 4096], P('ctx', 'tp'), may hold values from -6 to 6
- pre_act: bfloat16 [8192, 4096], P('ctx', 'tp'), may hold values from -6 to 6
- normed: bfloat16 [8192, 12800], P('ctx', 'tp'), may hold values from -5 to 5
- inverse_std: float32 [8192], P('ctx'), may hold values from 0.5 to 2
- w_up: bfloat16 [4096, 12800], P(None, 'tp')
- w_down: bfloat16 [4096, 4096], P(None, 'tp'), may hold values from -0.09375 to 0.09375
- ln_gain: float32 [12800], P('tp'), may hold values from 0.25 to 1.75
- owner_map: int32 [8, 4], P('ctx'), may hold values from 0 to 15, as said below
Outputs:
- grad_w2: float32 [4096, 4096], P('ctx', 'tp')
- grad_w1: float32 [4096, 12800], P('ctx', 'tp')
- grad_b1: float32 [4096], P('tp')
- grad_b2: float32 [4096], P('tp')
- ln_grads: float32 [2, 12800], P(None, 'tp')
- vit_grad: bfloat16 [32768, 12800], P(('ctx', 'tp'))
Inputs may be any that keep to these rules, and one draw needn't show every extreme that they name: `owner_map`: within each context shard, every encoder rank owns at most 1 of the 4 images, and some rank owns exactly 1.
All inputs are finite; a program needn't handle non-finite values.
Results may differ from a plain program's by a relative error of at most 0.007.
Values may be sent and summed in bfloat16 or wider, within the bound.
A program may use at most 192 MiB of HBM per device.

v0:
```python
import math

import jax
import jax.numpy as jnp
from jax import lax
from jax.sharding import PartitionSpec as P


def gelu_parts(linear):
    normal_cdf = 0.5 * (1.0 + jax.scipy.special.erf(linear * 2.0 ** (-0.5)))
    density = jnp.exp(-0.5 * linear * linear) * (2.0 * math.pi) ** (-0.5)
    return (linear * normal_cdf, normal_cdf + linear * density)


def slot_numbers(owners, capacity):
    position = jnp.arange(owners.shape[0])
    earlier = (owners[None, :] == owners[:, None]) & (position[None, :] < position[:, None])
    return owners * capacity + jnp.sum(earlier.astype(jnp.int32), axis=1)


def row_product(left, right):
    return lax.dot_general(
        left, right, (((0,), (0,)), ((), ())), preferred_element_type=jnp.float32
    )


def per_device(out_grad, pre_act, normed, inverse_std, w_up, w_down, ln_gain, owner_map):
    ctx_count = lax.axis_size("ctx")
    tp_count = lax.axis_size("tp")
    row_count = out_grad.shape[0]
    grad_scale = float(row_count * ctx_count) ** (-0.5)
    gelu_value, gelu_slope = gelu_parts(pre_act.astype(jnp.float32))
    hidden = gelu_value.astype(jnp.bfloat16)
    full_grad = lax.all_gather(out_grad, "tp", axis=1, tiled=True)
    back_hidden = jnp.dot(full_grad, w_down, preferred_element_type=jnp.float32)
    back_part = (back_hidden * gelu_slope).astype(jnp.bfloat16)
    columns = full_grad
    grad_w2 = (
        lax.psum_scatter(row_product(columns, hidden), "ctx", scatter_dimension=0, tiled=True)
        * grad_scale
    )
    bias_down, bias_up = lax.psum(
        (
            jnp.sum(out_grad.astype(jnp.float32), axis=0),
            jnp.sum(back_part.astype(jnp.float32), axis=0),
        ),
        "ctx",
    )
    back_linear = lax.all_gather(back_part, "tp", axis=1, tiled=True)
    columns = back_linear
    grad_w1 = (
        lax.psum_scatter(row_product(columns, normed), "ctx", scatter_dimension=0, tiled=True)
        * grad_scale
    )
    norm_grad = jnp.dot(back_linear, w_up, preferred_element_type=jnp.float32)
    features = normed.astype(jnp.float32)
    gained = ln_gain[None, :] * norm_grad
    sum_first, sum_second = lax.psum(
        (jnp.sum(gained, axis=-1), jnp.sum(gained * features, axis=-1)), "tp"
    )
    full_width = float(normed.shape[1] * tp_count)
    mean_first = sum_first / full_width
    mean_second = sum_second / full_width
    visual = (
        inverse_std[:, None] * (gained - mean_first[:, None] - features * mean_second[:, None])
    ).astype(jnp.bfloat16)
    gain_sum, bias_sum = lax.psum(
        (jnp.sum(norm_grad * features, axis=0), jnp.sum(norm_grad, axis=0)), "ctx"
    )
    ln_grads = jnp.stack([gain_sum, bias_sum]) * grad_scale
    owners = owner_map[0]
    image_count = owners.shape[0]
    image_rows = row_count // image_count
    capacity = max(1, 2 * image_count // tp_count)
    slot_of = slot_numbers(owners, capacity)
    slot_ids = jnp.arange(tp_count * capacity)
    matches = slot_of[None, :] == slot_ids[:, None]
    present = jnp.any(matches, axis=1)
    source_image = jnp.sum(jnp.where(matches, jnp.arange(image_count)[None, :], 0), axis=1)
    images = visual.reshape(image_count, image_rows, visual.shape[1])
    picked = jnp.take(images, source_image, axis=0)
    outgoing = jnp.where(present[:, None, None], picked, jnp.zeros((), jnp.bfloat16)).reshape(
        tp_count * capacity * image_rows, visual.shape[1]
    )
    vit_grad = lax.all_to_all(outgoing, "tp", split_axis=0, concat_axis=1, tiled=True)
    return (grad_w2, grad_w1, bias_up * grad_scale, bias_down * grad_scale, ln_grads, vit_grad)


def solution(mesh):
    return jax.shard_map(
        per_device,
        mesh=mesh,
        in_specs=(
            P("ctx", "tp"),
            P("ctx", "tp"),
            P("ctx", "tp"),
            P("ctx"),
            P(None, "tp"),
            P(None, "tp"),
            P("tp"),
            P("ctx", None),
        ),
        out_specs=(
            P("ctx", "tp"),
            P("ctx", "tp"),
            P("tp"),
            P("tp"),
            P(None, "tp"),
            P(("ctx", "tp"), None),
        ),
        check_vma=False,
    )
```

profile of v0, /device:TPU:0, one launch (start us, length us, event | category | flops | bytes accessed | tf_op | source)
XLA Modules:
  0.0 356.5 jit_solution(15268767459479100883)
XLA Ops:
  7.2 0.0 copy-start
  7.2 0.0 all-gather.3.cloned.1.call-start
  7.2 0.7 all-gather.3.cloned.1.call-update
  7.9 0.0 copy-start.4
  7.9 0.0 all-gather.5.cloned.1.call-start
  8.0 83.2 %all-gather.3.cloned.1.call-done = bf16[1024,4096]{1,0:T(8,128)(2,1)} async-done(((bf16[1024,256]{1,0:T(8,128)(2,1)}), bf16[1024,4096]{1,0:T(8,128)(2,1)}) %all-gather.3.cloned.1.call-update) | async-done | bytes 8388624 | tf_op jit(solution)/shard_map/all_gather | solution.py:34
  91.2 0.0 copy-done
  91.2 6.8 %convert_reduce_fusion.1 = (f32[256]{0:T(256)S(1)}, bf16[1024,256]{1,0:T(8,128)(2,1)}) fusion(bf16[1024,256]{1,0:T(8,128)(2,1)} %param.9, bf16[1024,4096]{1,0:T(8,128)(2,1)} %all-gather.3.cloned.1.call-done, bf16[4096,256]{1,0:T(8,128)(2,1)S(1)} %copy-done), kind=kOutput, calls=%fused_computation.28 | convolution fusion | flops 2150891264 | bytes 11535360 | tf_op jit(solution)/shard_map/dot_general | solution.py:35
  97.9 0.0 all-gather.5.cloned.1.call-update
  97.9 0.0 reduce-scatter.3.cloned.1.call-start
  98.0 0.0 copy-done.4
  98.0 7.8 %convolution_bitcast_fusion = f32[4096,256]{0,1:T(8,128)} fusion(bf16[1024,4096]{1,0:T(8,128)(2,1)} %all-gather.3.cloned.1.call-done, bf16[1024,256]{1,0:T(8,128)(2,1)S(1)} %copy-done.4), kind=kOutput, calls=%fused_computation.2 | convolution fusion | flops 2149056512 | bytes 13107200 | tf_op jit(solution)/shard_map/dot_general | solution.py:22
  105.8 0.0 copy-start.3
  105.8 0.0 reduce-scatter.3.cloned.1.call-update
  105.9 0.0 reduce-scatter.5.cloned.1.call-start
  105.9 69.9 %all-gather.5.cloned.1.call-done = bf16[1024,4096]{1,0:T(8,128)(2,1)} async-done(((bf16[1024,256]{1,0:T(8,128)(2,1)}), bf16[1024,4096]{1,0:T(8,128)(2,1)}) %all-gather.5.cloned.1.call-update) | async-done | bytes 8388624 | tf_op jit(solution)/shard_map/all_gather | solution.py:49
  175.9 0.0 copy-done.3
  175.9 13.2 %fusion.19 = f32[4096,800]{0,1:T(8,128)} fusion(bf16[1024,800]{0,1:T(8,128)(2,1)S(1)} %copy-done.3, bf16[1024,4096]{1,0:T(8,128)(2,1)} %all-gather.5.cloned.1.call-done), kind=kOutput, calls=%fused_computation.49 | convolution fusion | flops 6710886400 | bytes 23134208 | tf_op jit(solution)/shard_map/dot_general | solution.py:22
  189.0 0.0 copy-start.5
  189.0 0.0 reduce-scatter.5.cloned.1.call-update
  189.1 0.6 copy-done.7
  189.7 0.2 convert_reduce_fusion.2
  189.9 0.1 select_reduce_fusion
  190.0 0.1 fusion.14
  190.1 0.0 copy-done.5
  190.1 0.0 copy-start.6
  190.1 13.3 %fusion.1 = (f32[1024]{0:T(1024)S(1)}, f32[800]{0:T(1024)S(1)}, f32[1024]{0:T(1024)S(1)}, f32[800]{0:T(1024)S(1)}, f32[1024,800]{0,1:T(8,128)}) fusion(bf16[1024,800]{0,1:T(8,128)(2,1)S(1)} %copy-done.3, f32[800]{0:T(1024)S(1)} %copy-done.5, bf16[1024,4096]{1,0:T(8,128)(2,1)} %all-gather.5.cloned.1.call-done, bf16[4096,800]{0,1:T(8,128)(2,1)} %param.12), kind=kOutput, calls=%fused_computation.7 | convolution fusion | flops 6717435904 | bytes 19875200 | tf_op jit(solution)/shard_map/dot_general | solution.py:55
  203.5 38.6 %all-reduce = (f32[1024]{0:T(1024)S(1)}, f32[1024]{0:T(1024)S(1)}) all-reduce(f32[1024]{0:T(1024)S(1)} %get-tuple-element.24, f32[1024]{0:T(1024)S(1)} %get-tuple-element.26), channel_id=1, replica_groups=mesh['ctx'=8,'tp'=16] {'tp'}, use_global_device_ids=true, to_apply=%region_16.17 | all-reduce | flops 2048 | bytes 16384 | tf_op jit(solution)/shard_map/psum | solution.py:58
  242.1 0.0 copy-done.6
  242.1 2.8 fusion.4
  244.9 0.1 copy.24
  245.0 3.8 %gather_fusion = bf16[16,256,800]{1,2,0:T(8,128)(2,1)} fusion(bf16[4,256,800]{1,2,0:T(8,128)(2,1)S(1)} %bitcast.27, s32[1024]{0:T(1024)S(1)} %pad_clamp_fusion), kind=kCustom, calls=%fused_computation | custom fusion | bytes 13107264 | tf_op jit(solution)/shard_map/jit(_take)/gather | solution.py:81
  248.8 6.6 %select_select_fusion = bf16[16,256,800]{1,2,0:T(8,128)(2,1)} fusion(bf16[16,256,800]{1,2,0:T(8,128)(2,1)} %gather_fusion, pred[16]{0:T(512)(128)(4,1)S(1)} %compare_and_fusion, pred[16]{0:T(512)(128)(4,1)S(1)} %fusion.14), kind=kLoop, calls=%fused_computation.1 | loop fusion | flops 6553600 | bytes 13107232 | tf_op jit(solution)/shard_map/jit(_where)/select_n | solution.py:82
  255.3 0.0 copy-start.2
  255.3 4.8 %all-to-all-start = ((bf16[16,256,800]{1,2,0:T(8,128)(2,1)}), bf16[16,256,800]{1,2,0:T(8,128)(2,1)}, u32[]{:S(2)}, u32[]{:S(2)}) async-start(bf16[16,256,800]{1,2,0:T(8,128)(2,1)} %select_select_fusion), calls=%async_computation.2 | async-start | bytes 13107200 | tf_op jit(solution)/shard_map/all_to_all | solution.py:85
  260.2 0.0 copy-done.2
  260.2 0.2 convert_reduce_fusion
  260.4 0.0 reduce-scatter.3.cloned.1.call-done
  260.4 1.1 broadcast_multiply_fusion.1
  261.5 1.0 copy.20
  262.5 14.5 %all-reduce.1 = (f32[256]{0:T(256)S(1)}, f32[256]{0:T(256)S(1)}, f32[1,800]{1,0:T(1,128)S(1)}, f32[1,800]{1,0:T(1,128)S(1)}) all-reduce(f32[256]{0:T(256)S(1)} %get-tuple-element.34, f32[256]{0:T(256)S(1)} %convert_reduce_fusion, f32[1,800]{1,0:T(1,128)S(1)} %stack.10, f32[1,800]{1,0:T(1,128)S(1)} %stack.9), channel_id=1, replica_groups=mesh['ctx'=8,'tp'=16] {'ctx'}, use_global_device_ids=true, to_apply=%region_3.0 | all-reduce | flops 2112 | bytes 16896 | tf_op jit(solution)/shard_map/psum | solution.py:42
  277.0 0.6 maximum_multiply_fusion
  277.6 0.6 broadcast_multiply_fusion.4
  278.2 59.2 %all-to-all-done = bf16[16,256,800]{1,2,0:T(8,128)(2,1)} async-done(((bf16[16,256,800]{1,2,0:T(8,128)(2,1)}), bf16[16,256,800]{1,2,0:T(8,128)(2,1)}, u32[]{:S(2)}, u32[]{:S(2)}) %all-to-all-start) | async-done | bytes 6553632 | tf_op jit(solution)/shard_map/all_to_all | solution.py:85
  337.4 0.0 copy-start.1
  337.4 9.7 %copy.21 = bf16[256,12800]{1,0:T(8,128)(2,1)} copy(bf16[256,12800]{0,1:T(8,128)(2,1)} %bitcast.7) | data formatting | bytes 13107200
  347.1 2.8 broadcast_multiply_fusion
  349.9 0.0 copy-done.1
  (9 shorter events, 0.0 us)
Async XLA Ops:
  7.2 84.0 %copy-start = (bf16[4096,256]{1,0:T(8,128)(2,1)S(1)}, bf16[4096,256]{1,0:T(8,128)(2,1)}, u32[]{:S(2)}) copy-start(bf16[4096,256]{1,0:T(8,128)(2,1)} %param.13) | copy-start | bytes 6291460
  7.2 84.0 %all-gather.3.cloned.1.call-start = ((), (), s32[]{:S(2)}) async-start(), calls=%async_computation.3 | async-start | bytes 8912896 | tf_op jit(solution)/shard_map/all_gather | solution.py:34
  7.9 90.1 %copy-start.4 = (bf16[1024,256]{1,0:T(8,128)(2,1)S(1)}, bf16[1024,256]{1,0:T(8,128)(2,1)}, u32[]{:S(2)}) copy-start(bf16[1024,256]{1,0:T(8,128)(2,1)} %param.9) | copy-start | bytes 1572868
  7.9 167.9 %all-gather.5.cloned.1.call-start = ((), (), s32[]{:S(2)}) async-start(), calls=%async_computation.5 | async-start | bytes 8912896 | tf_op jit(solution)/shard_map/all_gather | solution.py:49
  97.9 162.4 %reduce-scatter.3.cloned.1.call-start = ((), (), s32[]{:S(2)}) async-start(), calls=%async_computation.4 | async-start | bytes 4718592 | tf_op jit(solution)/shard_map/reduce_scatter | solution.py:39
  105.8 70.0 %copy-start.3 = (bf16[1024,800]{0,1:T(8,128)(2,1)S(1)}, bf16[1024,800]{0,1:T(8,128)(2,1)}, u32[]{:S(2)}) copy-start(bf16[1024,800]{0,1:T(8,128)(2,1)} %param.10) | copy-start | bytes 4915204
  105.9 241.3 %reduce-scatter.5.cloned.1.call-start = ((), (), s32[]{:S(2)}) async-start(), calls=%async_computation.6 | async-start | bytes 14745600 | tf_op jit(solution)/shard_map/reduce_scatter | solution.py:52
  189.0 0.7 copy-start.7
  189.0 1.0 copy-start.5
  190.1 52.0 %copy-start.6 = (f32[1024]{0:T(1024)S(1)}, f32[1024]{0:T(1024)}, u32[]{:S(2)}) copy-start(f32[1024]{0:T(1024)} %param.11) | copy-start | bytes 12292
  255.3 4.8 %copy-start.2 = (bf16[1024,256]{1,0:T(8,128)(2,1)S(1)}, bf16[1024,256]{1,0:T(8,128)(2,1)}, u32[]{:S(2)}) copy-start(bf16[1024,256]{1,0:T(8,128)(2,1)} %param.8) | copy-start | bytes 1572868
  255.3 82.1 %all-to-all-start = ((bf16[16,256,800]{1,2,0:T(8,128)(2,1)}), bf16[16,256,800]{1,2,0:T(8,128)(2,1)}, u32[]{:S(2)}, u32[]{:S(2)}) async-start(bf16[16,256,800]{1,2,0:T(8,128)(2,1)} %select_select_fusion), calls=%async_computation.2 | async-start | bytes 13107200 | tf_op jit(solution)/shard_map/all_to_all | solution.py:85
  337.4 12.5 %copy-start.1 = (bf16[4096,256]{1,0:T(8,128)(2,1)S(1)}, bf16[4096,256]{1,0:T(8,128)(2,1)}, u32[]{:S(2)}) copy-start(bf16[4096,256]{1,0:T(8,128)(2,1)} %param.13) | copy-start | bytes 6291460
Sparse Core Ops, SparseCore 0:
  10.1 80.9 all-gather.2
  98.1 77.7 all-gather.4
  178.3 37.0 reduce-scatter.2
  217.6 74.3 reduce-scatter.4
where the time goes:
time: 357 us; the launch traced here: 356 us
  waiting for transfers between devices  213 us (60%)
  blocking collectives  53.1 us (15%)
  matrix products  41.1 us (12%)
  local copies, waits for them, and re-layouts  15.2 us (4%)
  other arithmetic  15 us (4%)
  between operations  13.9 us (4%)
  starting transfers between devices  4.99 us (1%)
    all_gather x1, waiting for transfers between devices, per_device(): full_grad = lax.all_gather(out_grad, 'tp', axis=1, tiled=True)  83.2 us
    all_gather x1, waiting for transfers between devices, per_device(): back_linear = lax.all_gather(back_part, 'tp', axis=1, tiled=True)  69.9 us
    all_to_all x1, waiting for transfers between devices, per_device(): lax.all_to_all(outgoing, 'tp', split_axis=0, concat_axis=1, tiled=True)  59.2 us
    psum x1, blocking collectives, per_device(): lax.psum((jnp.sum(gained, axis=-1), jnp.sum(gained * features, axis=-1)),...  38.6 us
    dot_general x2, matrix products, row_product(): lax.dot_general(left, right, (((0,), (0,)), ((), ())), preferred_element_...  21 us
    psum x1, blocking collectives, per_device(): lax.psum((jnp.sum(out_grad.astype(jnp.float32), axis=0), jnp.sum(back_par...  14.5 us
    dot_general x1, matrix products, per_device(): norm_grad = jnp.dot(back_linear, w_up, preferred_element_type=jnp.float32)  13.3 us
    unnamed x18, local copies, waits for them, and re-layouts  11.3 us
  transfers between devices with their start and end apart: 5, of which 3 were waited for; matrix products, arithmetic and copies ran while one was open for 17% of the time, Pallas kernels for 0%

commit v1 on v0

v1 whole, which is shorter than its diff:
```python
import math

import jax
import jax.numpy as jnp
from jax import lax
from jax.experimental import pallas as pl
from jax.experimental.pallas import tpu as pltpu
from jax.sharding import PartitionSpec as P

MESH = pl.DeviceIdType.MESH
SIDE = 4
TP = SIDE * SIDE
RINGS = 4
SUBS = 2
VMEM_LIMIT = 60 * 2**20


def gelu_parts(linear):
    normal_cdf = 0.5 * (1.0 + lax.erf(linear * 2.0 ** (-0.5)))
    density = jnp.exp(-0.5 * linear * linear) * (2.0 * math.pi) ** (-0.5)
    return (linear * normal_cdf, normal_cdf + linear * density)


def dot(left, right):
    return lax.dot_general(
        left, right, (((1,), (0,)), ((), ())), preferred_element_type=jnp.float32
    )


def row_product(left, right):
    return lax.dot_general(
        left, right, (((0,), (0,)), ((), ())), preferred_element_type=jnp.float32
    )


class Rings:
    def __init__(self, me):
        z, y = me // SIDE, me % SIDE
        b = (y + z) % SIDE
        last, first = b // 3, (3 - b) // 3

        def at(zz, yy):
            return ((zz + SIDE) % SIDE) * SIDE + (yy + SIDE) % SIDE

        self.positions = (z * SIDE + b, y * SIDE + b)
        self.targets = (
            at(z + last, y + 1 - last),
            at(z - first, y - 1 + first),
            at(z + 1 - last, y + last),
            at(z - 1 + first, y - first),
        )

    def origin(self, ring, step):
        signed = step if ring % 2 else TP - step
        q = (self.positions[ring // 2] + signed) % TP
        major, minor = q // SIDE, (q % SIDE - q // SIDE + SIDE) % SIDE
        return major * SIDE + minor if ring < 2 else minor * SIDE + major


def greet(targets):
    barrier = pltpu.get_barrier_semaphore()
    for target in targets:
        pl.semaphore_signal(barrier, inc=1, device_id={"tp": target}, device_id_type=MESH)
    pl.semaphore_wait(barrier, len(targets))


def ring_gather(prepare, rings, full_ref, send_sem, recv_sem, consume):
    quarter = full_ref.shape[1] // RINGS
    part = quarter // SUBS

    def copy(ring, step, sub, at):
        spot = full_ref.at[rings.origin(ring, at), pl.ds(ring * quarter + sub * part, part)]
        return pltpu.make_async_remote_copy(
            src_ref=spot,
            dst_ref=spot,
            send_sem=send_sem.at[ring, step, sub],
            recv_sem=recv_sem.at[ring, step, sub],
            device_id={"tp": rings.targets[ring]},
            device_id_type=MESH,
        )

    for sub in range(SUBS):
        for ring in range(RINGS):
            copy(ring, 0, sub, 0).start()
    prepare()

    def hop(step, carry):
        for sub in range(SUBS):
            for ring in range(RINGS):
                copy(ring, step - 1, sub, step).wait_recv()
                copy(ring, step, sub, step).start()
            for ring in range(RINGS // SUBS * sub, RINGS // SUBS * (sub + 1)):
                consume(rings.origin(ring, step - 1), ring)
        return carry

    lax.fori_loop(1, TP - 1, hop, 0)
    for ring in range(RINGS):
        consume(rings.origin(ring, TP - 2), ring)
    for ring in range(RINGS):
        for sub in range(SUBS):
            copy(ring, TP - 2, sub, TP - 1).wait_recv()
        consume(rings.origin(ring, TP - 1), ring)

    def drain(step, carry):
        for sub in range(SUBS):
            for ring in range(RINGS):
                copy(ring, step, sub, step).wait_send()
        return carry

    lax.fori_loop(0, TP - 1, drain, 0)


def down_kernel(
    grad_ref, w_hbm, pre_ref, part_ref, gw2_ref, full_ref, w_ref, total, gw2, hidden, slope, w_sem, send_sem, recv_sem
):
    me = lax.axis_index("tp")
    rings = Rings(me)
    load = pltpu.make_async_copy(w_hbm, w_ref, w_sem)
    load.start()
    full_ref[me] = grad_ref[...]
    greet(rings.targets)
    rows_all, width = grad_ref.shape
    quarter = rows_all // RINGS

    def prepare():
        def rows_of(i, carry):
            rows = pl.ds(pl.multiple_of(i * 64, 64), 64)
            value, steep = gelu_parts(pre_ref[rows, :].astype(jnp.float32))
            hidden[rows, :] = value.astype(jnp.bfloat16)
            slope[rows, :] = steep
            return carry

        lax.fori_loop(0, rows_all // 64, rows_of, 0)
        total[...] = jnp.zeros_like(total)
        gw2[...] = jnp.zeros_like(gw2)
        load.wait()

    def consume(origin, ring):
        rows = pl.ds(ring * quarter, quarter)
        features = pl.ds(pl.multiple_of(origin * width, width), width)
        block = full_ref[origin, rows, :]
        total[rows, :] += dot(block, w_ref[features, :])
        gw2[features, :] += row_product(block, hidden[rows, :])

    ring_gather(prepare, rings, full_ref, send_sem, recv_sem, consume)
    part_ref[...] = (total[...] * slope[...]).astype(jnp.bfloat16)
    gw2_ref[...] = gw2[...].astype(jnp.bfloat16)


def down(out_grad, w_down, pre_act):
    rows, width = out_grad.shape
    features, hid = w_down.shape
    vmem = pl.BlockSpec(memory_space=pltpu.VMEM)
    return pl.pallas_call(
        down_kernel,
        out_shape=(
            jax.ShapeDtypeStruct((rows, hid), jnp.bfloat16),
            jax.ShapeDtypeStruct((features, hid), jnp.bfloat16),
        ),
        in_specs=[vmem, pl.BlockSpec(memory_space=pl.ANY), vmem],
        out_specs=(vmem, vmem),
        scratch_shapes=[
            pltpu.VMEM((TP, rows, width), jnp.bfloat16),
            pltpu.VMEM((features, hid), jnp.bfloat16),
            pltpu.VMEM((rows, hid), jnp.float32),
            pltpu.VMEM((features, hid), jnp.float32),
            pltpu.VMEM((rows, hid), jnp.bfloat16),
            pltpu.VMEM((rows, hid), jnp.float32),
            pltpu.SemaphoreType.DMA,
            pltpu.SemaphoreType.DMA((RINGS, TP - 1, SUBS)),
            pltpu.SemaphoreType.DMA((RINGS, TP - 1, SUBS)),
        ],
        compiler_params=pltpu.CompilerParams(
            collective_id=0, has_side_effects=True, vmem_limit_bytes=VMEM_LIMIT
        ),
        name="down_ring",
    )(out_grad, w_down, pre_act)


def up_kernel(
    part_ref, w_hbm, normed_hbm, norm_ref, gw1_ref, full_ref, w_ref, normed_ref, gw1, w_sem, send_sem, recv_sem
):
    me = lax.axis_index("tp")
    rings = Rings(me)
    loads = [
        pltpu.make_async_copy(w_hbm, w_ref, w_sem.at[0]),
        pltpu.make_async_copy(normed_hbm, normed_ref, w_sem.at[1]),
    ]
    for load in loads:
        load.start()
    full_ref[me] = part_ref[...]
    greet(rings.targets)
    rows_all, width = part_ref.shape
    quarter = rows_all // RINGS

    def prepare():
        norm_ref[...] = jnp.zeros_like(norm_ref)
        gw1[...] = jnp.zeros_like(gw1)
        for load in loads:
            load.wait()

    def consume(origin, ring):
        rows = pl.ds(ring * quarter, quarter)
        units = pl.ds(pl.multiple_of(origin * width, width), width)
        block = full_ref[origin, rows, :]
        norm_ref[rows, :] += dot(block, w_ref[units, :])
        gw1[units, :] += row_product(block, normed_ref[rows, :])

    ring_gather(prepare, rings, full_ref, send_sem, recv_sem, consume)
    gw1_ref[...] = gw1[...].astype(jnp.bfloat16)


def up(back_part, w_up, normed):
    rows, width = back_part.shape
    units, channels = w_up.shape
    vmem = pl.BlockSpec(memory_space=pltpu.VMEM)
    anywhere = pl.BlockSpec(memory_space=pl.ANY)
    return pl.pallas_call(
        up_kernel,
        out_shape=(
            jax.ShapeDtypeStruct((rows, channels), jnp.float32),
            jax.ShapeDtypeStruct((units, channels), jnp.bfloat16),
        ),
        in_specs=[vmem, anywhere, anywhere],
        out_specs=(vmem, vmem),
        scratch_shapes=[
            pltpu.VMEM((TP, rows, width), jnp.bfloat16),
            pltpu.VMEM((units, channels), jnp.bfloat16),
            pltpu.VMEM((rows, channels), jnp.bfloat16),
            pltpu.VMEM((units, channels), jnp.float32),
            pltpu.SemaphoreType.DMA((2,)),
            pltpu.SemaphoreType.DMA((RINGS, TP - 1, SUBS)),
            pltpu.SemaphoreType.DMA((RINGS, TP - 1, SUBS)),
        ],
        compiler_params=pltpu.CompilerParams(
            collective_id=1, has_side_effects=True, vmem_limit_bytes=VMEM_LIMIT
        ),
        name="up_ring",
    )(back_part, w_up, normed)


def slot_numbers(owners, capacity):
    position = jnp.arange(owners.shape[0])
    earlier = (owners[None, :] == owners[:, None]) & (position[None, :] < position[:, None])
    return owners * capacity + jnp.sum(earlier.astype(jnp.int32), axis=1)


def per_device(out_grad, pre_act, normed, inverse_std, w_up, w_down, ln_gain, owner_map):
    ctx_count = lax.axis_size("ctx")
    tp_count = lax.axis_size("tp")
    row_count = out_grad.shape[0]
    grad_scale = float(row_count * ctx_count) ** (-0.5)
    back_part, gw2 = down(out_grad, w_down, pre_act)
    grad_w2 = (
        lax.psum_scatter(gw2, "ctx", scatter_dimension=0, tiled=True).astype(jnp.float32) * grad_scale
    )
    norm_grad, gw1 = up(back_part, w_up, normed)
    grad_w1 = (
        lax.psum_scatter(gw1, "ctx", scatter_dimension=0, tiled=True).astype(jnp.float32) * grad_scale
    )
    features = normed.astype(jnp.float32)
    gained = ln_gain[None, :] * norm_grad
    sum_first, sum_second = lax.psum(
        (jnp.sum(gained, axis=-1), jnp.sum(gained * features, axis=-1)), "tp"
    )
    full_width = float(normed.shape[1] * tp_count)
    mean_first = sum_first / full_width
    mean_second = sum_second / full_width
    visual = (
        inverse_std[:, None] * (gained - mean_first[:, None] - features * mean_second[:, None])
    ).astype(jnp.bfloat16)
    bias_down, bias_up, gain_sum, bias_sum = lax.psum(
        (
            jnp.sum(out_grad.astype(jnp.float32), axis=0),
            jnp.sum(back_part.astype(jnp.float32), axis=0),
            jnp.sum(norm_grad * features, axis=0),
            jnp.sum(norm_grad, axis=0),
        ),
        "ctx",
    )
    ln_grads = jnp.stack([gain_sum, bias_sum]) * grad_scale
    owners = owner_map[0]
    image_count = owners.shape[0]
    image_rows = row_count // image_count
    slot_of = slot_numbers(owners, 1)
    images = visual.reshape(image_count, image_rows, visual.shape[1])
    slot_ids = jnp.arange(tp_count)[:, None, None]
    outgoing = jnp.zeros((), jnp.bfloat16)
    for i in range(image_count):
        outgoing = jnp.where(slot_ids == slot_of[i], images[i][None], outgoing)
    outgoing = outgoing.reshape(tp_count * image_rows, visual.shape[1])
    vit_grad = lax.all_to_all(outgoing, "tp", split_axis=0, concat_axis=1, tiled=True)
    return (grad_w2, grad_w1, bias_up * grad_scale, bias_down * grad_scale, ln_grads, vit_grad)


def solution(mesh):
    return jax.shard_map(
        per_device,
        mesh=mesh,
        in_specs=(
            P("ctx", "tp"),
            P("ctx", "tp"),
            P("ctx", "tp"),
            P("ctx"),
            P(None, "tp"),
            P(None, "tp"),
            P("tp"),
            P("ctx", None),
        ),
        out_specs=(
            P("ctx", "tp"),
            P("ctx", "tp"),
            P("tp"),
            P("tp"),
            P(None, "tp"),
            P(("ctx", "tp"), None),
        ),
        check_vma=False,
    )
```

time: 357 us -> 318 us (0.89)
  waiting for transfers between devices: 213 us -> 39.8 us
  Pallas kernels: 0 us -> 145 us
  matrix products: 41.1 us -> 0 us
  blocking collectives: 53.1 us -> 67.5 us
  local copies, waits for them, and re-layouts: 15.2 us -> 27.2 us
    all_gather x2 -> x0, waiting for transfers between devices: 153 us -> none  [the longest x1 83.2 us: per_device(): full_grad = lax.all_gather(out_grad, 'tp', axis=1, tiled=True)]
    pallas_call x0 -> x2, Pallas kernels: none -> 145 us  [the longest x1 72.6 us: up(): pl.pallas_call(up_kernel, out_shape=(jax.ShapeDtypeStruct((rows, channels...]
    dot_general x4 -> x0, matrix products: 41.1 us -> none  [the longest x2 21 us: row_product(): lax.dot_general(left, right, (((0,), (0,)), ((), ())), preferred_element_...]
    all_to_all x1, waiting for transfers between devices: 59.2 us -> 39.8 us  [per_device(): lax.all_to_all(outgoing, 'tp', split_axis=0, concat_axis=1, tiled=True)]
    psum x1, blocking collectives: 38.6 us -> 53.8 us  [per_device(): lax.psum((jnp.sum(gained, axis=-1), jnp.sum(gained * features, axis=-1)),...]
    unnamed x18, local copies, waits for them, and re-layouts: 11.3 us -> 25.7 us
    gather x1 -> x0, local copies, waits for them, and re-layouts: 3.76 us -> none  [per_device(): picked = jnp.take(images, source_image, axis=0)]
  transfers between devices with their start and end apart: 5 -> 3, of which waited for: 3 -> 1; matrix products, arithmetic and copies ran while one was open for 17% -> 13% of each run, Pallas kernels for 0% -> 23%
where the time goes in v1:
time: 318 us; the launch traced here: 317 us
  Pallas kernels  145 us (46%)
  blocking collectives  67.5 us (21%)
  waiting for transfers between devices  39.8 us (13%)
  local copies, waits for them, and re-layouts  27.2 us (9%)
  other arithmetic  17.8 us (6%)
  between operations  14.2 us (4%)
  starting transfers between devices  5.03 us (2%)
    pallas_call x1, Pallas kernels, up(): pl.pallas_call(up_kernel, out_shape=(jax.ShapeDtypeStruct((rows, channels...  72.6 us
    pallas_call x1, Pallas kernels, down(): pl.pallas_call(down_kernel, out_shape=(jax.ShapeDtypeStruct((rows, hid),...  72.3 us
    psum x1, blocking collectives, per_device(): lax.psum((jnp.sum(gained, axis=-1), jnp.sum(gained * features, axis=-1)),...  53.8 us
    all_to_all x1, waiting for transfers between devices, per_device(): lax.all_to_all(outgoing, 'tp', split_axis=0, concat_axis=1, tiled=True)  39.8 us
    unnamed x18, local copies, waits for them, and re-layouts  25.7 us
    psum x1, blocking collectives, per_device(): lax.psum((jnp.sum(out_grad.astype(jnp.float32), axis=0), jnp.sum(back_par...  13.7 us
  transfers between devices with their start and end apart: 3, of which 1 were waited for; matrix products, arithmetic and copies ran while one was open for 13% of the time, Pallas kernels for 23%

profile of v1, /device:TPU:0, one launch (start us, length us, event | category | flops | bytes accessed | tf_op | source)
XLA Modules:
  0.0 316.6 jit_solution(2801930618186491134)
XLA Ops:
  7.2 0.0 reduce-scatter.3.cloned.1.call-start
  7.2 72.3 %down_ring.1 = (bf16[1024,256]{1,0:T(8,128)(2,1)}, bf16[4096,256]{1,0:T(8,128)(2,1)}) custom-call(bf16[1024,256]{1,0:T(8,128)(2,1)} %grad_ref.1, bf16[4096,256]{1,0:T(8,128)(2,1)} %w_hbm.2, bf16[1024,256]{1,0:T(8,128)(2,1)} %pre_ref.1), custom_call_target="tpu_custom_call" | custom-call | tf_op jit(solution)/shard_map/down_ring/pallas_call | solution.py:154
  79.6 0.0 reduce-scatter.3.cloned.1.call-update
  79.6 0.0 copy-start.3
  79.6 0.2 reduce-scatter.5.cloned.1.call-start
  79.8 10.7 %copy.27.w_hbm = bf16[4096,800]{1,0:T(8,128)(2,1)} copy(bf16[4096,800]{0,1:T(8,128)(2,1)} %param.12) | data formatting | bytes 13107200 | tf_op args[4]
  90.5 0.0 copy-done.3
  90.5 2.4 copy.28.normed_hbm
  92.9 72.6 %up_ring.1 = (f32[1024,800]{1,0:T(8,128)}, bf16[4096,800]{1,0:T(8,128)(2,1)}) custom-call(bf16[1024,256]{1,0:T(8,128)(2,1)} %get-tuple-element.11.part_ref, bf16[4096,800]{1,0:T(8,128)(2,1)} %copy.27.w_hbm, bf16[1024,800]{1,0:T(8,128)(2,1)} %copy.28.normed_hbm), custom_call_target="tpu_custom_call" | custom-call | tf_op jit(solution)/shard_map/up_ring/pallas_call | solution.py:218
  165.6 0.0 copy-start
  165.6 0.0 copy-start.4
  165.6 0.0 reduce-scatter.5.cloned.1.call-update
  165.6 0.0 copy-start.5
  165.7 1.4 copy-done
  167.1 0.0 copy-done.4
  167.1 3.4 %fusion.1 = (f32[1024]{0:T(1024)S(1)}, f32[800]{0:T(1024)S(1)}, f32[1024]{0:T(1024)S(1)}, f32[800]{0:T(1024)S(1)}) fusion(bf16[1024,800]{1,0:T(8,128)(2,1)S(1)} %copy-done, f32[1024,800]{1,0:T(8,128)} %get-tuple-element.13, f32[800]{0:T(1024)S(1)} %copy-done.4), kind=kLoop, calls=%fused_computation.5 | loop fusion | flops 6549952 | bytes 4932992 | tf_op jit(solution)/shard_map/reduce_sum | solution.py:264
  170.5 53.8 %all-reduce = (f32[1024]{0:T(1024)S(1)}, f32[1024]{0:T(1024)S(1)}) all-reduce(f32[1024]{0:T(1024)S(1)} %get-tuple-element.32, f32[1024]{0:T(1024)S(1)} %get-tuple-element.34), channel_id=1, replica_groups=mesh['ctx'=8,'tp'=16] {'tp'}, use_global_device_ids=true, to_apply=%region_14.0 | all-reduce | flops 2048 | bytes 16384 | tf_op jit(solution)/shard_map/psum | solution.py:263
  224.4 0.0 copy-done.5
  224.4 2.6 fusion.4
  227.0 0.0 copy-start.6
  227.0 0.1 fusion.6
  227.2 0.2 copy.33
  227.4 0.2 copy.32
  227.5 0.2 copy.31
  227.7 0.2 copy.30
  227.9 0.0 copy-done.6
  227.9 0.2 convert_reduce_fusion.2
  228.1 0.6 fusion.7
  228.7 1.3 iota_compare_fusion.1
  230.0 1.3 iota_compare_fusion.3
  231.3 4.4 %select_select_fusion = bf16[16,256,800]{1,2,0:T(8,128)(2,1)} fusion(pred[16]{0:T(512)(128)(4,1)S(1)} %get-tuple-element.54, pred[16]{0:T(512)(128)(4,1)S(1)} %get-tuple-element.55, pred[16]{0:T(512)(128)(4,1)S(1)} %get-tuple-element.56, pred[16]{0:T(512)(128)(4,1)S(1)} %get-tuple-element.57, bf16[256,800]{0,1:T(8,128)(2,1)S(1)} %copy.33, ...), kind=kLoop, calls=%fused_computation | loop fusion | flops 13107200 | bytes 8192064 | tf_op jit(solution)/shard_map/jit(_where)/select_n | solution.py:290
  235.7 0.0 copy-start.1
  235.7 0.0 copy-start.2
  235.7 4.8 %all-to-all-start = ((bf16[16,256,800]{1,2,0:T(8,128)(2,1)}), bf16[16,256,800]{1,2,0:T(8,128)(2,1)}, u32[]{:S(2)}, u32[]{:S(2)}) async-start(bf16[16,256,800]{1,2,0:T(8,128)(2,1)} %select_select_fusion), calls=%async_computation.2 | async-start | bytes 13107200 | tf_op jit(solution)/shard_map/all_to_all | solution.py:292
  240.5 0.0 copy-done.1
  240.5 0.2 convert_reduce_fusion.1
  240.7 0.0 copy-done.2
  240.7 0.2 convert_reduce_fusion
  240.8 13.7 %all-reduce.1 = (f32[256]{0:T(256)S(1)}, f32[256]{0:T(256)S(1)}, f32[1,800]{1,0:T(1,128)S(1)}, f32[1,800]{1,0:T(1,128)S(1)}) all-reduce(f32[256]{0:T(256)S(1)} %convert_reduce_fusion.1, f32[256]{0:T(256)S(1)} %convert_reduce_fusion, f32[1,800]{1,0:T(1,128)S(1)} %stack.10, f32[1,800]{1,0:T(1,128)S(1)} %stack.9), channel_id=1, replica_groups=mesh['ctx'=8,'tp'=16] {'ctx'}, use_global_device_ids=true, to_apply=%region_3.0 | all-reduce | flops 2112 | bytes 16896 | tf_op jit(solution)/shard_map/psum | solution.py:272
  254.5 0.6 maximum_multiply_fusion
  255.1 0.6 broadcast_multiply_fusion.2
  255.7 0.0 reduce-scatter.3.cloned.1.call-done
  255.7 1.8 convert_multiply_fusion.4
  257.5 39.8 %all-to-all-done = bf16[16,256,800]{1,2,0:T(8,128)(2,1)} async-done(((bf16[16,256,800]{1,2,0:T(8,128)(2,1)}), bf16[16,256,800]{1,2,0:T(8,128)(2,1)}, u32[]{:S(2)}, u32[]{:S(2)}) %all-to-all-start) | async-done | bytes 6553632 | tf_op jit(solution)/shard_map/all_to_all | solution.py:292
  297.3 9.5 %copy.35 = bf16[256,12800]{1,0:T(8,128)(2,1)} copy(bf16[256,12800]{0,1:T(8,128)(2,1)} %bitcast.6) | data formatting | bytes 13107200
  306.8 0.0 reduce-scatter.5.cloned.1.call-done
  306.8 1.3 convert_multiply_fusion.3
  308.1 1.6 copy.34
  (4 shorter events, 0.0 us)
Async XLA Ops:
  7.2 248.5 %reduce-scatter.3.cloned.1.call-start = ((), (), s32[]{:S(2)}) async-start(), calls=%async_computation.3 | async-start | bytes 2359296 | tf_op jit(solution)/shard_map/reduce_scatter | solution.py:255
  79.6 10.9 %copy-start.3 = (bf16[1024,800]{0,1:T(8,128)(2,1)S(1)}, bf16[1024,800]{0,1:T(8,128)(2,1)}, u32[]{:S(2)}) copy-start(bf16[1024,800]{0,1:T(8,128)(2,1)} %param.10) | copy-start | bytes 4915204
  79.6 227.2 %reduce-scatter.5.cloned.1.call-start = ((), (), s32[]{:S(2)}) async-start(), calls=%async_computation.4 | async-start | bytes 8257536 | tf_op jit(solution)/shard_map/reduce_scatter | solution.py:259
  165.6 1.5 copy-start
  165.6 1.5 copy-start.4
  165.6 58.7 %copy-start.5 = (f32[1024]{0:T(1024)S(1)}, f32[1024]{0:T(1024)}, u32[]{:S(2)}) copy-start(f32[1024]{0:T(1024)} %param.11) | copy-start | bytes 12292
  227.0 0.9 copy-start.6
  235.7 4.8 %copy-start.1 = (bf16[1024,256]{1,0:T(8,128)(2,1)S(1)}, bf16[1024,256]{1,0:T(8,128)(2,1)}, u32[]{:S(2)}) copy-start(bf16[1024,256]{1,0:T(8,128)(2,1)} %get-tuple-element.11.part_ref) | copy-start | bytes 1572868
  235.7 5.0 %copy-start.2 = (bf16[1024,256]{1,0:T(8,128)(2,1)S(1)}, bf16[1024,256]{1,0:T(8,128)(2,1)}, u32[]{:S(2)}) copy-start(bf16[1024,256]{1,0:T(8,128)(2,1)} %grad_ref.1) | copy-start | bytes 1572868
  235.7 61.6 %all-to-all-start = ((bf16[16,256,800]{1,2,0:T(8,128)(2,1)}), bf16[16,256,800]{1,2,0:T(8,128)(2,1)}, u32[]{:S(2)}, u32[]{:S(2)}) async-start(bf16[16,256,800]{1,2,0:T(8,128)(2,1)} %select_select_fusion), calls=%async_computation.2 | async-start | bytes 13107200 | tf_op jit(solution)/shard_map/all_to_all | solution.py:292
Sparse Core Ops, SparseCore 0:
  79.7 33.9 reduce-scatter.2
  165.8 46.5 reduce-scatter.4

commit v2 on v1

--- a/solution.py
+++ b/solution.py
@@ -1,3 +1,4 @@
+import functools
 import math
 
 import jax
@@ -30,6 +31,12 @@
 def row_product(left, right):
     return lax.dot_general(
         left, right, (((0,), (0,)), ((), ())), preferred_element_type=jnp.float32
+    )
+
+
+def dot_last(left, right):
+    return lax.dot_general(
+        left, right, (((1,), (1,)), ((), ())), preferred_element_type=jnp.float32
     )
 
 
@@ -111,7 +118,7 @@
 
 
 def down_kernel(
-    grad_ref, w_hbm, pre_ref, part_ref, gw2_ref, full_ref, w_ref, total, gw2, hidden, slope, w_sem, send_sem, recv_sem
+    grad_ref, w_hbm, pre_ref, part_ref, gw2_ref, bias_ref, full_ref, w_ref, total, gw2, hidden, slope, w_sem, send_sem, recv_sem
 ):
     me = lax.axis_index("tp")
     rings = Rings(me)
@@ -131,6 +138,7 @@
             return carry
 
         lax.fori_loop(0, rows_all // 64, rows_of, 0)
+        bias_ref[0:1, :] = jnp.sum(grad_ref[...].astype(jnp.float32), axis=0, keepdims=True)
         total[...] = jnp.zeros_like(total)
         gw2[...] = jnp.zeros_like(gw2)
         load.wait()
@@ -143,7 +151,9 @@
         gw2[features, :] += row_product(block, hidden[rows, :])
 
     ring_gather(prepare, rings, full_ref, send_sem, recv_sem, consume)
-    part_ref[...] = (total[...] * slope[...]).astype(jnp.bfloat16)
+    part = (total[...] * slope[...]).astype(jnp.bfloat16)
+    part_ref[...] = part
+    bias_ref[1:2, :] = jnp.sum(part.astype(jnp.float32), axis=0, keepdims=True)
     gw2_ref[...] = gw2[...].astype(jnp.bfloat16)
 
 
@@ -156,9 +166,10 @@
         out_shape=(
             jax.ShapeDtypeStruct((rows, hid), jnp.bfloat16),
             jax.ShapeDtypeStruct((features, hid), jnp.bfloat16),
+            jax.ShapeDtypeStruct((2, hid), jnp.float32),
         ),
         in_specs=[vmem, pl.BlockSpec(memory_space=pl.ANY), vmem],
-        out_specs=(vmem, vmem),
+        out_specs=(vmem, vmem, vmem),
         scratch_shapes=[
             pltpu.VMEM((TP, rows, width), jnp.bfloat16),
             pltpu.VMEM((features, hid), jnp.bfloat16),
@@ -192,6 +203,7 @@
     greet(rings.targets)
     rows_all, width = part_ref.shape
     quarter = rows_all // RINGS
+    per_owner = gw1.shape[2] // width
 
     def prepare():
         norm_ref[...] = jnp.zeros_like(norm_ref)
@@ -202,32 +214,33 @@
     def consume(origin, ring):
         rows = pl.ds(ring * quarter, quarter)
         units = pl.ds(pl.multiple_of(origin * width, width), width)
+        within = pl.ds(pl.multiple_of(origin % per_owner * width, width), width)
         block = full_ref[origin, rows, :]
-        norm_ref[rows, :] += dot(block, w_ref[units, :])
-        gw1[units, :] += row_product(block, normed_ref[rows, :])
+        norm_ref[:, rows] += dot_last(w_ref[:, units], block)
+        gw1[origin // per_owner, :, within] += dot(normed_ref[:, rows], block)
 
     ring_gather(prepare, rings, full_ref, send_sem, recv_sem, consume)
     gw1_ref[...] = gw1[...].astype(jnp.bfloat16)
 
 
-def up(back_part, w_up, normed):
+def up(back_part, w_up_t, normed_t, ctx_count):
     rows, width = back_part.shape
-    units, channels = w_up.shape
+    channels, units = w_up_t.shape
     vmem = pl.BlockSpec(memory_space=pltpu.VMEM)
     anywhere = pl.BlockSpec(memory_space=pl.ANY)
     return pl.pallas_call(
         up_kernel,
         out_shape=(
-            jax.ShapeDtypeStruct((rows, channels), jnp.float32),
-            jax.ShapeDtypeStruct((units, channels), jnp.bfloat16),
+            jax.ShapeDtypeStruct((channels, rows), jnp.float32),
+            jax.ShapeDtypeStruct((ctx_count, channels, units // ctx_count), jnp.bfloat16),
         ),
         in_specs=[vmem, anywhere, anywhere],
         out_specs=(vmem, vmem),
         scratch_shapes=[
             pltpu.VMEM((TP, rows, width), jnp.bfloat16),
-            pltpu.VMEM((units, channels), jnp.bfloat16),
-            pltpu.VMEM((rows, channels), jnp.bfloat16),
-            pltpu.VMEM((units, channels), jnp.float32),
+            pltpu.VMEM((channels, units), jnp.bfloat16),
+            pltpu.VMEM((channels, rows), jnp.bfloat16),
+            pltpu.VMEM((ctx_count, channels, units // ctx_count), jnp.float32),
             pltpu.SemaphoreType.DMA((2,)),
             pltpu.SemaphoreType.DMA((RINGS, TP - 1, SUBS)),
             pltpu.SemaphoreType.DMA((RINGS, TP - 1, SUBS)),
@@ -235,14 +248,350 @@
         compiler_params=pltpu.CompilerParams(
             collective_id=1, has_side_effects=True, vmem_limit_bytes=VMEM_LIMIT
         ),
+        cost_estimate=pl.CostEstimate(
+            flops=4 * rows * units * channels, bytes_accessed=20 * 2**20, transcendentals=0
+        ),
         name="up_ring",
-    )(back_part, w_up, normed)
-
-
-def slot_numbers(owners, capacity):
-    position = jnp.arange(owners.shape[0])
-    earlier = (owners[None, :] == owners[:, None]) & (position[None, :] < position[:, None])
-    return owners * capacity + jnp.sum(earlier.astype(jnp.int32), axis=1)
+    )(back_part, w_up_t, normed_t)
+
+
+HALVES = 2
+LANES = 128
+
+
+class Torus:
+    def __init__(self, half, me):
+        z, y = me // SIDE, me % SIDE
+        self.half = half
+        self.along, self.cross = (y, z) if half == 0 else (z, y)
+
+    def place(self, along, cross):
+        along, cross = along % SIDE, cross % SIDE
+        return cross * SIDE + along if self.half == 0 else along * SIDE + cross
+
+
+def hand_kernel(
+    full_width,
+    grad_scale,
+    norm_ref,
+    normed_ref,
+    gain_ref,
+    std_ref,
+    owner_ref,
+    bias_ref,
+    ln_ref,
+    up_ref,
+    down_ref,
+    out_ref,
+    own_y, next_y, far_y, prev_y,
+    own_z, next_z, far_z, prev_z,
+    message,
+    final,
+    product,
+    stats_y,
+    stats_z,
+    sums,
+    near_send, near_recv, relay_send, relay_recv, cross_send, cross_recv, stat_send, stat_recv, sum_send, sum_recv,
+):
+    me = lax.axis_index("tp")
+    group = lax.axis_index("ctx")
+    ctx_count = sums.shape[0]
+    torus = [Torus(half, me) for half in range(HALVES)]
+    held = [[own_y, next_y, far_y, prev_y], [own_z, next_z, far_z, prev_z]]
+    images, channels, _ = own_y.shape
+    image_rows = norm_ref.shape[1] // images
+    chunk = channels // 5
+
+    def along_peer(half, d):
+        t = torus[half]
+        return t.place(t.along + d, t.cross)
+
+    def cross_peer(half, d):
+        t = torus[half]
+        return t.place(t.along, t.cross + d)
+
+    barrier = pltpu.get_barrier_semaphore()
+    for half in range(HALVES):
+        for d in range(1, SIDE):
+            pl.semaphore_signal(barrier, inc=1, device_id={"tp": along_peer(half, d)}, device_id_type=MESH)
+    for d in range(1, ctx_count):
+        pl.semaphore_signal(barrier, inc=1, device_id={"ctx": (group + d) % ctx_count}, device_id_type=MESH)
+
+    ones = jnp.ones((8, image_rows), jnp.float32)
+    columns = [jnp.zeros((8, channels), jnp.float32)] * 2
+    for i in range(images):
+        rows = pl.ds(i * image_rows, image_rows)
+
+        def some(k, carry):
+            part = pl.ds(pl.multiple_of(k * chunk, chunk), chunk)
+            value = norm_ref[part, rows]
+            feature = normed_ref[part, rows].astype(jnp.float32)
+            gained = gain_ref[part, :] * value
+            both = value * feature
+            product[part, :] = both
+            return (
+                carry[0] + jnp.sum(gained, axis=0, keepdims=True),
+                carry[1] + jnp.sum(gained * feature, axis=0, keepdims=True),
+            )
+
+        zero = jnp.zeros((1, image_rows), jnp.float32)
+        first, second = lax.fori_loop(0, 5, some, (zero, zero))
+        stats_y[0, i : i + 1, :] = first
+        stats_y[0, images + i : images + i + 1, :] = second
+        columns = [
+            total
+            + lax.dot_general(
+                ones,
+                right,
+                (((1,), (1,)), ((), ())),
+                precision=lax.Precision.HIGHEST,
+                preferred_element_type=jnp.float32,
+            )
+            for total, right in zip(columns, (product[...], norm_ref[:, rows]))
+        ]
+    sums[0, 0:1, 0:channels] = columns[0][0:1]
+    sums[0, 1:2, 0:channels] = columns[1][0:1]
+    sums[0, 2:4, 0 : bias_ref.shape[1]] = bias_ref[...]
+    pl.semaphore_wait(barrier, HALVES * (SIDE - 1) + ctx_count - 1)
+
+    def stat_copy(half, d):
+        buffer = (stats_y, stats_z)[half]
+        return pltpu.make_async_remote_copy(
+            src_ref=buffer.at[0],
+            dst_ref=buffer.at[d],
+            send_sem=stat_send.at[half, d - 1],
+            recv_sem=stat_recv.at[half, d - 1],
+            device_id={"tp": along_peer(half, d)},
+            device_id_type=MESH,
+        )
+
+    def sum_copy(d):
+        return pltpu.make_async_remote_copy(
+            src_ref=sums.at[0],
+            dst_ref=sums.at[d],
+            send_sem=sum_send.at[d - 1],
+            recv_sem=sum_recv.at[d - 1],
+            device_id={"ctx": (group + d) % ctx_count},
+            device_id_type=MESH,
+        )
+
+    for d in range(1, SIDE):
+        stat_copy(0, d).start()
+    for d in range(1, SIDE):
+        stat_copy(0, d).wait_recv()
+    stats_z[0] = stats_y[0] + stats_y[1] + stats_y[2] + stats_y[3]
+    for d in range(1, SIDE):
+        stat_copy(1, d).start()
+    for d in range(1, SIDE):
+        stat_copy(1, d).wait_recv()
+    means = (stats_z[0] + stats_z[1] + stats_z[2] + stats_z[3]) * (1.0 / full_width)
+
+    def near(half, sign, pair):
+        piece = pl.ds(pair * (images // 2), images // 2)
+        return pltpu.make_async_remote_copy(
+            src_ref=held[half][0].at[piece],
+            dst_ref=held[half][3 if sign == 1 else 1].at[piece],
+            send_sem=near_send.at[half, sign // 2, pair],
+            recv_sem=near_recv.at[half, sign // 2, pair],
+            device_id={"tp": along_peer(half, sign)},
+            device_id_type=MESH,
+        )
+
+    def relay(half, sign):
+        pair = sign // 2
+        piece = pl.ds(pair * (images // 2), images // 2)
+        return pltpu.make_async_remote_copy(
+            src_ref=held[half][3 if sign == 1 else 1].at[piece],
+            dst_ref=held[half][2].at[piece],
+            send_sem=relay_send.at[half, pair],
+            recv_sem=relay_recv.at[half, pair],
+            device_id={"tp": along_peer(half, sign)},
+            device_id_type=MESH,
+        )
+
+    def across(half, target, d):
+        t = torus[half]
+        slot = (t.along + d) % SIDE
+        if half == 0:
+            spot = final.at[0, t.cross, pl.ds(pl.multiple_of(slot * channels, 16), channels)]
+        else:
+            spot = final.at[1, slot, pl.ds(pl.multiple_of(t.cross * channels, 16), channels)]
+        if target == 0:
+            return spot
+        return pltpu.make_async_remote_copy(
+            src_ref=message.at[half, target - 1, d],
+            dst_ref=spot,
+            send_sem=cross_send.at[half, target - 1, d],
+            recv_sem=cross_recv.at[half, target - 1, d],
+            device_id={"tp": cross_peer(half, target)},
+            device_id_type=MESH,
+        )
+
+    for i in range(images):
+        rows = pl.ds(i * image_rows, image_rows)
+        mean_first, mean_second = means[i : i + 1, :], means[images + i : images + i + 1, :]
+        inverse = std_ref[:, rows]
+
+        def visual(k, carry):
+            part = pl.ds(pl.multiple_of(k * chunk, chunk), chunk)
+            value = gain_ref[part, :] * norm_ref[part, rows]
+            feature = normed_ref[part, rows].astype(jnp.float32)
+            seen = (inverse * (value - mean_first - feature * mean_second)).astype(jnp.bfloat16)
+            own_y[i, part, :] = seen[:, :LANES]
+            own_z[i, part, :] = seen[:, LANES:]
+            return carry
+
+        lax.fori_loop(0, 5, visual, 0)
+        if i % 2:
+            for half in range(HALVES):
+                near(half, 1, i // 2).start()
+                near(half, 3, i // 2).start()
+    for d in range(1, ctx_count):
+        sum_copy(d).start()
+
+    owners = [owner_ref[0, i] for i in range(images)]
+    slots = []
+    for i in range(images):
+        earlier = jnp.int32(0)
+        for j in range(i):
+            earlier += (owners[j] == owners[i]).astype(jnp.int32)
+        slots.append(owners[i] + earlier)
+
+    def choice(place):
+        source, present = jnp.int32(0), jnp.int32(0)
+        for i in range(images):
+            match = (slots[i] == place).astype(jnp.int32)
+            source += i * match
+            present += match
+        return source, present
+
+    chosen = [[choice(cross_peer(half, target)) for target in range(SIDE)] for half in range(HALVES)]
+
+    def forward(half, d):
+        block = held[half][d]
+        for target in (2, 1, 3, 0):
+            source, present = chosen[half][target]
+            spot = across(half, 0, d) if target == 0 else message.at[half, target - 1, d]
+
+            def pick(k, carry):
+                part = pl.ds(pl.multiple_of(k * chunk, chunk), chunk)
+                value = block[source, part, :]
+                spot[part, :] = jnp.where(present > 0, value, jnp.zeros_like(value))
+                return carry
+
+            lax.fori_loop(0, 5, pick, 0)
+            if target:
+                across(half, target, d).start()
+
+    for half in range(HALVES):
+        forward(half, 0)
+    for half in range(HALVES):
+        near(half, 1, 0).wait_recv()
+        relay(half, 1).start()
+    for half in range(HALVES):
+        near(half, 3, 1).wait_recv()
+        relay(half, 3).start()
+    for half in range(HALVES):
+        near(half, 1, 1).wait_recv()
+        forward(half, 3)
+        near(half, 3, 0).wait_recv()
+        forward(half, 1)
+    for half in range(HALVES):
+        relay(half, 1).wait_recv()
+        relay(half, 3).wait_recv()
+        forward(half, 2)
+
+    for d in range(1, ctx_count):
+        sum_copy(d).wait_recv()
+    whole = sums[0]
+    for d in range(1, ctx_count):
+        whole = whole + sums[d]
+    whole = whole * grad_scale
+    ln_ref[...] = whole[0:2, 0:channels]
+    down_ref[...] = whole[2:3, 0 : bias_ref.shape[1]]
+    up_ref[...] = whole[3:4, 0 : bias_ref.shape[1]]
+
+    wide = SIDE * channels
+
+    def turn(half, z):
+        def tile(k, carry):
+            block = final[half, z, pl.ds(pl.multiple_of(k * LANES, LANES), LANES), :]
+            at = pl.ds(pl.multiple_of(z * wide + k * LANES, LANES), LANES)
+            out_ref[half * LANES : (half + 1) * LANES, at] = block.T
+            return carry
+
+        lax.fori_loop(0, wide // LANES, tile, 0)
+
+    for d in (0, 3, 1, 2):
+        if d == 0:
+            turn(0, torus[0].cross)
+        else:
+            for e in range(SIDE):
+                across(0, d, e).wait_recv()
+            turn(0, (torus[0].cross - d + SIDE) % SIDE)
+    for e in (0, 3, 1, 2):
+        for d in range(1, SIDE):
+            across(1, d, e).wait_recv()
+        turn(1, (torus[1].along + e) % SIDE)
+
+    for half in range(HALVES):
+        for sign in (1, 3):
+            for pair in range(2):
+                near(half, sign, pair).wait_send()
+            relay(half, sign).wait_send()
+        for d in range(1, SIDE):
+            stat_copy(half, d).wait_send()
+            for e in range(SIDE):
+                across(half, d, e).wait_send()
+    for d in range(1, ctx_count):
+        sum_copy(d).wait_send()
+
+
+def hand_over(norm_t, normed_t, gain, inverse_std, owner_map, bias, full_width, grad_scale, ctx_count):
+    channels, rows = norm_t.shape
+    images = owner_map.shape[1]
+    image_rows = rows // images
+    width = bias.shape[1]
+    vmem = pl.BlockSpec(memory_space=pltpu.VMEM)
+    block = pltpu.VMEM((images, channels, LANES), jnp.bfloat16)
+    dma = pltpu.SemaphoreType.DMA
+    return pl.pallas_call(
+        functools.partial(hand_kernel, full_width, grad_scale),
+        out_shape=(
+            jax.ShapeDtypeStruct((2, channels), jnp.float32),
+            jax.ShapeDtypeStruct((1, width), jnp.float32),
+            jax.ShapeDtypeStruct((1, width), jnp.float32),
+            jax.ShapeDtypeStruct((image_rows, TP * channels), jnp.bfloat16),
+        ),
+        in_specs=[vmem, vmem, vmem, vmem, pl.BlockSpec(memory_space=pltpu.SMEM), vmem],
+        out_specs=(vmem, vmem, vmem, vmem),
+        scratch_shapes=[block] * 8
+        + [
+            pltpu.VMEM((HALVES, SIDE - 1, SIDE, channels, LANES), jnp.bfloat16),
+            pltpu.VMEM((HALVES, SIDE, SIDE * channels, LANES), jnp.bfloat16),
+            pltpu.VMEM((channels, image_rows), jnp.float32),
+            pltpu.VMEM((SIDE, 2 * images, image_rows), jnp.float32),
+            pltpu.VMEM((SIDE, 2 * images, image_rows), jnp.float32),
+            pltpu.VMEM((ctx_count, 8, 1024), jnp.float32),
+            dma((HALVES, 2, 2)),
+            dma((HALVES, 2, 2)),
+            dma((HALVES, 2)),
+            dma((HALVES, 2)),
+            dma((HALVES, SIDE - 1, SIDE)),
+            dma((HALVES, SIDE - 1, SIDE)),
+            dma((HALVES, SIDE - 1)),
+            dma((HALVES, SIDE - 1)),
+            dma((ctx_count - 1,)),
+            dma((ctx_count - 1,)),
+        ],
+        compiler_params=pltpu.CompilerParams(
+            collective_id=2, has_side_effects=True, vmem_limit_bytes=VMEM_LIMIT
+        ),
+        cost_estimate=pl.CostEstimate(
+            flops=20 * rows * channels, bytes_accessed=200 * 2**20, transcendentals=0
+        ),
+        name="hand_over",
+    )(norm_t, normed_t, gain, inverse_std, owner_map, bias)
 
 
 def per_device(out_grad, pre_act, normed, inverse_std, w_up, w_down, ln_gain, owner_map):
@@ -250,47 +599,26 @@
     tp_count = lax.axis_size("tp")
     row_count = out_grad.shape[0]
     grad_scale = float(row_count * ctx_count) ** (-0.5)
-    back_part, gw2 = down(out_grad, w_down, pre_act)
+    back_part, gw2, bias = down(out_grad, w_down, pre_act)
     grad_w2 = (
         lax.psum_scatter(gw2, "ctx", scatter_dimension=0, tiled=True).astype(jnp.float32) * grad_scale
     )
-    norm_grad, gw1 = up(back_part, w_up, normed)
-    grad_w1 = (
-        lax.psum_scatter(gw1, "ctx", scatter_dimension=0, tiled=True).astype(jnp.float32) * grad_scale
+    normed_t = normed.T
+    norm_t, gw1 = up(back_part, w_up.T, normed_t, ctx_count)
+    grad_w1_t = lax.psum_scatter(gw1, "ctx", scatter_dimension=0, tiled=True)
+    grad_w1 = (grad_w1_t[0].astype(jnp.float32) * grad_scale).T
+    ln_grads, bias_up, bias_down, vit_grad = hand_over(
+        norm_t,
+        normed_t,
+        ln_gain[:, None],
+        inverse_std[None, :],
+        owner_map,
+        bias,
+        float(normed.shape[1] * tp_count),
+        grad_scale,
+        ctx_count,
     )
-    features = normed.astype(jnp.float32)
-    gained = ln_gain[None, :] * norm_grad
-    sum_first, sum_second = lax.psum(
-        (jnp.sum(gained, axis=-1), jnp.sum(gained * features, axis=-1)), "tp"
-    )
-    full_width = float(normed.shape[1] * tp_count)
-    mean_first = sum_first / full_width
-    mean_second = sum_second / full_width
-    visual = (
-        inverse_std[:, None] * (gained - mean_first[:, None] - features * mean_second[:, None])
-    ).astype(jnp.bfloat16)
-    bias_down, bias_up, gain_sum, bias_sum = lax.psum(
-        (
-            jnp.sum(out_grad.astype(jnp.float32), axis=0),
-            jnp.sum(back_part.astype(jnp.float32), axis=0),
-            jnp.sum(norm_grad * features, axis=0),
-            jnp.sum(norm_grad, axis=0),
-        ),
-        "ctx",
-    )
-    ln_grads = jnp.stack([gain_sum, bias_sum]) * grad_scale
-    owners = owner_map[0]
-    image_count = owners.shape[0]
-    image_rows = row_count // image_count
-    slot_of = slot_numbers(owners, 1)
-    images = visual.reshape(image_count, image_rows, visual.shape[1])
-    slot_ids = jnp.arange(tp_count)[:, None, None]
-    outgoing = jnp.zeros((), jnp.bfloat16)
-    for i in range(image_count):
-        outgoing = jnp.where(slot_ids == slot_of[i], images[i][None], outgoing)
-    outgoing = outgoing.reshape(tp_count * image_rows, visual.shape[1])
-    vit_grad = lax.all_to_all(outgoing, "tp", split_axis=0, concat_axis=1, tiled=True)
-    return (grad_w2, grad_w1, bias_up * grad_scale, bias_down * grad_scale, ln_grads, vit_grad)
+    return (grad_w2, grad_w1, bias_up[0], bias_down[0], ln_grads, vit_grad)
 
 
 def solution(mesh):

time: 318 us -> 265 us (0.83)
  Pallas kernels: 145 us -> 237 us
  blocking collectives: 67.5 us -> 0 us
  waiting for transfers between devices: 39.8 us -> 0.06 us
  local copies, waits for them, and re-layouts: 27.2 us -> 9.38 us
  other arithmetic: 17.8 us -> 4.33 us
  starting transfers between devices: 5.03 us -> 0.08 us
    pallas_call x1 -> x2, Pallas kernels: 72.6 us -> 164 us  [the longest x1 91.6 us: hand_over(): pl.pallas_call(functools.partial(hand_kernel, full_width, grad_scale), ou...]
    psum x2 -> x0, blocking collectives: 67.5 us -> none  [the longest x1 53.8 us: per_device(): lax.psum((jnp.sum(gained, axis=-1), jnp.sum(gained * features, axis=-1)),...]
    all_to_all x1 -> x0, waiting for transfers between devices: 39.8 us -> none  [per_device(): lax.all_to_all(outgoing, 'tp', split_axis=0, concat_axis=1, tiled=True)]
    unnamed x18 -> x12, local copies, waits for them, and re-layouts: 25.7 us -> 8.46 us
    all_to_all x1 -> x0, starting transfers between devices: 4.77 us -> none  [per_device(): lax.all_to_all(outgoing, 'tp', split_axis=0, concat_axis=1, tiled=True)]
    select_n x1 -> x0, other arithmetic: 4.37 us -> none  [per_device(): outgoing = jnp.where(slot_ids == slot_of[i], images[i][None], outgoing)]
    reduce_sum x4 -> x0, other arithmetic: 3.89 us -> none  [the longest x1 3.41 us: per_device(): jnp.sum(gained * features, axis=-1)]
  transfers between devices with their start and end apart: 3 -> 2, of which waited for: 1 -> 0; matrix products, arithmetic and copies ran while one was open for 13% -> 1% of each run, Pallas kernels for 23% -> 62%
where the time goes in v2:
time: 265 us
  Pallas kernels  237 us (89%)
  between operations  14.1 us (5%)
  local copies, waits for them, and re-layouts  9.38 us (4%)
  other arithmetic  4.33 us (2%)
    pallas_call x1, Pallas kernels, hand_over(): pl.pallas_call(functools.partial(hand_kernel, full_width, grad_scale), ou...  91.6 us
    pallas_call x1, Pallas kernels, down(): pl.pallas_call(down_kernel, out_shape=(jax.ShapeDtypeStruct((rows, hid),...  72.7 us
    pallas_call x1, Pallas kernels, up(): pl.pallas_call(up_kernel, out_shape=(jax.ShapeDtypeStruct((channels, rows...  72.6 us
    unnamed x12, local copies, waits for them, and re-layouts  8.46 us
  transfers between devices with their start and end apart: 2, of which 0 were waited for; matrix products, arithmetic and copies ran while one was open for 1% of the time, Pallas kernels for 62%

profile of v2, /device:TPU:0, one launch (start us, length us, event | category | flops | bytes accessed | tf_op | source)
XLA Modules:
  0.0 264.8 jit_solution(17358443776011687405)
XLA Ops:
  7.2 0.0 reduce-scatter.3.cloned.1.call-start
  7.2 72.7 %down_ring.1 = (bf16[1024,256]{1,0:T(8,128)(2,1)}, bf16[4096,256]{1,0:T(8,128)(2,1)}, f32[2,256]{1,0:T(2,128)}) custom-call(bf16[1024,256]{1,0:T(8,128)(2,1)} %grad_ref.1, bf16[4096,256]{1,0:T(8,128)(2,1)} %w_hbm.1, bf16[1024,256]{1,0:T(8,128)(2,1)} %pre_ref.1), custom_call_target="tpu_custom_call" | custom-call | tf_op jit(solution)/shard_map/down_ring/pallas_call | solution.py:164
  79.9 0.0 reduce-scatter.3.cloned.1.call-update
  79.9 0.0 reduce-scatter.5.cloned.1.call-start
  80.0 72.6 %up_ring.1 = (f32[800,1024]{1,0:T(8,128)}, bf16[8,800,512]{2,1,0:T(8,128)(2,1)}) custom-call(bf16[1024,256]{1,0:T(8,128)(2,1)} %get-tuple-element.16.part_ref, bf16[800,4096]{1,0:T(8,128)(2,1)} %bitcast.14, bf16[800,1024]{1,0:T(8,128)(2,1)} %bitcast.9), custom_call_target="tpu_custom_call" | custom-call | flops 13421772800 | bytes 20971520 | tf_op jit(solution)/shard_map/up_ring/pallas_call | solution.py:231
  152.5 0.0 copy-start.1
  152.6 0.0 reduce-scatter.5.cloned.1.call-update
  152.6 0.7 copy-done.1
  153.2 0.9 broadcast_in_dim.8.gain_ref
  154.2 91.6 %hand_over.1 = (f32[2,800]{1,0:T(2,128)}, f32[1,256]{1,0:T(1,128)}, f32[1,256]{1,0:T(1,128)}, bf16[256,12800]{1,0:T(8,128)(2,1)}) custom-call(f32[800,1024]{1,0:T(8,128)} %get-tuple-element.18.norm_ref, bf16[800,1024]{1,0:T(8,128)(2,1)} %bitcast.10, f32[800,1]{1,0:T(8,128)} %broadcast_in_dim.8.gain_ref, f32[1,1024]{1,0:T(1,128)} %bitcast.11, ...), custom_call_target="tpu_custom_call" | custom-call | flops 16384000 | bytes 209715200 | tf_op jit(solution)/shard_map/hand_over/pallas_call | solution.py:558
  245.8 0.0 copy-start.3
  245.8 0.0 copy-start.2
  245.8 0.0 copy-start
  245.8 0.0 reduce-scatter.3.cloned.1.call-done
  245.8 1.8 convert_multiply_fusion
  247.6 0.0 reduce-scatter.5.cloned.1.call-done
  247.6 2.5 multiply_bitcast_fusion
  250.2 0.0 copy-done.3
  250.2 0.6 copy.19
  250.7 0.0 copy-done.2
  250.7 0.6 copy.20
  251.3 0.0 copy-done
  251.3 0.6 copy.21
  251.9 6.1 %copy.22 = bf16[256,12800]{1,0:T(8,128)(2,1)} copy(bf16[256,12800]{1,0:T(8,128)(2,1)} %get-tuple-element.35) | data formatting | bytes 13107200
Async XLA Ops:
  7.2 238.6 %reduce-scatter.3.cloned.1.call-start = ((), (), s32[]{:S(2)}) async-start(), calls=%async_computation.2 | async-start | bytes 2359296 | tf_op jit(solution)/shard_map/reduce_scatter | solution.py:604
  79.9 167.7 %reduce-scatter.5.cloned.1.call-start = ((), (), s32[]{:S(2)}) async-start(), calls=%async_computation.3 | async-start | bytes 7372800 | tf_op jit(solution)/shard_map/reduce_scatter | solution.py:608
  152.5 0.7 copy-start.1
  245.8 4.4 %copy-start.3 = (f32[1,256]{1,0:T(1,128)S(1)}, f32[1,256]{1,0:T(1,128)}, u32[]{:S(2)}) copy-start(f32[1,256]{1,0:T(1,128)} %get-tuple-element.20) | copy-start | bytes 3076
  245.8 5.0 %copy-start.2 = (f32[1,256]{1,0:T(1,128)S(1)}, f32[1,256]{1,0:T(1,128)}, u32[]{:S(2)}) copy-start(f32[1,256]{1,0:T(1,128)} %get-tuple-element.21) | copy-start | bytes 3076
  245.8 5.5 %copy-start = (f32[2,800]{1,0:T(2,128)S(1)}, f32[2,800]{1,0:T(2,128)}, u32[]{:S(2)}) copy-start(f32[2,800]{1,0:T(2,128)} %get-tuple-element.34) | copy-start | bytes 19204
Sparse Core Ops, SparseCore 0:
  80.0 34.2 reduce-scatter.2
  152.7 44.9 reduce-scatter.4

commit v3 on v2

--- a/solution.py
+++ b/solution.py
@@ -11,8 +11,6 @@
 MESH = pl.DeviceIdType.MESH
 SIDE = 4
 TP = SIDE * SIDE
-RINGS = 4
-SUBS = 2
 VMEM_LIMIT = 60 * 2**20
 
 
@@ -40,28 +38,9 @@
     )
 
 
-class Rings:
-    def __init__(self, me):
-        z, y = me // SIDE, me % SIDE
-        b = (y + z) % SIDE
-        last, first = b // 3, (3 - b) // 3
-
-        def at(zz, yy):
-            return ((zz + SIDE) % SIDE) * SIDE + (yy + SIDE) % SIDE
-
-        self.positions = (z * SIDE + b, y * SIDE + b)
-        self.targets = (
-            at(z + last, y + 1 - last),
-            at(z - first, y - 1 + first),
-            at(z + 1 - last, y + last),
-            at(z - 1 + first, y - first),
-        )
-
-    def origin(self, ring, step):
-        signed = step if ring % 2 else TP - step
-        q = (self.positions[ring // 2] + signed) % TP
-        major, minor = q // SIDE, (q % SIDE - q // SIDE + SIDE) % SIDE
-        return major * SIDE + minor if ring < 2 else minor * SIDE + major
+def around(half, me):
+    t = Torus(half, me)
+    return ((t.along + 1, t.cross), (t.along + SIDE - 1, t.cross))
 
 
 def greet(targets):
@@ -71,47 +50,91 @@
     pl.semaphore_wait(barrier, len(targets))
 
 
-def ring_gather(prepare, rings, full_ref, send_sem, recv_sem, consume):
-    quarter = full_ref.shape[1] // RINGS
-    part = quarter // SUBS
-
-    def copy(ring, step, sub, at):
-        spot = full_ref.at[rings.origin(ring, at), pl.ds(ring * quarter + sub * part, part)]
+class Torus:
+    def __init__(self, half, me):
+        z, y = me // SIDE, me % SIDE
+        self.half = half
+        self.along, self.cross = (y, z) if half == 0 else (z, y)
+
+    def place(self, along, cross):
+        along, cross = along % SIDE, cross % SIDE
+        return cross * SIDE + along if self.half == 0 else along * SIDE + cross
+
+
+QUARTERS = 4
+ARRIVALS = (
+    (3, 0), (1, 0), (0, 3), (2, 0), (3, 3), (1, 3), (0, 1), (2, 3),
+    (3, 1), (0, 2), (1, 1), (3, 2), (2, 1), (1, 2), (2, 2),
+)
+
+
+def numbered(values, index):
+    out = jnp.int32(values[0])
+    for i, value in enumerate(values[1:], 1):
+        out = jnp.where(index == i, jnp.int32(value), out)
+    return out
+
+
+def tree_gather(prepare, me, full_ref, send_sem, recv_sem, consume):
+    rows = full_ref.shape[1] // QUARTERS
+    torus = [Torus(half, me) for half in range(2)]
+
+    def origin(quarter, along, cross):
+        t, sign = torus[quarter // 2], 1 - quarter % 2 * 2
+        return t.place(t.along + sign * along + SIDE, t.cross + sign * cross + SIDE)
+
+    def copy(quarter, block, number, target):
+        spot = full_ref.at[origin(quarter, *block), pl.ds(quarter * rows, rows)]
         return pltpu.make_async_remote_copy(
             src_ref=spot,
             dst_ref=spot,
-            send_sem=send_sem.at[ring, step, sub],
-            recv_sem=recv_sem.at[ring, step, sub],
-            device_id={"tp": rings.targets[ring]},
+            send_sem=send_sem.at[quarter, number],
+            recv_sem=recv_sem.at[quarter, number],
+            device_id={"tp": origin(quarter, *target)},
             device_id_type=MESH,
         )
 
-    for sub in range(SUBS):
-        for ring in range(RINGS):
-            copy(ring, 0, sub, 0).start()
+    def send(block, seen):
+        target = ((block[0] - seen[0]) % SIDE, (block[1] - seen[1]) % SIDE)
+        for quarter in range(QUARTERS):
+            copy(quarter, block, ARRIVALS.index(seen), target).start()
+
+    send((0, 0), (3, 0))
+    send((0, 0), (1, 0))
+    send((0, 0), (0, 3))
+    send((0, 0), (0, 1))
     prepare()
-
-    def hop(step, carry):
-        for sub in range(SUBS):
-            for ring in range(RINGS):
-                copy(ring, step - 1, sub, step).wait_recv()
-                copy(ring, step, sub, step).start()
-            for ring in range(RINGS // SUBS * sub, RINGS // SUBS * (sub + 1)):
-                consume(rings.origin(ring, step - 1), ring)
+    for quarter in range(QUARTERS):
+        consume(me, quarter)
+
+    def arrive(k, carry):
+        along = numbered([block[0] for block in ARRIVALS], k)
+        cross = numbered([block[1] for block in ARRIVALS], k)
+        for quarter in range(QUARTERS):
+            copy(quarter, (along, cross), k, (1, 0)).wait_recv()
+        for number, block in enumerate(ARRIVALS):
+            if block[1] not in (0, 3):
+                continue
+
+            @pl.when(k == number)
+            def _():
+                if block == (3, 0):
+                    send(block, (2, 0))
+                if block[1] == 0:
+                    send(block, (block[0], 3))
+                    send(block, (block[0], 1))
+                else:
+                    send(block, (block[0], 2))
+
+        for quarter in range(QUARTERS):
+            consume(origin(quarter, along, cross), quarter)
         return carry
 
-    lax.fori_loop(1, TP - 1, hop, 0)
-    for ring in range(RINGS):
-        consume(rings.origin(ring, TP - 2), ring)
-    for ring in range(RINGS):
-        for sub in range(SUBS):
-            copy(ring, TP - 2, sub, TP - 1).wait_recv()
-        consume(rings.origin(ring, TP - 1), ring)
-
-    def drain(step, carry):
-        for sub in range(SUBS):
-            for ring in range(RINGS):
-                copy(ring, step, sub, step).wait_send()
+    lax.fori_loop(0, TP - 1, arrive, 0)
+
+    def drain(k, carry):
+        for quarter in range(QUARTERS):
+            copy(quarter, (0, 0), k, (1, 0)).wait_send()
         return carry
 
     lax.fori_loop(0, TP - 1, drain, 0)
@@ -121,13 +144,12 @@
     grad_ref, w_hbm, pre_ref, part_ref, gw2_ref, bias_ref, full_ref, w_ref, total, gw2, hidden, slope, w_sem, send_sem, recv_sem
 ):
     me = lax.axis_index("tp")
-    rings = Rings(me)
     load = pltpu.make_async_copy(w_hbm, w_ref, w_sem)
     load.start()
     full_ref[me] = grad_ref[...]
-    greet(rings.targets)
+    greet([Torus(half, me).place(*at) for half in range(2) for at in around(half, me)])
     rows_all, width = grad_ref.shape
-    quarter = rows_all // RINGS
+    quarter = rows_all // QUARTERS
 
     def prepare():
         def rows_of(i, carry):
@@ -143,14 +165,14 @@
         gw2[...] = jnp.zeros_like(gw2)
         load.wait()
 
-    def consume(origin, ring):
-        rows = pl.ds(ring * quarter, quarter)
+    def consume(origin, part):
+        rows = pl.ds(part * quarter, quarter)
         features = pl.ds(pl.multiple_of(origin * width, width), width)
         block = full_ref[origin, rows, :]
         total[rows, :] += dot(block, w_ref[features, :])
         gw2[features, :] += row_product(block, hidden[rows, :])
 
-    ring_gather(prepare, rings, full_ref, send_sem, recv_sem, consume)
+    tree_gather(prepare, me, full_ref, send_sem, recv_sem, consume)
     part = (total[...] * slope[...]).astype(jnp.bfloat16)
     part_ref[...] = part
     bias_ref[1:2, :] = jnp.sum(part.astype(jnp.float32), axis=0, keepdims=True)
@@ -178,13 +200,13 @@
             pltpu.VMEM((rows, hid), jnp.bfloat16),
             pltpu.VMEM((rows, hid), jnp.float32),
             pltpu.SemaphoreType.DMA,
-            pltpu.SemaphoreType.DMA((RINGS, TP - 1, SUBS)),
-            pltpu.SemaphoreType.DMA((RINGS, TP - 1, SUBS)),
+            pltpu.SemaphoreType.DMA((QUARTERS, TP - 1)),
+            pltpu.SemaphoreType.DMA((QUARTERS, TP - 1)),
         ],
         compiler_params=pltpu.CompilerParams(
             collective_id=0, has_side_effects=True, vmem_limit_bytes=VMEM_LIMIT
         ),
-        name="down_ring",
+        name="down_gather",
     )(out_grad, w_down, pre_act)
 
 
@@ -192,7 +214,6 @@
     part_ref, w_hbm, normed_hbm, norm_ref, gw1_ref, full_ref, w_ref, normed_ref, gw1, w_sem, send_sem, recv_sem
 ):
     me = lax.axis_index("tp")
-    rings = Rings(me)
     loads = [
         pltpu.make_async_copy(w_hbm, w_ref, w_sem.at[0]),
         pltpu.make_async_copy(normed_hbm, normed_ref, w_sem.at[1]),
@@ -200,9 +221,9 @@
     for load in loads:
         load.start()
     full_ref[me] = part_ref[...]
-    greet(rings.targets)
+    greet([Torus(half, me).place(*at) for half in range(2) for at in around(half, me)])
     rows_all, width = part_ref.shape
-    quarter = rows_all // RINGS
+    quarter = rows_all // QUARTERS
     per_owner = gw1.shape[2] // width
 
     def prepare():
@@ -211,15 +232,15 @@
         for load in loads:
             load.wait()
 
-    def consume(origin, ring):
-        rows = pl.ds(ring * quarter, quarter)
+    def consume(origin, part):
+        rows = pl.ds(part * quarter, quarter)
         units = pl.ds(pl.multiple_of(origin * width, width), width)
         within = pl.ds(pl.multiple_of(origin % per_owner * width, width), width)
         block = full_ref[origin, rows, :]
         norm_ref[:, rows] += dot_last(w_ref[:, units], block)
         gw1[origin // per_owner, :, within] += dot(normed_ref[:, rows], block)
 
-    ring_gather(prepare, rings, full_ref, send_sem, recv_sem, consume)
+    tree_gather(prepare, me, full_ref, send_sem, recv_sem, consume)
     gw1_ref[...] = gw1[...].astype(jnp.bfloat16)
 
 
@@ -242,8 +263,8 @@
             pltpu.VMEM((channels, rows), jnp.bfloat16),
             pltpu.VMEM((ctx_count, channels, units // ctx_count), jnp.float32),
             pltpu.SemaphoreType.DMA((2,)),
-            pltpu.SemaphoreType.DMA((RINGS, TP - 1, SUBS)),
-            pltpu.SemaphoreType.DMA((RINGS, TP - 1, SUBS)),
+            pltpu.SemaphoreType.DMA((QUARTERS, TP - 1)),
+            pltpu.SemaphoreType.DMA((QUARTERS, TP - 1)),
         ],
         compiler_params=pltpu.CompilerParams(
             collective_id=1, has_side_effects=True, vmem_limit_bytes=VMEM_LIMIT
@@ -251,23 +272,12 @@
         cost_estimate=pl.CostEstimate(
             flops=4 * rows * units * channels, bytes_accessed=20 * 2**20, transcendentals=0
         ),
-        name="up_ring",
+        name="up_gather",
     )(back_part, w_up_t, normed_t)
 
 
 HALVES = 2
 LANES = 128
-
-
-class Torus:
-    def __init__(self, half, me):
-        z, y = me // SIDE, me % SIDE
-        self.half = half
-        self.along, self.cross = (y, z) if half == 0 else (z, y)
-
-    def place(self, along, cross):
-        along, cross = along % SIDE, cross % SIDE
-        return cross * SIDE + along if self.half == 0 else along * SIDE + cross
 
 
 def hand_kernel(

time: 265 us -> 229 us (0.86)
  Pallas kernels: 237 us -> 201 us
    pallas_call x1, Pallas kernels: 72.6 us -> 52.6 us  [up(): pl.pallas_call(up_kernel, out_shape=(jax.ShapeDtypeStruct((channels, rows...]
    pallas_call x1, Pallas kernels: 72.7 us -> 54.4 us  [down(): pl.pallas_call(down_kernel, out_shape=(jax.ShapeDtypeStruct((rows, hid),...]
  transfers between devices with their start and end apart: 2 -> 2, of which waited for: 0 -> 0; matrix products, arithmetic and copies ran while one was open for 1% -> 1% of each run, Pallas kernels for 62% -> 64%
where the time goes in v3:
time: 229 us
  Pallas kernels  201 us (88%)
  between operations  14.1 us (6%)
  local copies, waits for them, and re-layouts  9.38 us (4%)
  other arithmetic  4.33 us (2%)
    pallas_call x1, Pallas kernels, hand_over(): pl.pallas_call(functools.partial(hand_kernel, full_width, grad_scale), ou...  93.8 us
    pallas_call x1, Pallas kernels, down(): pl.pallas_call(down_kernel, out_shape=(jax.ShapeDtypeStruct((rows, hid),...  54.4 us
    pallas_call x1, Pallas kernels, up(): pl.pallas_call(up_kernel, out_shape=(jax.ShapeDtypeStruct((channels, rows...  52.6 us
    unnamed x12, local copies, waits for them, and re-layouts  8.46 us
  transfers between devices with their start and end apart: 2, of which 0 were waited for; matrix products, arithmetic and copies ran while one was open for 1% of the time, Pallas kernels for 64%

profile of v3, /device:TPU:0, one launch (start us, length us, event | category | flops | bytes accessed | tf_op | source)
XLA Modules:
  0.0 228.9 jit_solution(11496386156887843283)
XLA Ops:
  7.2 0.0 reduce-scatter.3.cloned.1.call-start
  7.2 54.4 %down_gather.1 = (bf16[1024,256]{1,0:T(8,128)(2,1)}, bf16[4096,256]{1,0:T(8,128)(2,1)}, f32[2,256]{1,0:T(2,128)}) custom-call(bf16[1024,256]{1,0:T(8,128)(2,1)} %grad_ref.1, bf16[4096,256]{1,0:T(8,128)(2,1)} %w_hbm.1, bf16[1024,256]{1,0:T(8,128)(2,1)} %pre_ref.1), custom_call_target="tpu_custom_call" | custom-call | tf_op jit(solution)/shard_map/down_gather/pallas_call | solution.py:186
  61.6 0.0 reduce-scatter.3.cloned.1.call-update
  61.7 0.2 reduce-scatter.5.cloned.1.call-start
  61.9 52.6 %up_gather.1 = (f32[800,1024]{1,0:T(8,128)}, bf16[8,800,512]{2,1,0:T(8,128)(2,1)}) custom-call(bf16[1024,256]{1,0:T(8,128)(2,1)} %get-tuple-element.16.part_ref, bf16[800,4096]{1,0:T(8,128)(2,1)} %bitcast.14, bf16[800,1024]{1,0:T(8,128)(2,1)} %bitcast.9), custom_call_target="tpu_custom_call" | custom-call | flops 13421772800 | bytes 20971520 | tf_op jit(solution)/shard_map/up_gather/pallas_call | solution.py:252
  114.5 0.0 copy-start.1
  114.5 0.0 reduce-scatter.5.cloned.1.call-update
  114.5 0.7 copy-done.1
  115.2 0.9 broadcast_in_dim.8.gain_ref
  116.1 93.8 %hand_over.1 = (f32[2,800]{1,0:T(2,128)}, f32[1,256]{1,0:T(1,128)}, f32[1,256]{1,0:T(1,128)}, bf16[256,12800]{1,0:T(8,128)(2,1)}) custom-call(f32[800,1024]{1,0:T(8,128)} %get-tuple-element.18.norm_ref, bf16[800,1024]{1,0:T(8,128)(2,1)} %bitcast.10, f32[800,1]{1,0:T(8,128)} %broadcast_in_dim.8.gain_ref, f32[1,1024]{1,0:T(1,128)} %bitcast.11, ...), custom_call_target="tpu_custom_call" | custom-call | flops 16384000 | bytes 209715200 | tf_op jit(solution)/shard_map/hand_over/pallas_call | solution.py:568
  209.9 0.0 copy-start.3
  209.9 0.0 copy-start.2
  209.9 0.0 copy-start
  209.9 0.0 reduce-scatter.3.cloned.1.call-done
  210.0 1.8 convert_multiply_fusion
  211.8 0.0 reduce-scatter.5.cloned.1.call-done
  211.8 2.5 %multiply_bitcast_fusion = f32[512,800]{0,1:T(8,128)} fusion(bf16[1,800,512]{2,1,0:T(8,128)(2,1)} %reduce-scatter.5.cloned.1.call-done), kind=kLoop, calls=%fused_computation | loop fusion | flops 819200 | bytes 2457600 | tf_op jit(solution)/shard_map/transpose | solution.py:619
  214.3 0.0 copy-done.3
  214.3 0.6 copy.19
  214.9 0.0 copy-done.2
  214.9 0.6 copy.20
  215.4 0.0 copy-done
  215.4 0.6 copy.21
  216.0 6.1 %copy.22 = bf16[256,12800]{1,0:T(8,128)(2,1)} copy(bf16[256,12800]{1,0:T(8,128)(2,1)} %get-tuple-element.35) | data formatting | bytes 13107200
Async XLA Ops:
  7.2 202.8 %reduce-scatter.3.cloned.1.call-start = ((), (), s32[]{:S(2)}) async-start(), calls=%async_computation.2 | async-start | bytes 2359296 | tf_op jit(solution)/shard_map/reduce_scatter | solution.py:614
  61.7 150.1 %reduce-scatter.5.cloned.1.call-start = ((), (), s32[]{:S(2)}) async-start(), calls=%async_computation.3 | async-start | bytes 7372800 | tf_op jit(solution)/shard_map/reduce_scatter | solution.py:618
  114.5 0.7 copy-start.1
  209.9 4.4 %copy-start.3 = (f32[1,256]{1,0:T(1,128)S(1)}, f32[1,256]{1,0:T(1,128)}, u32[]{:S(2)}) copy-start(f32[1,256]{1,0:T(1,128)} %get-tuple-element.20) | copy-start | bytes 3076
  209.9 5.0 %copy-start.2 = (f32[1,256]{1,0:T(1,128)S(1)}, f32[1,256]{1,0:T(1,128)}, u32[]{:S(2)}) copy-start(f32[1,256]{1,0:T(1,128)} %get-tuple-element.21) | copy-start | bytes 3076
  209.9 5.5 %copy-start = (f32[2,800]{1,0:T(2,128)S(1)}, f32[2,800]{1,0:T(2,128)}, u32[]{:S(2)}) copy-start(f32[2,800]{1,0:T(2,128)} %get-tuple-element.34) | copy-start | bytes 19204
Sparse Core Ops, SparseCore 0:
  61.8 32.6 reduce-scatter.2
  114.6 44.9 reduce-scatter.4

commit v4 on v3

--- a/solution.py
+++ b/solution.py
@@ -289,19 +289,16 @@
     std_ref,
     owner_ref,
     bias_ref,
-    ln_ref,
-    up_ref,
-    down_ref,
-    out_ref,
+    sum_ref,
+    final,
     own_y, next_y, far_y, prev_y,
     own_z, next_z, far_z, prev_z,
     message,
-    final,
     product,
     stats_y,
     stats_z,
     sums,
-    near_send, near_recv, relay_send, relay_recv, cross_send, cross_recv, stat_send, stat_recv, sum_send, sum_recv,
+    near_send, near_recv, relay_send, relay_recv, cross_send, cross_recv, own_sem, stat_send, stat_recv, sum_send, sum_recv,
 ):
     me = lax.axis_index("tp")
     group = lax.axis_index("ctx")
@@ -327,27 +324,166 @@
     for d in range(1, ctx_count):
         pl.semaphore_signal(barrier, inc=1, device_id={"ctx": (group + d) % ctx_count}, device_id_type=MESH)
 
+    for i in range(images):
+        rows = pl.ds(i * image_rows, image_rows)
+
+        def some(k, carry):
+            part = pl.ds(pl.multiple_of(k * chunk, chunk), chunk)
+            feature = normed_ref[part, rows].astype(jnp.float32)
+            gained = gain_ref[part, :] * norm_ref[part, rows]
+            return (
+                carry[0] + jnp.sum(gained, axis=0, keepdims=True),
+                carry[1] + jnp.sum(gained * feature, axis=0, keepdims=True),
+            )
+
+        zero = jnp.zeros((1, image_rows), jnp.float32)
+        first, second = lax.fori_loop(0, 5, some, (zero, zero))
+        stats_y[0, i : i + 1, :] = first
+        stats_y[0, images + i : images + i + 1, :] = second
+    pl.semaphore_wait(barrier, HALVES * (SIDE - 1) + ctx_count - 1)
+
+    def stat_copy(half, d):
+        buffer = (stats_y, stats_z)[half]
+        return pltpu.make_async_remote_copy(
+            src_ref=buffer.at[0],
+            dst_ref=buffer.at[d],
+            send_sem=stat_send.at[half, d - 1],
+            recv_sem=stat_recv.at[half, d - 1],
+            device_id={"tp": along_peer(half, d)},
+            device_id_type=MESH,
+        )
+
+    def sum_copy(d):
+        return pltpu.make_async_remote_copy(
+            src_ref=sums.at[0],
+            dst_ref=sums.at[d],
+            send_sem=sum_send.at[d - 1],
+            recv_sem=sum_recv.at[d - 1],
+            device_id={"ctx": (group + d) % ctx_count},
+            device_id_type=MESH,
+        )
+
+    for d in range(1, SIDE):
+        stat_copy(0, d).start()
+    for d in range(1, SIDE):
+        stat_copy(0, d).wait_recv()
+    stats_z[0] = stats_y[0] + stats_y[1] + stats_y[2] + stats_y[3]
+    for d in range(1, SIDE):
+        stat_copy(1, d).start()
+    for d in range(1, SIDE):
+        stat_copy(1, d).wait_recv()
+    means = (stats_z[0] + stats_z[1] + stats_z[2] + stats_z[3]) * (1.0 / full_width)
+
+    def near(half, sign, pair):
+        piece = pl.ds(pair * (images // 2), images // 2)
+        return pltpu.make_async_remote_copy(
+            src_ref=held[half][0].at[piece],
+            dst_ref=held[half][3 if sign == 1 else 1].at[piece],
+            send_sem=near_send.at[half, sign // 2, pair],
+            recv_sem=near_recv.at[half, sign // 2, pair],
+            device_id={"tp": along_peer(half, sign)},
+            device_id_type=MESH,
+        )
+
+    def relay(half, sign):
+        pair = sign // 2
+        piece = pl.ds(pair * (images // 2), images // 2)
+        return pltpu.make_async_remote_copy(
+            src_ref=held[half][3 if sign == 1 else 1].at[piece],
+            dst_ref=held[half][2].at[piece],
+            send_sem=relay_send.at[half, pair],
+            recv_sem=relay_recv.at[half, pair],
+            device_id={"tp": along_peer(half, sign)},
+            device_id_type=MESH,
+        )
+
+    def across(half, target, d):
+        t = torus[half]
+        slot = (t.along + d) % SIDE
+        source = t.cross * SIDE + slot if half == 0 else slot * SIDE + t.cross
+        spot = final.at[half, pl.ds(pl.multiple_of(source * channels, 16), channels)]
+        if target == 0:
+            return pltpu.make_async_copy(message.at[half, 0, d], spot, own_sem.at[half, d])
+        return pltpu.make_async_remote_copy(
+            src_ref=message.at[half, target, d],
+            dst_ref=spot,
+            send_sem=cross_send.at[half, target - 1, d],
+            recv_sem=cross_recv.at[half, target - 1, d],
+            device_id={"tp": cross_peer(half, target)},
+            device_id_type=MESH,
+        )
+
+    for i in range(images):
+        rows = pl.ds(i * image_rows, image_rows)
+        mean_first, mean_second = means[i : i + 1, :], means[images + i : images + i + 1, :]
+        inverse = std_ref[:, rows]
+
+        def visual(k, carry):
+            part = pl.ds(pl.multiple_of(k * chunk, chunk), chunk)
+            value = gain_ref[part, :] * norm_ref[part, rows]
+            feature = normed_ref[part, rows].astype(jnp.float32)
+            seen = (inverse * (value - mean_first - feature * mean_second)).astype(jnp.bfloat16)
+            own_y[i, part, :] = seen[:, :LANES]
+            own_z[i, part, :] = seen[:, LANES:]
+            return carry
+
+        lax.fori_loop(0, 5, visual, 0)
+        if i % 2:
+            for half in range(HALVES):
+                near(half, 1, i // 2).start()
+                near(half, 3, i // 2).start()
+    owners = [owner_ref[0, i] for i in range(images)]
+    slots = []
+    for i in range(images):
+        earlier = jnp.int32(0)
+        for j in range(i):
+            earlier += (owners[j] == owners[i]).astype(jnp.int32)
+        slots.append(owners[i] + earlier)
+
+    def choice(place):
+        source, present = jnp.int32(0), jnp.int32(0)
+        for i in range(images):
+            match = (slots[i] == place).astype(jnp.int32)
+            source += i * match
+            present += match
+        return source, present
+
+    chosen = [[choice(cross_peer(half, target)) for target in range(SIDE)] for half in range(HALVES)]
+
+    def forward(half, d):
+        block = held[half][d]
+        for target in (2, 1, 3, 0):
+            source, present = chosen[half][target]
+            spot = message.at[half, target, d]
+
+            def pick(k, carry):
+                part = pl.ds(pl.multiple_of(k * chunk, chunk), chunk)
+                value = block[source, part, :]
+                spot[part, :] = jnp.where(present > 0, value, jnp.zeros_like(value))
+                return carry
+
+            lax.fori_loop(0, 5, pick, 0)
+            across(half, target, d).start()
+
+    for half in range(HALVES):
+        forward(half, 0)
+    for half in range(HALVES):
+        near(half, 1, 0).wait_recv()
+        relay(half, 1).start()
+    for half in range(HALVES):
+        near(half, 3, 1).wait_recv()
+        relay(half, 3).start()
+    for half in range(HALVES):
+        near(half, 1, 1).wait_recv()
+        forward(half, 3)
+        near(half, 3, 0).wait_recv()
+        forward(half, 1)
+
     ones = jnp.ones((8, image_rows), jnp.float32)
     columns = [jnp.zeros((8, channels), jnp.float32)] * 2
     for i in range(images):
         rows = pl.ds(i * image_rows, image_rows)
-
-        def some(k, carry):
-            part = pl.ds(pl.multiple_of(k * chunk, chunk), chunk)
-            value = norm_ref[part, rows]
-            feature = normed_ref[part, rows].astype(jnp.float32)
-            gained = gain_ref[part, :] * value
-            both = value * feature
-            product[part, :] = both
-            return (
-                carry[0] + jnp.sum(gained, axis=0, keepdims=True),
-                carry[1] + jnp.sum(gained * feature, axis=0, keepdims=True),
-            )
-
-        zero = jnp.zeros((1, image_rows), jnp.float32)
-        first, second = lax.fori_loop(0, 5, some, (zero, zero))
-        stats_y[0, i : i + 1, :] = first
-        stats_y[0, images + i : images + i + 1, :] = second
+        product[...] = norm_ref[:, rows] * normed_ref[:, rows].astype(jnp.float32)
         columns = [
             total
             + lax.dot_general(
@@ -362,150 +498,9 @@
     sums[0, 0:1, 0:channels] = columns[0][0:1]
     sums[0, 1:2, 0:channels] = columns[1][0:1]
     sums[0, 2:4, 0 : bias_ref.shape[1]] = bias_ref[...]
-    pl.semaphore_wait(barrier, HALVES * (SIDE - 1) + ctx_count - 1)
-
-    def stat_copy(half, d):
-        buffer = (stats_y, stats_z)[half]
-        return pltpu.make_async_remote_copy(
-            src_ref=buffer.at[0],
-            dst_ref=buffer.at[d],
-            send_sem=stat_send.at[half, d - 1],
-            recv_sem=stat_recv.at[half, d - 1],
-            device_id={"tp": along_peer(half, d)},
-            device_id_type=MESH,
-        )
-
-    def sum_copy(d):
-        return pltpu.make_async_remote_copy(
-            src_ref=sums.at[0],
-            dst_ref=sums.at[d],
-            send_sem=sum_send.at[d - 1],
-            recv_sem=sum_recv.at[d - 1],
-            device_id={"ctx": (group + d) % ctx_count},
-            device_id_type=MESH,
-        )
-
-    for d in range(1, SIDE):
-        stat_copy(0, d).start()
-    for d in range(1, SIDE):
-        stat_copy(0, d).wait_recv()
-    stats_z[0] = stats_y[0] + stats_y[1] + stats_y[2] + stats_y[3]
-    for d in range(1, SIDE):
-        stat_copy(1, d).start()
-    for d in range(1, SIDE):
-        stat_copy(1, d).wait_recv()
-    means = (stats_z[0] + stats_z[1] + stats_z[2] + stats_z[3]) * (1.0 / full_width)
-
-    def near(half, sign, pair):
-        piece = pl.ds(pair * (images // 2), images // 2)
-        return pltpu.make_async_remote_copy(
-            src_ref=held[half][0].at[piece],
-            dst_ref=held[half][3 if sign == 1 else 1].at[piece],
-            send_sem=near_send.at[half, sign // 2, pair],
-            recv_sem=near_recv.at[half, sign // 2, pair],
-            device_id={"tp": along_peer(half, sign)},
-            device_id_type=MESH,
-        )
-
-    def relay(half, sign):
-        pair = sign // 2
-        piece = pl.ds(pair * (images // 2), images // 2)
-        return pltpu.make_async_remote_copy(
-            src_ref=held[half][3 if sign == 1 else 1].at[piece],
-            dst_ref=held[half][2].at[piece],
-            send_sem=relay_send.at[half, pair],
-            recv_sem=relay_recv.at[half, pair],
-            device_id={"tp": along_peer(half, sign)},
-            device_id_type=MESH,
-        )
-
-    def across(half, target, d):
-        t = torus[half]
-        slot = (t.along + d) % SIDE
-        if half == 0:
-            spot = final.at[0, t.cross, pl.ds(pl.multiple_of(slot * channels, 16), channels)]
-        else:
-            spot = final.at[1, slot, pl.ds(pl.multiple_of(t.cross * channels, 16), channels)]
-        if target == 0:
-            return spot
-        return pltpu.make_async_remote_copy(
-            src_ref=message.at[half, target - 1, d],
-            dst_ref=spot,
-            send_sem=cross_send.at[half, target - 1, d],
-            recv_sem=cross_recv.at[half, target - 1, d],
-            device_id={"tp": cross_peer(half, target)},
-            device_id_type=MESH,
-        )
-
-    for i in range(images):
-        rows = pl.ds(i * image_rows, image_rows)
-        mean_first, mean_second = means[i : i + 1, :], means[images + i : images + i + 1, :]
-        inverse = std_ref[:, rows]
-
-        def visual(k, carry):
-            part = pl.ds(pl.multiple_of(k * chunk, chunk), chunk)
-            value = gain_ref[part, :] * norm_ref[part, rows]
-            feature = normed_ref[part, rows].astype(jnp.float32)
-            seen = (inverse * (value - mean_first - feature * mean_second)).astype(jnp.bfloat16)
-            own_y[i, part, :] = seen[:, :LANES]
-            own_z[i, part, :] = seen[:, LANES:]
-            return carry
-
-        lax.fori_loop(0, 5, visual, 0)
-        if i % 2:
-            for half in range(HALVES):
-                near(half, 1, i // 2).start()
-                near(half, 3, i // 2).start()
     for d in range(1, ctx_count):
         sum_copy(d).start()
 
-    owners = [owner_ref[0, i] for i in range(images)]
-    slots = []
-    for i in range(images):
-        earlier = jnp.int32(0)
-        for j in range(i):
-            earlier += (owners[j] == owners[i]).astype(jnp.int32)
-        slots.append(owners[i] + earlier)
-
-    def choice(place):
-        source, present = jnp.int32(0), jnp.int32(0)
-        for i in range(images):
-            match = (slots[i] == place).astype(jnp.int32)
-            source += i * match
-            present += match
-        return source, present
-
-    chosen = [[choice(cross_peer(half, target)) for target in range(SIDE)] for half in range(HALVES)]
-
-    def forward(half, d):
-        block = held[half][d]
-        for target in (2, 1, 3, 0):
-            source, present = chosen[half][target]
-            spot = across(half, 0, d) if target == 0 else message.at[half, target - 1, d]
-
-            def pick(k, carry):
-                part = pl.ds(pl.multiple_of(k * chunk, chunk), chunk)
-                value = block[source, part, :]
-                spot[part, :] = jnp.where(present > 0, value, jnp.zeros_like(value))
-                return carry
-
-            lax.fori_loop(0, 5, pick, 0)
-            if target:
-                across(half, target, d).start()
-
-    for half in range(HALVES):
-        forward(half, 0)
-    for half in range(HALVES):
-        near(half, 1, 0).wait_recv()
-        relay(half, 1).start()
-    for half in range(HALVES):
-        near(half, 3, 1).wait_recv()
-        relay(half, 3).start()
-    for half in range(HALVES):
-        near(half, 1, 1).wait_recv()
-        forward(half, 3)
-        near(half, 3, 0).wait_recv()
-        forward(half, 1)
     for half in range(HALVES):
         relay(half, 1).wait_recv()
         relay(half, 3).wait_recv()
@@ -516,34 +511,13 @@
     whole = sums[0]
     for d in range(1, ctx_count):
         whole = whole + sums[d]
-    whole = whole * grad_scale
-    ln_ref[...] = whole[0:2, 0:channels]
-    down_ref[...] = whole[2:3, 0 : bias_ref.shape[1]]
-    up_ref[...] = whole[3:4, 0 : bias_ref.shape[1]]
-
-    wide = SIDE * channels
-
-    def turn(half, z):
-        def tile(k, carry):
-            block = final[half, z, pl.ds(pl.multiple_of(k * LANES, LANES), LANES), :]
-            at = pl.ds(pl.multiple_of(z * wide + k * LANES, LANES), LANES)
-            out_ref[half * LANES : (half + 1) * LANES, at] = block.T
-            return carry
-
-        lax.fori_loop(0, wide // LANES, tile, 0)
-
-    for d in (0, 3, 1, 2):
-        if d == 0:
-            turn(0, torus[0].cross)
-        else:
-            for e in range(SIDE):
-                across(0, d, e).wait_recv()
-            turn(0, (torus[0].cross - d + SIDE) % SIDE)
-    for e in (0, 3, 1, 2):
-        for d in range(1, SIDE):
-            across(1, d, e).wait_recv()
-        turn(1, (torus[1].along + e) % SIDE)
-
+    sum_ref[...] = whole * grad_scale
+
+    for half in range(HALVES):
+        for d in range(SIDE):
+            for target in range(1, SIDE):
+                across(half, target, d).wait_recv()
+            across(half, 0, d).wait()
     for half in range(HALVES):
         for sign in (1, 3):
             for pair in range(2):
@@ -561,24 +535,20 @@
     channels, rows = norm_t.shape
     images = owner_map.shape[1]
     image_rows = rows // images
-    width = bias.shape[1]
     vmem = pl.BlockSpec(memory_space=pltpu.VMEM)
     block = pltpu.VMEM((images, channels, LANES), jnp.bfloat16)
     dma = pltpu.SemaphoreType.DMA
     return pl.pallas_call(
         functools.partial(hand_kernel, full_width, grad_scale),
         out_shape=(
-            jax.ShapeDtypeStruct((2, channels), jnp.float32),
-            jax.ShapeDtypeStruct((1, width), jnp.float32),
-            jax.ShapeDtypeStruct((1, width), jnp.float32),
-            jax.ShapeDtypeStruct((image_rows, TP * channels), jnp.bfloat16),
+            jax.ShapeDtypeStruct((8, 1024), jnp.float32),
+            jax.ShapeDtypeStruct((HALVES, TP * channels, LANES), jnp.bfloat16),
         ),
         in_specs=[vmem, vmem, vmem, vmem, pl.BlockSpec(memory_space=pltpu.SMEM), vmem],
-        out_specs=(vmem, vmem, vmem, vmem),
+        out_specs=(vmem, pl.BlockSpec(memory_space=pl.ANY)),
         scratch_shapes=[block] * 8
         + [
-            pltpu.VMEM((HALVES, SIDE - 1, SIDE, channels, LANES), jnp.bfloat16),
-            pltpu.VMEM((HALVES, SIDE, SIDE * channels, LANES), jnp.bfloat16),
+            pltpu.VMEM((HALVES, SIDE, SIDE, channels, LANES), jnp.bfloat16),
             pltpu.VMEM((channels, image_rows), jnp.float32),
             pltpu.VMEM((SIDE, 2 * images, image_rows), jnp.float32),
             pltpu.VMEM((SIDE, 2 * images, image_rows), jnp.float32),
@@ -589,6 +559,7 @@
             dma((HALVES, 2)),
             dma((HALVES, SIDE - 1, SIDE)),
             dma((HALVES, SIDE - 1, SIDE)),
+            dma((HALVES, SIDE)),
             dma((HALVES, SIDE - 1)),
             dma((HALVES, SIDE - 1)),
             dma((ctx_count - 1,)),
@@ -604,20 +575,67 @@
     )(norm_t, normed_t, gain, inverse_std, owner_map, bias)
 
 
+def finish_kernel(grad_scale, final_ref, gw2_ref, gw1_ref, sum_ref, out_ref, grad_w2_ref, grad_w1_ref, ln_ref, up_ref, down_ref):
+    lanes = out_ref.shape[0]
+    row = lax.broadcasted_iota(jnp.int32, (lanes, lanes), 0)
+    column = lax.broadcasted_iota(jnp.int32, (lanes, lanes), 1)
+    identity = jnp.where(row == column, 1.0, 0.0).astype(jnp.bfloat16)
+    block = jnp.concatenate([final_ref[0], final_ref[1]], axis=1)
+    out_ref[...] = dot_last(identity, block).astype(jnp.bfloat16)
+    grad_w2_ref[...] = gw2_ref[...].astype(jnp.float32) * grad_scale
+    grad_w1_ref[...] = gw1_ref[...].astype(jnp.float32) * grad_scale
+    ln_ref[...] = sum_ref[0:2, 0 : ln_ref.shape[1]]
+    down_ref[...] = sum_ref[2:3, 0 : down_ref.shape[1]]
+    up_ref[...] = sum_ref[3:4, 0 : up_ref.shape[1]]
+
+
+def finish(final, gw2, gw1_t, sums, width, grad_scale):
+    steps = 10
+    wide = final.shape[1] // steps
+    channels, units = gw1_t.shape
+    vmem = pl.BlockSpec(memory_space=pltpu.VMEM)
+    last = 7
+    return pl.pallas_call(
+        functools.partial(finish_kernel, grad_scale),
+        grid=(steps,),
+        out_shape=(
+            jax.ShapeDtypeStruct((HALVES * LANES, final.shape[1]), jnp.bfloat16),
+            jax.ShapeDtypeStruct(gw2.shape, jnp.float32),
+            jax.ShapeDtypeStruct(gw1_t.shape, jnp.float32),
+            jax.ShapeDtypeStruct((2, channels), jnp.float32),
+            jax.ShapeDtypeStruct((1, width), jnp.float32),
+            jax.ShapeDtypeStruct((1, width), jnp.float32),
+        ),
+        in_specs=[
+            pl.BlockSpec((HALVES, wide, LANES), lambda k: (0, k, 0)),
+            pl.BlockSpec((gw2.shape[0] // 8, width), lambda k: (jnp.minimum(k, last), 0)),
+            pl.BlockSpec((channels // steps, units), lambda k: (k, 0)),
+            vmem,
+        ],
+        out_specs=(
+            pl.BlockSpec((HALVES * LANES, wide), lambda k: (0, k)),
+            pl.BlockSpec((gw2.shape[0] // 8, width), lambda k: (jnp.minimum(k, last), 0)),
+            pl.BlockSpec((channels // steps, units), lambda k: (k, 0)),
+            vmem,
+            vmem,
+            vmem,
+        ),
+        compiler_params=pltpu.CompilerParams(vmem_limit_bytes=VMEM_LIMIT),
+        name="finish",
+    )(final, gw2, gw1_t, sums)
+
+
 def per_device(out_grad, pre_act, normed, inverse_std, w_up, w_down, ln_gain, owner_map):
     ctx_count = lax.axis_size("ctx")
     tp_count = lax.axis_size("tp")
     row_count = out_grad.shape[0]
     grad_scale = float(row_count * ctx_count) ** (-0.5)
     back_part, gw2, bias = down(out_grad, w_down, pre_act)
-    grad_w2 = (
-        lax.psum_scatter(gw2, "ctx", scatter_dimension=0, tiled=True).astype(jnp.float32) * grad_scale
-    )
+    gw2 = lax.psum_scatter(gw2, "ctx", scatter_dimension=0, tiled=True)
     normed_t = normed.T
     norm_t, gw1 = up(back_part, w_up.T, normed_t, ctx_count)
-    grad_w1_t = lax.psum_scatter(gw1, "ctx", scatter_dimension=0, tiled=True)
-    grad_w1 = (grad_w1_t[0].astype(jnp.float32) * grad_scale).T
-    ln_grads, bias_up, bias_down, vit_grad = hand_over(
+    gw1 = lax.psum_scatter(gw1, "ctx", scatter_dimension=0, tiled=True)
+    sums, final = hand_over(
         norm_t,
         normed_t,
         ln_gain[:, None],
@@ -628,7 +646,10 @@
         grad_scale,
         ctx_count,
     )
-    return (grad_w2, grad_w1, bias_up[0], bias_down[0], ln_grads, vit_grad)
+    vit_grad, grad_w2, grad_w1_t, ln_grads, bias_up, bias_down = finish(
+        final, gw2, gw1[0], sums, bias.shape[1], grad_scale
+    )
+    return (grad_w2, grad_w1_t.T, bias_up[0], bias_down[0], ln_grads, vit_grad)
 
 
 def solution(mesh):

time: 229 us -> 212 us (0.926)
  local copies, waits for them, and re-layouts: 9.38 us -> 1.58 us
  Pallas kernels: 201 us -> 196 us
  other arithmetic: 4.33 us -> 0 us
    pallas_call x1, Pallas kernels: 93.8 us -> 77.7 us  [hand_over(): pl.pallas_call(functools.partial(hand_kernel, full_width, grad_scale), ou...]
    pallas_call x0 -> x1, Pallas kernels: none -> 10.9 us  [finish(): pl.pallas_call(functools.partial(finish_kernel, grad_scale), grid=(steps,...]
    unnamed x12 -> x2, local copies, waits for them, and re-layouts: 8.46 us -> 0.66 us
    transpose x1 -> x0, other arithmetic: 2.54 us -> none  [per_device(): grad_w1 = (grad_w1_t[0].astype(jnp.float32) * grad_scale).T]
  transfers between devices with their start and end apart: 2 -> 2, of which waited for: 0 -> 0; matrix products, arithmetic and copies ran while one was open for 1% -> 0% of each run, Pallas kernels for 64% -> 62%
where the time goes in v4:
time: 212 us
  Pallas kernels  196 us (92%)
  between operations  14.1 us (7%)
    pallas_call x1, Pallas kernels, hand_over(): pl.pallas_call(functools.partial(hand_kernel, full_width, grad_scale), ou...  77.7 us
    pallas_call x1, Pallas kernels, down(): pl.pallas_call(down_kernel, out_shape=(jax.ShapeDtypeStruct((rows, hid),...  54.4 us
    pallas_call x1, Pallas kernels, up(): pl.pallas_call(up_kernel, out_shape=(jax.ShapeDtypeStruct((channels, rows...  52.6 us
    pallas_call x1, Pallas kernels, finish(): pl.pallas_call(functools.partial(finish_kernel, grad_scale), grid=(steps,...  10.9 us
  transfers between devices with their start and end apart: 2, of which 0 were waited for; matrix products, arithmetic and copies ran while one was open for 0% of the time, Pallas kernels for 62%

profile of v4, /device:TPU:0, one launch (start us, length us, event | category | flops | bytes accessed | tf_op | source)
XLA Modules:
  0.0 211.6 jit_solution(16691107272981306969)
XLA Ops:
  7.2 0.0 reduce-scatter.3.cloned.1.call-start
  7.2 54.4 %down_gather.1 = (bf16[1024,256]{1,0:T(8,128)(2,1)}, bf16[4096,256]{1,0:T(8,128)(2,1)}, f32[2,256]{1,0:T(2,128)}) custom-call(bf16[1024,256]{1,0:T(8,128)(2,1)} %grad_ref.1, bf16[4096,256]{1,0:T(8,128)(2,1)} %w_hbm.1, bf16[1024,256]{1,0:T(8,128)(2,1)} %pre_ref.1), custom_call_target="tpu_custom_call" | custom-call | tf_op jit(solution)/shard_map/down_gather/pallas_call | solution.py:186
  61.6 0.0 reduce-scatter.3.cloned.1.call-update
  61.7 0.2 reduce-scatter.5.cloned.1.call-start
  61.9 52.6 %up_gather.1 = (f32[800,1024]{1,0:T(8,128)}, bf16[8,800,512]{2,1,0:T(8,128)(2,1)}) custom-call(bf16[1024,256]{1,0:T(8,128)(2,1)} %get-tuple-element.19.part_ref, bf16[800,4096]{1,0:T(8,128)(2,1)} %bitcast.11, bf16[800,1024]{1,0:T(8,128)(2,1)} %bitcast.7), custom_call_target="tpu_custom_call" | custom-call | flops 13421772800 | bytes 20971520 | tf_op jit(solution)/shard_map/up_gather/pallas_call | solution.py:252
  114.5 0.0 copy-start
  114.5 0.0 reduce-scatter.5.cloned.1.call-update
  114.5 0.7 copy-done
  115.2 0.9 broadcast_in_dim.8.gain_ref
  116.1 77.7 %hand_over.1 = (f32[8,1024]{1,0:T(8,128)}, bf16[2,12800,128]{2,1,0:T(8,128)(2,1)}) custom-call(f32[800,1024]{1,0:T(8,128)} %get-tuple-element.20.norm_ref, bf16[800,1024]{1,0:T(8,128)(2,1)} %bitcast.8, f32[800,1]{1,0:T(8,128)} %broadcast_in_dim.8.gain_ref, f32[1,1024]{1,0:T(1,128)} %bitcast.10, s32[1,4]{1,0:T(1,128)} %owner_ref.1, ...), custom_call_target="tpu_custom_call" | custom-call | flops 16384000 | bytes 209715200 | tf_op jit(solution)/shard_map/hand_over/pallas_call | solution.py:541
  193.8 0.0 reduce-scatter.3.cloned.1.call-done.gw2_ref
  193.8 0.0 reduce-scatter.5.cloned.1.call-done
  193.9 10.9 %finish.1 = (bf16[256,12800]{1,0:T(8,128)(2,1)}, f32[512,256]{1,0:T(8,128)}, f32[800,512]{1,0:T(8,128)}, f32[2,800]{1,0:T(2,128)}, f32[1,256]{1,0:T(1,128)}, /*index=5*/f32[1,256]{1,0:T(1,128)}) custom-call(bf16[2,12800,128]{2,1,0:T(8,128)(2,1)} %get-tuple-element.22.final_ref, bf16[512,256]{1,0:T(8,128)(2,1)} %reduce-scatter.3.cloned.1.call-done.gw2_ref, ...), custom_call_target="tpu_custom_call" | custom-call | tf_op jit(solution)/shard_map/finish/pallas_call | solution.py:598
Async XLA Ops:
  7.2 186.7 %reduce-scatter.3.cloned.1.call-start = ((), (), s32[]{:S(2)}) async-start(), calls=%async_computation.2 | async-start | bytes 2359296 | tf_op jit(solution)/shard_map/reduce_scatter | solution.py:634
  61.7 132.2 %reduce-scatter.5.cloned.1.call-start = ((), (), s32[]{:S(2)}) async-start(), calls=%async_computation.3 | async-start | bytes 7372800 | tf_op jit(solution)/shard_map/reduce_scatter | solution.py:637
  114.5 0.7 copy-start
Sparse Core Ops, SparseCore 0:
  61.8 32.6 reduce-scatter.2
  114.6 43.5 reduce-scatter.4

commit v5 on v4

--- a/solution.py
+++ b/solution.py
@@ -68,6 +68,30 @@
 )
 
 
+def full_at(y, z):
+    turns = ((y, z), (-y % SIDE, -z % SIDE), (z, y), (-z % SIDE, -y % SIDE))
+    return max(ARRIVALS.index(turn) for turn in turns if turn != (0, 0))
+
+
+FULL_AT = {(y, z): full_at(y, z) for y in range(SIDE) for z in range(SIDE) if (y, z) != (0, 0)}
+FULL_AT[(0, 0)] = min(FULL_AT.values())
+
+
+def gain_column(gain_ref, column_ref):
+    channels = gain_ref.shape[0]
+    rows = channels // 5
+    at = lax.broadcasted_iota(jnp.int32, (rows, channels), 1) - lax.broadcasted_iota(
+        jnp.int32, (rows, channels), 0
+    )
+
+    def some(k, carry):
+        picked = jnp.where(at == k * rows, jnp.broadcast_to(gain_ref[...], (rows, channels)), 0.0)
+        column_ref[pl.ds(pl.multiple_of(k * rows, rows), rows), :] = jnp.sum(picked, axis=1, keepdims=True)
+        return carry
+
+    lax.fori_loop(0, 5, some, 0)
+
+
 def numbered(values, index):
     out = jnp.int32(values[0])
     for i, value in enumerate(values[1:], 1):
@@ -75,7 +99,7 @@
     return out
 
 
-def tree_gather(prepare, me, full_ref, send_sem, recv_sem, consume):
+def tree_gather(prepare, me, full_ref, send_sem, recv_sem, consume, complete):
     rows = full_ref.shape[1] // QUARTERS
     torus = [Torus(half, me) for half in range(2)]
 
@@ -128,6 +152,14 @@
 
         for quarter in range(QUARTERS):
             consume(origin(quarter, along, cross), quarter)
+        for number in sorted(set(FULL_AT.values())):
+
+            @pl.when(k == number)
+            def _():
+                for block, at in FULL_AT.items():
+                    if at == number:
+                        complete(torus[0].place(torus[0].along + block[0], torus[0].cross + block[1]))
+
         return carry
 
     lax.fori_loop(0, TP - 1, arrive, 0)
@@ -141,7 +173,7 @@
 
 
 def down_kernel(
-    grad_ref, w_hbm, pre_ref, part_ref, gw2_ref, bias_ref, full_ref, w_ref, total, gw2, hidden, slope, w_sem, send_sem, recv_sem
+    grad_ref, w_hbm, pre_ref, part_ref, gw2_hbm, bias_ref, full_ref, w_ref, total, gw2, short, hidden, slope, w_sem, out_sem, send_sem, recv_sem
 ):
     me = lax.axis_index("tp")
     load = pltpu.make_async_copy(w_hbm, w_ref, w_sem)
@@ -172,11 +204,21 @@
         total[rows, :] += dot(block, w_ref[features, :])
         gw2[features, :] += row_product(block, hidden[rows, :])
 
-    tree_gather(prepare, me, full_ref, send_sem, recv_sem, consume)
+    def write(origin):
+        features = pl.ds(pl.multiple_of(origin * width, width), width)
+        return pltpu.make_async_copy(short.at[features], gw2_hbm.at[features], out_sem.at[origin])
+
+    def complete(origin):
+        features = pl.ds(pl.multiple_of(origin * width, width), width)
+        short[features, :] = gw2[features, :].astype(jnp.bfloat16)
+        write(origin).start()
+
+    tree_gather(prepare, me, full_ref, send_sem, recv_sem, consume, complete)
     part = (total[...] * slope[...]).astype(jnp.bfloat16)
     part_ref[...] = part
     bias_ref[1:2, :] = jnp.sum(part.astype(jnp.float32), axis=0, keepdims=True)
-    gw2_ref[...] = gw2[...].astype(jnp.bfloat16)
+    for origin in range(TP):
+        write(origin).wait()
 
 
 def down(out_grad, w_down, pre_act):
@@ -191,15 +233,17 @@
             jax.ShapeDtypeStruct((2, hid), jnp.float32),
         ),
         in_specs=[vmem, pl.BlockSpec(memory_space=pl.ANY), vmem],
-        out_specs=(vmem, vmem, vmem),
+        out_specs=(vmem, pl.BlockSpec(memory_space=pl.ANY), vmem),
         scratch_shapes=[
             pltpu.VMEM((TP, rows, width), jnp.bfloat16),
             pltpu.VMEM((features, hid), jnp.bfloat16),
             pltpu.VMEM((rows, hid), jnp.float32),
             pltpu.VMEM((features, hid), jnp.float32),
+            pltpu.VMEM((features, hid), jnp.bfloat16),
             pltpu.VMEM((rows, hid), jnp.bfloat16),
             pltpu.VMEM((rows, hid), jnp.float32),
             pltpu.SemaphoreType.DMA,
+            pltpu.SemaphoreType.DMA((TP,)),
             pltpu.SemaphoreType.DMA((QUARTERS, TP - 1)),
             pltpu.SemaphoreType.DMA((QUARTERS, TP - 1)),
         ],
@@ -211,7 +255,8 @@
 
 
 def up_kernel(
-    part_ref, w_hbm, normed_hbm, norm_ref, gw1_ref, full_ref, w_ref, normed_ref, gw1, w_sem, send_sem, recv_sem
+    part_ref, w_hbm, normed_hbm, gain_ref, norm_hbm, gw1_hbm, stat_ref,
+    full_ref, w_ref, normed_ref, norm_ref, gw1, short, column, w_sem, out_sem, send_sem, recv_sem,
 ):
     me = lax.axis_index("tp")
     loads = [
@@ -225,10 +270,15 @@
     rows_all, width = part_ref.shape
     quarter = rows_all // QUARTERS
     per_owner = gw1.shape[2] // width
+    channels = norm_ref.shape[0]
+    chunk = channels // 5
+    images = stat_ref.shape[0] // 2
+    image_rows = rows_all // images
 
     def prepare():
         norm_ref[...] = jnp.zeros_like(norm_ref)
         gw1[...] = jnp.zeros_like(gw1)
+        gain_column(gain_ref, column)
         for load in loads:
             load.wait()
 
@@ -240,11 +290,51 @@
         norm_ref[:, rows] += dot_last(w_ref[:, units], block)
         gw1[origin // per_owner, :, within] += dot(normed_ref[:, rows], block)
 
-    tree_gather(prepare, me, full_ref, send_sem, recv_sem, consume)
-    gw1_ref[...] = gw1[...].astype(jnp.bfloat16)
-
-
-def up(back_part, w_up_t, normed_t, ctx_count):
+    def write(origin):
+        within = pl.ds(pl.multiple_of(origin % per_owner * width, width), width)
+        owner = origin // per_owner
+        return pltpu.make_async_copy(
+            short.at[owner, :, within], gw1_hbm.at[owner, :, within], out_sem.at[origin]
+        )
+
+    def complete(origin):
+        within = pl.ds(pl.multiple_of(origin % per_owner * width, width), width)
+        owner = origin // per_owner
+
+        def some(k, carry):
+            part = pl.ds(pl.multiple_of(k * chunk, chunk), chunk)
+            short[owner, part, within] = gw1[owner, part, within].astype(jnp.bfloat16)
+            return carry
+
+        lax.fori_loop(0, 5, some, 0)
+        write(origin).start()
+
+    tree_gather(prepare, me, full_ref, send_sem, recv_sem, consume, complete)
+    store = pltpu.make_async_copy(norm_ref, norm_hbm, w_sem.at[0])
+    store.start()
+
+    for i in range(images):
+        rows = pl.ds(i * image_rows, image_rows)
+
+        def some(k, carry):
+            part = pl.ds(pl.multiple_of(k * chunk, chunk), chunk)
+            feature = normed_ref[part, rows].astype(jnp.float32)
+            gained = column[part, :] * norm_ref[part, rows]
+            return (
+                carry[0] + jnp.sum(gained, axis=0, keepdims=True),
+                carry[1] + jnp.sum(gained * feature, axis=0, keepdims=True),
+            )
+
+        zero = jnp.zeros((1, image_rows), jnp.float32)
+        first, second = lax.fori_loop(0, 5, some, (zero, zero))
+        stat_ref[i : i + 1, :] = first
+        stat_ref[images + i : images + i + 1, :] = second
+    store.wait()
+    for origin in range(TP):
+        write(origin).wait()
+
+
+def up(back_part, w_up_t, normed_t, gain, ctx_count, images):
     rows, width = back_part.shape
     channels, units = w_up_t.shape
     vmem = pl.BlockSpec(memory_space=pltpu.VMEM)
@@ -254,15 +344,20 @@
         out_shape=(
             jax.ShapeDtypeStruct((channels, rows), jnp.float32),
             jax.ShapeDtypeStruct((ctx_count, channels, units // ctx_count), jnp.bfloat16),
-        ),
-        in_specs=[vmem, anywhere, anywhere],
-        out_specs=(vmem, vmem),
+            jax.ShapeDtypeStruct((2 * images, rows // images), jnp.float32),
+        ),
+        in_specs=[vmem, anywhere, anywhere, vmem],
+        out_specs=(anywhere, anywhere, vmem),
         scratch_shapes=[
             pltpu.VMEM((TP, rows, width), jnp.bfloat16),
             pltpu.VMEM((channels, units), jnp.bfloat16),
             pltpu.VMEM((channels, rows), jnp.bfloat16),
+            pltpu.VMEM((channels, rows), jnp.float32),
             pltpu.VMEM((ctx_count, channels, units // ctx_count), jnp.float32),
+            pltpu.VMEM((ctx_count, channels, units // ctx_count), jnp.bfloat16),
+            pltpu.VMEM((channels, 1), jnp.float32),
             pltpu.SemaphoreType.DMA((2,)),
+            pltpu.SemaphoreType.DMA((TP,)),
             pltpu.SemaphoreType.DMA((QUARTERS, TP - 1)),
             pltpu.SemaphoreType.DMA((QUARTERS, TP - 1)),
         ],
@@ -273,7 +368,7 @@
             flops=4 * rows * units * channels, bytes_accessed=20 * 2**20, transcendentals=0
         ),
         name="up_gather",
-    )(back_part, w_up_t, normed_t)
+    )(back_part, w_up_t, normed_t, gain)
 
 
 HALVES = 2
@@ -283,22 +378,26 @@
 def hand_kernel(
     full_width,
     grad_scale,
-    norm_ref,
-    normed_ref,
-    gain_ref,
+    norm_hbm,
+    normed_hbm,
+    gain_row,
     std_ref,
     owner_ref,
     bias_ref,
+    stat_ref,
     sum_ref,
     final,
     own_y, next_y, far_y, prev_y,
     own_z, next_z, far_z, prev_z,
     message,
+    norm_ref,
+    normed_ref,
+    gain_ref,
     product,
     stats_y,
     stats_z,
     sums,
-    near_send, near_recv, relay_send, relay_recv, cross_send, cross_recv, own_sem, stat_send, stat_recv, sum_send, sum_recv,
+    load_sem, near_send, near_recv, relay_send, relay_recv, cross_send, cross_recv, own_sem, stat_send, stat_recv, sum_send, sum_recv,
 ):
     me = lax.axis_index("tp")
     group = lax.axis_index("ctx")
@@ -324,22 +423,14 @@
     for d in range(1, ctx_count):
         pl.semaphore_signal(barrier, inc=1, device_id={"ctx": (group + d) % ctx_count}, device_id_type=MESH)
 
-    for i in range(images):
-        rows = pl.ds(i * image_rows, image_rows)
-
-        def some(k, carry):
-            part = pl.ds(pl.multiple_of(k * chunk, chunk), chunk)
-            feature = normed_ref[part, rows].astype(jnp.float32)
-            gained = gain_ref[part, :] * norm_ref[part, rows]
-            return (
-                carry[0] + jnp.sum(gained, axis=0, keepdims=True),
-                carry[1] + jnp.sum(gained * feature, axis=0, keepdims=True),
-            )
-
-        zero = jnp.zeros((1, image_rows), jnp.float32)
-        first, second = lax.fori_loop(0, 5, some, (zero, zero))
-        stats_y[0, i : i + 1, :] = first
-        stats_y[0, images + i : images + i + 1, :] = second
+    loads = [
+        pltpu.make_async_copy(norm_hbm, norm_ref, load_sem.at[0]),
+        pltpu.make_async_copy(normed_hbm, normed_ref, load_sem.at[1]),
+    ]
+    for load in loads:
+        load.start()
+    stats_y[0] = stat_ref[...]
+    gain_column(gain_row, gain_ref)
     pl.semaphore_wait(barrier, HALVES * (SIDE - 1) + ctx_count - 1)
 
     def stat_copy(half, d):
@@ -372,6 +463,8 @@
         stat_copy(1, d).start()
     for d in range(1, SIDE):
         stat_copy(1, d).wait_recv()
+    for load in loads:
+        load.wait()
     means = (stats_z[0] + stats_z[1] + stats_z[2] + stats_z[3]) * (1.0 / full_width)
 
     def near(half, sign, pair):
@@ -531,7 +624,7 @@
         sum_copy(d).wait_send()
 
 
-def hand_over(norm_t, normed_t, gain, inverse_std, owner_map, bias, full_width, grad_scale, ctx_count):
+def hand_over(norm_t, normed_t, gain, inverse_std, owner_map, bias, stats, full_width, grad_scale, ctx_count):
     channels, rows = norm_t.shape
     images = owner_map.shape[1]
     image_rows = rows // images
@@ -544,15 +637,27 @@
             jax.ShapeDtypeStruct((8, 1024), jnp.float32),
             jax.ShapeDtypeStruct((HALVES, TP * channels, LANES), jnp.bfloat16),
         ),
-        in_specs=[vmem, vmem, vmem, vmem, pl.BlockSpec(memory_space=pltpu.SMEM), vmem],
+        in_specs=[
+            pl.BlockSpec(memory_space=pl.ANY),
+            pl.BlockSpec(memory_space=pl.ANY),
+            vmem,
+            vmem,
+            pl.BlockSpec(memory_space=pltpu.SMEM),
+            vmem,
+            vmem,
+        ],
         out_specs=(vmem, pl.BlockSpec(memory_space=pl.ANY)),
         scratch_shapes=[block] * 8
         + [
             pltpu.VMEM((HALVES, SIDE, SIDE, channels, LANES), jnp.bfloat16),
+            pltpu.VMEM((channels, rows), jnp.float32),
+            pltpu.VMEM((channels, rows), jnp.bfloat16),
+            pltpu.VMEM((channels, 1), jnp.float32),
             pltpu.VMEM((channels, image_rows), jnp.float32),
             pltpu.VMEM((SIDE, 2 * images, image_rows), jnp.float32),
             pltpu.VMEM((SIDE, 2 * images, image_rows), jnp.float32),
             pltpu.VMEM((ctx_count, 8, 1024), jnp.float32),
+            dma((2,)),
             dma((HALVES, 2, 2)),
             dma((HALVES, 2, 2)),
             dma((HALVES, 2)),
@@ -572,32 +677,76 @@
             flops=20 * rows * channels, bytes_accessed=200 * 2**20, transcendentals=0
         ),
         name="hand_over",
-    )(norm_t, normed_t, gain, inverse_std, owner_map, bias)
-
-
-def finish_kernel(grad_scale, final_ref, gw2_ref, gw1_ref, sum_ref, out_ref, grad_w2_ref, grad_w1_ref, ln_ref, up_ref, down_ref):
-    lanes = out_ref.shape[0]
+    )(norm_t, normed_t, gain, inverse_std, owner_map, bias, stats)
+
+
+STEPS = 10
+
+
+def finish_kernel(
+    grad_scale, final_hbm, gw2_hbm, gw1_hbm, sum_ref, out_hbm, grad_w2_hbm, grad_w1_hbm, ln_ref, up_ref, down_ref,
+    final, out, gw2, grad_w2, gw1, grad_w1, in_sem, out_sem,
+):
+    wide = final.shape[1] // STEPS
+    small_in = [
+        pltpu.make_async_copy(gw2_hbm, gw2, in_sem.at[STEPS]),
+        pltpu.make_async_copy(gw1_hbm, gw1, in_sem.at[STEPS + 1]),
+    ]
+    small_out = [
+        pltpu.make_async_copy(grad_w2, grad_w2_hbm, out_sem.at[STEPS]),
+        pltpu.make_async_copy(grad_w1, grad_w1_hbm, out_sem.at[STEPS + 1]),
+    ]
+
+    def load(k):
+        part = pl.ds(pl.multiple_of(k * wide, wide), wide)
+        return pltpu.make_async_copy(final_hbm.at[:, part], final.at[:, part], in_sem.at[k])
+
+    def store(k):
+        part = pl.ds(pl.multiple_of(k * wide, wide), wide)
+        return pltpu.make_async_copy(out.at[:, part], out_hbm.at[:, part], out_sem.at[k])
+
+    load(0).start()
+    load(1).start()
+    for copy in small_in:
+        copy.start()
+    for k in range(2, STEPS):
+        load(k).start()
+    lanes = out.shape[0]
     row = lax.broadcasted_iota(jnp.int32, (lanes, lanes), 0)
     column = lax.broadcasted_iota(jnp.int32, (lanes, lanes), 1)
     identity = jnp.where(row == column, 1.0, 0.0).astype(jnp.bfloat16)
-    block = jnp.concatenate([final_ref[0], final_ref[1]], axis=1)
-    out_ref[...] = dot_last(identity, block).astype(jnp.bfloat16)
-    grad_w2_ref[...] = gw2_ref[...].astype(jnp.float32) * grad_scale
-    grad_w1_ref[...] = gw1_ref[...].astype(jnp.float32) * grad_scale
+
+    def turn(k, carry):
+        part = pl.ds(pl.multiple_of(k * wide, wide), wide)
+        load(k).wait()
+        block = jnp.concatenate([final[0, part, :], final[1, part, :]], axis=1)
+        out[:, part] = dot_last(identity, block).astype(jnp.bfloat16)
+        store(k).start()
+        return carry
+
+    lax.fori_loop(0, STEPS // 2, turn, 0)
+    for copy in small_in:
+        copy.wait()
+    grad_w2[...] = gw2[...].astype(jnp.float32) * grad_scale
+    small_out[0].start()
+    grad_w1[...] = gw1[...].astype(jnp.float32) * grad_scale
+    small_out[1].start()
+    lax.fori_loop(STEPS // 2, STEPS, turn, 0)
     ln_ref[...] = sum_ref[0:2, 0 : ln_ref.shape[1]]
     down_ref[...] = sum_ref[2:3, 0 : down_ref.shape[1]]
     up_ref[...] = sum_ref[3:4, 0 : up_ref.shape[1]]
+    for copy in small_out:
+        copy.wait()
+    for k in range(STEPS):
+        store(k).wait()
 
 
 def finish(final, gw2, gw1_t, sums, width, grad_scale):
-    steps = 10
-    wide = final.shape[1] // steps
-    channels, units = gw1_t.shape
+    channels = gw1_t.shape[0]
     vmem = pl.BlockSpec(memory_space=pltpu.VMEM)
-    last = 7
+    anywhere = pl.BlockSpec(memory_space=pl.ANY)
     return pl.pallas_call(
         functools.partial(finish_kernel, grad_scale),
-        grid=(steps,),
         out_shape=(
             jax.ShapeDtypeStruct((HALVES * LANES, final.shape[1]), jnp.bfloat16),
             jax.ShapeDtypeStruct(gw2.shape, jnp.float32),
@@ -606,20 +755,18 @@
             jax.ShapeDtypeStruct((1, width), jnp.float32),
             jax.ShapeDtypeStruct((1, width), jnp.float32),
         ),
-        in_specs=[
-            pl.BlockSpec((HALVES, wide, LANES), lambda k: (0, k, 0)),
-            pl.BlockSpec((gw2.shape[0] // 8, width), lambda k: (jnp.minimum(k, last), 0)),
-            pl.BlockSpec((channels // steps, units), lambda k: (k, 0)),
-            vmem,
+        in_specs=[anywhere, anywhere, anywhere, vmem],
+        out_specs=(anywhere, anywhere, anywhere, vmem, vmem, vmem),
+        scratch_shapes=[
+            pltpu.VMEM(final.shape, jnp.bfloat16),
+            pltpu.VMEM((HALVES * LANES, final.shape[1]), jnp.bfloat16),
+            pltpu.VMEM(gw2.shape, jnp.bfloat16),
+            pltpu.VMEM(gw2.shape, jnp.float32),
+            pltpu.VMEM(gw1_t.shape, jnp.bfloat16),
+            pltpu.VMEM(gw1_t.shape, jnp.float32),
+            pltpu.SemaphoreType.DMA((STEPS + 2,)),
+            pltpu.SemaphoreType.DMA((STEPS + 2,)),
         ],
-        out_specs=(
-            pl.BlockSpec((HALVES * LANES, wide), lambda k: (0, k)),
-            pl.BlockSpec((gw2.shape[0] // 8, width), lambda k: (jnp.minimum(k, last), 0)),
-            pl.BlockSpec((channels // steps, units), lambda k: (k, 0)),
-            vmem,
-            vmem,
-            vmem,
-        ),
         compiler_params=pltpu.CompilerParams(vmem_limit_bytes=VMEM_LIMIT),
         name="finish",
     )(final, gw2, gw1_t, sums)
@@ -633,15 +780,17 @@
     back_part, gw2, bias = down(out_grad, w_down, pre_act)
     gw2 = lax.psum_scatter(gw2, "ctx", scatter_dimension=0, tiled=True)
     normed_t = normed.T
-    norm_t, gw1 = up(back_part, w_up.T, normed_t, ctx_count)
+    gain = ln_gain
+    norm_t, gw1, stats = up(back_part, w_up.T, normed_t, gain, ctx_count, owner_map.shape[1])
     gw1 = lax.psum_scatter(gw1, "ctx", scatter_dimension=0, tiled=True)
     sums, final = hand_over(
         norm_t,
         normed_t,
-        ln_gain[:, None],
+        gain,
         inverse_std[None, :],
         owner_map,
         bias,
+        stats,
         float(normed.shape[1] * tp_count),
         grad_scale,
         ctx_count,

time: 212 us -> 205 us (0.967)
  Pallas kernels: 196 us -> 190 us
    pallas_call x1, Pallas kernels: 10.9 us -> 7.5 us  [finish(): pl.pallas_call(functools.partial(finish_kernel, grad_scale), out_shape=(j...]
  transfers between devices with their start and end apart: 2 -> 2, of which waited for: 0 -> 0; matrix products, arithmetic and copies ran while one was open for 0% -> 0% of each run, Pallas kernels for 62% -> 63%
where the time goes in v5:
time: 205 us
  Pallas kernels  190 us (93%)
  between operations  14.1 us (7%)
    pallas_call x1, Pallas kernels, hand_over(): pl.pallas_call(functools.partial(hand_kernel, full_width, grad_scale), ou...  75.8 us
    pallas_call x1, Pallas kernels, down(): pl.pallas_call(down_kernel, out_shape=(jax.ShapeDtypeStruct((rows, hid),...  54.2 us
    pallas_call x1, Pallas kernels, up(): pl.pallas_call(up_kernel, out_shape=(jax.ShapeDtypeStruct((channels, rows...  52.7 us
    pallas_call x1, Pallas kernels, finish(): pl.pallas_call(functools.partial(finish_kernel, grad_scale), out_shape=(j...  7.5 us
  transfers between devices with their start and end apart: 2, of which 0 were waited for; matrix products, arithmetic and copies ran while one was open for 0% of the time, Pallas kernels for 63%

profile of v5, /device:TPU:0, one launch (start us, length us, event | category | flops | bytes accessed | tf_op | source)
XLA Modules:
  0.0 204.7 jit_solution(14521207007356574420)
XLA Ops:
  7.2 0.0 reduce-scatter.3.cloned.1.call-start
  7.2 54.2 %down_gather.1 = (bf16[1024,256]{1,0:T(8,128)(2,1)}, bf16[4096,256]{1,0:T(8,128)(2,1)}, f32[2,256]{1,0:T(2,128)}) custom-call(bf16[1024,256]{1,0:T(8,128)(2,1)} %grad_ref.1, bf16[4096,256]{1,0:T(8,128)(2,1)} %w_hbm.1, bf16[1024,256]{1,0:T(8,128)(2,1)} %pre_ref.1), custom_call_target="tpu_custom_call" | custom-call | tf_op jit(solution)/shard_map/down_gather/pallas_call | solution.py:228
  61.4 0.0 reduce-scatter.3.cloned.1.call-update
  61.4 0.2 reduce-scatter.5.cloned.1.call-start
  61.7 52.7 %up_gather.1 = (f32[800,1024]{1,0:T(8,128)}, bf16[8,800,512]{2,1,0:T(8,128)(2,1)}, f32[8,256]{1,0:T(8,128)}) custom-call(bf16[1024,256]{1,0:T(8,128)(2,1)} %get-tuple-element.20.part_ref, bf16[800,4096]{1,0:T(8,128)(2,1)} %bitcast.11, bf16[800,1024]{1,0:T(8,128)(2,1)} %bitcast.7, f32[800]{0:T(1024)} %gain_row.1), custom_call_target="tpu_custom_call" | custom-call | flops 13421772800 | bytes 20971520 | tf_op jit(solution)/shard_map/up_gather/pallas_call | solution.py:342
  114.4 0.0 reduce-scatter.5.cloned.1.call-update
  114.4 75.8 %hand_over.1 = (f32[8,1024]{1,0:T(8,128)}, bf16[2,12800,128]{2,1,0:T(8,128)(2,1)}) custom-call(f32[800,1024]{1,0:T(8,128)} %get-tuple-element.21.norm_hbm, bf16[800,1024]{1,0:T(8,128)(2,1)} %bitcast.8, f32[800]{0:T(1024)} %gain_row.1, f32[1,1024]{1,0:T(1,128)} %bitcast.10, s32[1,4]{1,0:T(1,128)} %owner_ref.1, f32[2,256]{1,0:T(2,128)} %get-tuple-element.22.bias_ref, ...), custom_call_target="tpu_custom_call" | custom-call | flops 16384000 | bytes 209715200 | tf_op jit(solution)/shard_map/hand_over/pallas_call | solution.py:634
  190.3 0.0 reduce-scatter.3.cloned.1.call-done.gw2_hbm
  190.3 0.0 reduce-scatter.5.cloned.1.call-done
  190.3 7.5 %finish.1 = (bf16[256,12800]{1,0:T(8,128)(2,1)}, f32[512,256]{1,0:T(8,128)}, f32[800,512]{1,0:T(8,128)}, f32[2,800]{1,0:T(2,128)}, f32[1,256]{1,0:T(1,128)}, /*index=5*/f32[1,256]{1,0:T(1,128)}) custom-call(bf16[2,12800,128]{2,1,0:T(8,128)(2,1)} %get-tuple-element.24.final_hbm, bf16[512,256]{1,0:T(8,128)(2,1)} %reduce-scatter.3.cloned.1.call-done.gw2_hbm, ...), custom_call_target="tpu_custom_call" | custom-call | tf_op jit(solution)/shard_map/finish/pallas_call | solution.py:748
Async XLA Ops:
  7.2 183.1 %reduce-scatter.3.cloned.1.call-start = ((), (), s32[]{:S(2)}) async-start(), calls=%async_computation.2 | async-start | bytes 2359296 | tf_op jit(solution)/shard_map/reduce_scatter | solution.py:781
  61.4 128.9 %reduce-scatter.5.cloned.1.call-start = ((), (), s32[]{:S(2)}) async-start(), calls=%async_computation.3 | async-start | bytes 7372800 | tf_op jit(solution)/shard_map/reduce_scatter | solution.py:785
Sparse Core Ops, SparseCore 0:
  61.5 32.6 reduce-scatter.2
  114.6 43.5 reduce-scatter.4

commit v6 on v5

--- a/solution.py
+++ b/solution.py
@@ -38,16 +38,19 @@
     )
 
 
-def around(half, me):
-    t = Torus(half, me)
-    return ((t.along + 1, t.cross), (t.along + SIDE - 1, t.cross))
-
-
-def greet(targets):
+def greet(half_targets):
     barrier = pltpu.get_barrier_semaphore()
-    for target in targets:
+    for target in half_targets:
         pl.semaphore_signal(barrier, inc=1, device_id={"tp": target}, device_id_type=MESH)
-    pl.semaphore_wait(barrier, len(targets))
+
+
+def met(count):
+    pl.semaphore_wait(pltpu.get_barrier_semaphore(), count)
+
+
+def peers(me, steps):
+    torus = [Torus(half, me) for half in range(2)]
+    return [t.place(t.along + d, t.cross) for t in torus for d in steps]
 
 
 class Torus:
@@ -172,18 +175,39 @@
     lax.fori_loop(0, TP - 1, drain, 0)
 
 
-def down_kernel(
-    grad_ref, w_hbm, pre_ref, part_ref, gw2_hbm, bias_ref, full_ref, w_ref, total, gw2, short, hidden, slope, w_sem, out_sem, send_sem, recv_sem
+def gather_kernel(
+    full_width, grad_ref, pre_ref, gain_ref, w_down_hbm, w_up_hbm, normed_hbm, norm_hbm, weight_hbm, mean_ref, bias_ref,
+    grads, parts, w_down, w_up, normed, total, hidden, slope, gw2, norm, gw1, short, column, stats_y, stats_z,
+    load_sem, out_sem, down_send, down_recv, up_send, up_recv, stat_send, stat_recv,
 ):
     me = lax.axis_index("tp")
-    load = pltpu.make_async_copy(w_hbm, w_ref, w_sem)
-    load.start()
-    full_ref[me] = grad_ref[...]
-    greet([Torus(half, me).place(*at) for half in range(2) for at in around(half, me)])
+    greet(peers(me, (1, 2, 3)))
+    loads = [
+        pltpu.make_async_copy(source, target, load_sem.at[i])
+        for i, (source, target) in enumerate(((w_down_hbm, w_down), (w_up_hbm, w_up), (normed_hbm, normed)))
+    ]
+    for load in loads:
+        load.start()
+    grads[me] = grad_ref[...]
+    met(6)
     rows_all, width = grad_ref.shape
     quarter = rows_all // QUARTERS
-
-    def prepare():
+    per_owner = gw1.shape[2] // width
+    channels = norm.shape[0]
+    chunk = channels // 5
+    images = mean_ref.shape[0] // 2
+    image_rows = rows_all // images
+
+    def block_of(ref, origin, first, count):
+        within = pl.ds(pl.multiple_of(origin % per_owner * width, width), width)
+        return ref.at[origin // per_owner, pl.ds(first, count), within]
+
+    def write_down(origin):
+        return pltpu.make_async_copy(
+            block_of(short, origin, 0, width), block_of(weight_hbm, origin, channels, width), out_sem.at[0, origin]
+        )
+
+    def prepare_down():
         def rows_of(i, carry):
             rows = pl.ds(pl.multiple_of(i * 64, 64), 64)
             value, steep = gelu_parts(pre_ref[rows, :].astype(jnp.float32))
@@ -195,180 +219,160 @@
         bias_ref[0:1, :] = jnp.sum(grad_ref[...].astype(jnp.float32), axis=0, keepdims=True)
         total[...] = jnp.zeros_like(total)
         gw2[...] = jnp.zeros_like(gw2)
-        load.wait()
-
-    def consume(origin, part):
+        loads[0].wait()
+
+    def consume_down(origin, part):
         rows = pl.ds(part * quarter, quarter)
         features = pl.ds(pl.multiple_of(origin * width, width), width)
-        block = full_ref[origin, rows, :]
-        total[rows, :] += dot(block, w_ref[features, :])
+        block = grads[origin, rows, :]
+        total[rows, :] += dot(block, w_down[features, :])
         gw2[features, :] += row_product(block, hidden[rows, :])
 
-    def write(origin):
+    def complete_down(origin):
         features = pl.ds(pl.multiple_of(origin * width, width), width)
-        return pltpu.make_async_copy(short.at[features], gw2_hbm.at[features], out_sem.at[origin])
-
-    def complete(origin):
-        features = pl.ds(pl.multiple_of(origin * width, width), width)
-        short[features, :] = gw2[features, :].astype(jnp.bfloat16)
-        write(origin).start()
-
-    tree_gather(prepare, me, full_ref, send_sem, recv_sem, consume, complete)
+        block_of(short, origin, 0, width)[...] = gw2[features, :].astype(jnp.bfloat16)
+        write_down(origin).start()
+
+    tree_gather(prepare_down, me, grads, down_send, down_recv, consume_down, complete_down)
     part = (total[...] * slope[...]).astype(jnp.bfloat16)
-    part_ref[...] = part
-    bias_ref[1:2, :] = jnp.sum(part.astype(jnp.float32), axis=0, keepdims=True)
+    parts[me] = part
+
+    def write_up(origin):
+        return pltpu.make_async_copy(
+            block_of(short, origin, 0, channels), block_of(weight_hbm, origin, 0, channels), out_sem.at[1, origin]
+        )
+
+    def prepare_up():
+        bias_ref[1:2, :] = jnp.sum(parts[me].astype(jnp.float32), axis=0, keepdims=True)
+        norm[...] = jnp.zeros_like(norm)
+        gw1[...] = jnp.zeros_like(gw1)
+        gain_column(gain_ref, column)
+        for origin in range(TP):
+            write_down(origin).wait()
+        for load in loads[1:]:
+            load.wait()
+
+    def consume_up(origin, part):
+        rows = pl.ds(part * quarter, quarter)
+        units = pl.ds(pl.multiple_of(origin * width, width), width)
+        within = pl.ds(pl.multiple_of(origin % per_owner * width, width), width)
+        block = parts[origin, rows, :]
+        norm[:, rows] += dot_last(w_up[:, units], block)
+        gw1[origin // per_owner, :, within] += dot(normed[:, rows], block)
+
+    def complete_up(origin):
+        within = pl.ds(pl.multiple_of(origin % per_owner * width, width), width)
+        owner = origin // per_owner
+
+        def some(k, carry):
+            part = pl.ds(pl.multiple_of(k * chunk, chunk), chunk)
+            short[owner, part, within] = gw1[owner, part, within].astype(jnp.bfloat16)
+            return carry
+
+        lax.fori_loop(0, 5, some, 0)
+        write_up(origin).start()
+
+    tree_gather(prepare_up, me, parts, up_send, up_recv, consume_up, complete_up)
+    store = pltpu.make_async_copy(norm, norm_hbm, load_sem.at[0])
+    store.start()
+
+    for i in range(images):
+        rows = pl.ds(i * image_rows, image_rows)
+
+        def some(k, carry):
+            part = pl.ds(pl.multiple_of(k * chunk, chunk), chunk)
+            feature = normed[part, rows].astype(jnp.float32)
+            gained = column[part, :] * norm[part, rows]
+            return (
+                carry[0] + jnp.sum(gained, axis=0, keepdims=True),
+                carry[1] + jnp.sum(gained * feature, axis=0, keepdims=True),
+            )
+
+        zero = jnp.zeros((1, image_rows), jnp.float32)
+        first, second = lax.fori_loop(0, 5, some, (zero, zero))
+        stats_y[0, i : i + 1, :] = first
+        stats_y[0, images + i : images + i + 1, :] = second
+
+    def stat_copy(half, d):
+        buffer = (stats_y, stats_z)[half]
+        return pltpu.make_async_remote_copy(
+            src_ref=buffer.at[0],
+            dst_ref=buffer.at[d],
+            send_sem=stat_send.at[half, d - 1],
+            recv_sem=stat_recv.at[half, d - 1],
+            device_id={"tp": peers(me, (d,))[half]},
+            device_id_type=MESH,
+        )
+
+    for d in range(1, SIDE):
+        stat_copy(0, d).start()
+    for d in range(1, SIDE):
+        stat_copy(0, d).wait_recv()
+    stats_z[0] = stats_y[0] + stats_y[1] + stats_y[2] + stats_y[3]
+    for d in range(1, SIDE):
+        stat_copy(1, d).start()
+    store.wait()
     for origin in range(TP):
-        write(origin).wait()
-
-
-def down(out_grad, w_down, pre_act):
+        write_up(origin).wait()
+    for d in range(1, SIDE):
+        stat_copy(1, d).wait_recv()
+    mean_ref[...] = (stats_z[0] + stats_z[1] + stats_z[2] + stats_z[3]) * (1.0 / full_width)
+    for half in range(2):
+        for d in range(1, SIDE):
+            stat_copy(half, d).wait_send()
+
+
+def gather(out_grad, pre_act, gain, w_down, w_up_t, normed_t, ctx_count, images, full_width):
     rows, width = out_grad.shape
-    features, hid = w_down.shape
+    channels, units = w_up_t.shape
+    features = w_down.shape[0]
     vmem = pl.BlockSpec(memory_space=pltpu.VMEM)
+    anywhere = pl.BlockSpec(memory_space=pl.ANY)
+    dma = pltpu.SemaphoreType.DMA
+    each = units // ctx_count
     return pl.pallas_call(
-        down_kernel,
+        functools.partial(gather_kernel, full_width),
         out_shape=(
-            jax.ShapeDtypeStruct((rows, hid), jnp.bfloat16),
-            jax.ShapeDtypeStruct((features, hid), jnp.bfloat16),
-            jax.ShapeDtypeStruct((2, hid), jnp.float32),
+            jax.ShapeDtypeStruct((channels, rows), jnp.float32),
+            jax.ShapeDtypeStruct((ctx_count, channels + width, each), jnp.bfloat16),
+            jax.ShapeDtypeStruct((2 * images, rows // images), jnp.float32),
+            jax.ShapeDtypeStruct((2, width), jnp.float32),
         ),
-        in_specs=[vmem, pl.BlockSpec(memory_space=pl.ANY), vmem],
-        out_specs=(vmem, pl.BlockSpec(memory_space=pl.ANY), vmem),
+        in_specs=[vmem, vmem, vmem, anywhere, anywhere, anywhere],
+        out_specs=(anywhere, anywhere, vmem, vmem),
         scratch_shapes=[
             pltpu.VMEM((TP, rows, width), jnp.bfloat16),
-            pltpu.VMEM((features, hid), jnp.bfloat16),
-            pltpu.VMEM((rows, hid), jnp.float32),
-            pltpu.VMEM((features, hid), jnp.float32),
-            pltpu.VMEM((features, hid), jnp.bfloat16),
-            pltpu.VMEM((rows, hid), jnp.bfloat16),
-            pltpu.VMEM((rows, hid), jnp.float32),
-            pltpu.SemaphoreType.DMA,
-            pltpu.SemaphoreType.DMA((TP,)),
-            pltpu.SemaphoreType.DMA((QUARTERS, TP - 1)),
-            pltpu.SemaphoreType.DMA((QUARTERS, TP - 1)),
+            pltpu.VMEM((TP, rows, width), jnp.bfloat16),
+            pltpu.VMEM((features, width), jnp.bfloat16),
+            pltpu.VMEM((channels, units), jnp.bfloat16),
+            pltpu.VMEM((channels, rows), jnp.bfloat16),
+            pltpu.VMEM((rows, width), jnp.float32),
+            pltpu.VMEM((rows, width), jnp.bfloat16),
+            pltpu.VMEM((rows, width), jnp.float32),
+            pltpu.VMEM((features, width), jnp.float32),
+            pltpu.VMEM((channels, rows), jnp.float32),
+            pltpu.VMEM((ctx_count, channels, each), jnp.float32),
+            pltpu.VMEM((ctx_count, channels, each), jnp.bfloat16),
+            pltpu.VMEM((channels, 1), jnp.float32),
+            pltpu.VMEM((SIDE, 2 * images, rows // images), jnp.float32),
+            pltpu.VMEM((SIDE, 2 * images, rows // images), jnp.float32),
+            dma((3,)),
+            dma((2, TP)),
+            dma((QUARTERS, TP - 1)),
+            dma((QUARTERS, TP - 1)),
+            dma((QUARTERS, TP - 1)),
+            dma((QUARTERS, TP - 1)),
+            dma((2, SIDE - 1)),
+            dma((2, SIDE - 1)),
         ],
         compiler_params=pltpu.CompilerParams(
             collective_id=0, has_side_effects=True, vmem_limit_bytes=VMEM_LIMIT
         ),
-        name="down_gather",
-    )(out_grad, w_down, pre_act)
-
-
-def up_kernel(
-    part_ref, w_hbm, normed_hbm, gain_ref, norm_hbm, gw1_hbm, stat_ref,
-    full_ref, w_ref, normed_ref, norm_ref, gw1, short, column, w_sem, out_sem, send_sem, recv_sem,
-):
-    me = lax.axis_index("tp")
-    loads = [
-        pltpu.make_async_copy(w_hbm, w_ref, w_sem.at[0]),
-        pltpu.make_async_copy(normed_hbm, normed_ref, w_sem.at[1]),
-    ]
-    for load in loads:
-        load.start()
-    full_ref[me] = part_ref[...]
-    greet([Torus(half, me).place(*at) for half in range(2) for at in around(half, me)])
-    rows_all, width = part_ref.shape
-    quarter = rows_all // QUARTERS
-    per_owner = gw1.shape[2] // width
-    channels = norm_ref.shape[0]
-    chunk = channels // 5
-    images = stat_ref.shape[0] // 2
-    image_rows = rows_all // images
-
-    def prepare():
-        norm_ref[...] = jnp.zeros_like(norm_ref)
-        gw1[...] = jnp.zeros_like(gw1)
-        gain_column(gain_ref, column)
-        for load in loads:
-            load.wait()
-
-    def consume(origin, part):
-        rows = pl.ds(part * quarter, quarter)
-        units = pl.ds(pl.multiple_of(origin * width, width), width)
-        within = pl.ds(pl.multiple_of(origin % per_owner * width, width), width)
-        block = full_ref[origin, rows, :]
-        norm_ref[:, rows] += dot_last(w_ref[:, units], block)
-        gw1[origin // per_owner, :, within] += dot(normed_ref[:, rows], block)
-
-    def write(origin):
-        within = pl.ds(pl.multiple_of(origin % per_owner * width, width), width)
-        owner = origin // per_owner
-        return pltpu.make_async_copy(
-            short.at[owner, :, within], gw1_hbm.at[owner, :, within], out_sem.at[origin]
-        )
-
-    def complete(origin):
-        within = pl.ds(pl.multiple_of(origin % per_owner * width, width), width)
-        owner = origin // per_owner
-
-        def some(k, carry):
-            part = pl.ds(pl.multiple_of(k * chunk, chunk), chunk)
-            short[owner, part, within] = gw1[owner, part, within].astype(jnp.bfloat16)
-            return carry
-
-        lax.fori_loop(0, 5, some, 0)
-        write(origin).start()
-
-    tree_gather(prepare, me, full_ref, send_sem, recv_sem, consume, complete)
-    store = pltpu.make_async_copy(norm_ref, norm_hbm, w_sem.at[0])
-    store.start()
-
-    for i in range(images):
-        rows = pl.ds(i * image_rows, image_rows)
-
-        def some(k, carry):
-            part = pl.ds(pl.multiple_of(k * chunk, chunk), chunk)
-            feature = normed_ref[part, rows].astype(jnp.float32)
-            gained = column[part, :] * norm_ref[part, rows]
-            return (
-                carry[0] + jnp.sum(gained, axis=0, keepdims=True),
-                carry[1] + jnp.sum(gained * feature, axis=0, keepdims=True),
-            )
-
-        zero = jnp.zeros((1, image_rows), jnp.float32)
-        first, second = lax.fori_loop(0, 5, some, (zero, zero))
-        stat_ref[i : i + 1, :] = first
-        stat_ref[images + i : images + i + 1, :] = second
-    store.wait()
-    for origin in range(TP):
-        write(origin).wait()
-
-
-def up(back_part, w_up_t, normed_t, gain, ctx_count, images):
-    rows, width = back_part.shape
-    channels, units = w_up_t.shape
-    vmem = pl.BlockSpec(memory_space=pltpu.VMEM)
-    anywhere = pl.BlockSpec(memory_space=pl.ANY)
-    return pl.pallas_call(
-        up_kernel,
-        out_shape=(
-            jax.ShapeDtypeStruct((channels, rows), jnp.float32),
-            jax.ShapeDtypeStruct((ctx_count, channels, units // ctx_count), jnp.bfloat16),
-            jax.ShapeDtypeStruct((2 * images, rows // images), jnp.float32),
+        cost_estimate=pl.CostEstimate(
+            flops=4 * rows * units * (channels + width), bytes_accessed=30 * 2**20, transcendentals=0
         ),
-        in_specs=[vmem, anywhere, anywhere, vmem],
-        out_specs=(anywhere, anywhere, vmem),
-        scratch_shapes=[
-            pltpu.VMEM((TP, rows, width), jnp.bfloat16),
-            pltpu.VMEM((channels, units), jnp.bfloat16),
-            pltpu.VMEM((channels, rows), jnp.bfloat16),
-            pltpu.VMEM((channels, rows), jnp.float32),
-            pltpu.VMEM((ctx_count, channels, units // ctx_count), jnp.float32),
-            pltpu.VMEM((ctx_count, channels, units // ctx_count), jnp.bfloat16),
-            pltpu.VMEM((channels, 1), jnp.float32),
-            pltpu.SemaphoreType.DMA((2,)),
-            pltpu.SemaphoreType.DMA((TP,)),
-            pltpu.SemaphoreType.DMA((QUARTERS, TP - 1)),
-            pltpu.SemaphoreType.DMA((QUARTERS, TP - 1)),
-        ],
-        compiler_params=pltpu.CompilerParams(
-            collective_id=1, has_side_effects=True, vmem_limit_bytes=VMEM_LIMIT
-        ),
-        cost_estimate=pl.CostEstimate(
-            flops=4 * rows * units * channels, bytes_accessed=20 * 2**20, transcendentals=0
-        ),
-        name="up_gather",
-    )(back_part, w_up_t, normed_t, gain)
+        name="gather",
+    )(out_grad, pre_act, gain, w_down, w_up_t, normed_t)
 
 
 HALVES = 2
@@ -376,7 +380,6 @@
 
 
 def hand_kernel(
-    full_width,
     grad_scale,
     norm_hbm,
     normed_hbm,
@@ -384,7 +387,7 @@
     std_ref,
     owner_ref,
     bias_ref,
-    stat_ref,
+    mean_ref,
     sum_ref,
     final,
     own_y, next_y, far_y, prev_y,
@@ -394,10 +397,8 @@
     normed_ref,
     gain_ref,
     product,
-    stats_y,
-    stats_z,
     sums,
-    load_sem, near_send, near_recv, relay_send, relay_recv, cross_send, cross_recv, own_sem, stat_send, stat_recv, sum_send, sum_recv,
+    load_sem, near_send, near_recv, relay_send, relay_recv, cross_send, cross_recv, own_sem, sum_send, sum_recv,
 ):
     me = lax.axis_index("tp")
     group = lax.axis_index("ctx")
@@ -429,20 +430,7 @@
     ]
     for load in loads:
         load.start()
-    stats_y[0] = stat_ref[...]
     gain_column(gain_row, gain_ref)
-    pl.semaphore_wait(barrier, HALVES * (SIDE - 1) + ctx_count - 1)
-
-    def stat_copy(half, d):
-        buffer = (stats_y, stats_z)[half]
-        return pltpu.make_async_remote_copy(
-            src_ref=buffer.at[0],
-            dst_ref=buffer.at[d],
-            send_sem=stat_send.at[half, d - 1],
-            recv_sem=stat_recv.at[half, d - 1],
-            device_id={"tp": along_peer(half, d)},
-            device_id_type=MESH,
-        )
 
     def sum_copy(d):
         return pltpu.make_async_remote_copy(
@@ -453,19 +441,6 @@
             device_id={"ctx": (group + d) % ctx_count},
             device_id_type=MESH,
         )
-
-    for d in range(1, SIDE):
-        stat_copy(0, d).start()
-    for d in range(1, SIDE):
-        stat_copy(0, d).wait_recv()
-    stats_z[0] = stats_y[0] + stats_y[1] + stats_y[2] + stats_y[3]
-    for d in range(1, SIDE):
-        stat_copy(1, d).start()
-    for d in range(1, SIDE):
-        stat_copy(1, d).wait_recv()
-    for load in loads:
-        load.wait()
-    means = (stats_z[0] + stats_z[1] + stats_z[2] + stats_z[3]) * (1.0 / full_width)
 
     def near(half, sign, pair):
         piece = pl.ds(pair * (images // 2), images // 2)
@@ -506,9 +481,11 @@
             device_id_type=MESH,
         )
 
+    for load in loads:
+        load.wait()
     for i in range(images):
         rows = pl.ds(i * image_rows, image_rows)
-        mean_first, mean_second = means[i : i + 1, :], means[images + i : images + i + 1, :]
+        mean_first, mean_second = mean_ref[i : i + 1, :], mean_ref[images + i : images + i + 1, :]
         inverse = std_ref[:, rows]
 
         def visual(k, carry):
@@ -521,6 +498,8 @@
             return carry
 
         lax.fori_loop(0, 5, visual, 0)
+        if i == 1:
+            pl.semaphore_wait(barrier, HALVES * (SIDE - 1) + ctx_count - 1)
         if i % 2:
             for half in range(HALVES):
                 near(half, 1, i // 2).start()
@@ -617,14 +596,13 @@
                 near(half, sign, pair).wait_send()
             relay(half, sign).wait_send()
         for d in range(1, SIDE):
-            stat_copy(half, d).wait_send()
             for e in range(SIDE):
                 across(half, d, e).wait_send()
     for d in range(1, ctx_count):
         sum_copy(d).wait_send()
 
 
-def hand_over(norm_t, normed_t, gain, inverse_std, owner_map, bias, stats, full_width, grad_scale, ctx_count):
+def hand_over(norm_t, normed_t, gain, inverse_std, owner_map, bias, means, grad_scale, ctx_count):
     channels, rows = norm_t.shape
     images = owner_map.shape[1]
     image_rows = rows // images
@@ -632,7 +610,7 @@
     block = pltpu.VMEM((images, channels, LANES), jnp.bfloat16)
     dma = pltpu.SemaphoreType.DMA
     return pl.pallas_call(
-        functools.partial(hand_kernel, full_width, grad_scale),
+        functools.partial(hand_kernel, grad_scale),
         out_shape=(
             jax.ShapeDtypeStruct((8, 1024), jnp.float32),
             jax.ShapeDtypeStruct((HALVES, TP * channels, LANES), jnp.bfloat16),
@@ -654,8 +632,6 @@
             pltpu.VMEM((channels, rows), jnp.bfloat16),
             pltpu.VMEM((channels, 1), jnp.float32),
             pltpu.VMEM((channels, image_rows), jnp.float32),
-            pltpu.VMEM((SIDE, 2 * images, image_rows), jnp.float32),
-            pltpu.VMEM((SIDE, 2 * images, image_rows), jnp.float32),
             pltpu.VMEM((ctx_count, 8, 1024), jnp.float32),
             dma((2,)),
             dma((HALVES, 2, 2)),
@@ -665,33 +641,28 @@
             dma((HALVES, SIDE - 1, SIDE)),
             dma((HALVES, SIDE - 1, SIDE)),
             dma((HALVES, SIDE)),
-            dma((HALVES, SIDE - 1)),
-            dma((HALVES, SIDE - 1)),
             dma((ctx_count - 1,)),
             dma((ctx_count - 1,)),
         ],
         compiler_params=pltpu.CompilerParams(
-            collective_id=2, has_side_effects=True, vmem_limit_bytes=VMEM_LIMIT
+            collective_id=1, has_side_effects=True, vmem_limit_bytes=VMEM_LIMIT
         ),
         cost_estimate=pl.CostEstimate(
             flops=20 * rows * channels, bytes_accessed=200 * 2**20, transcendentals=0
         ),
         name="hand_over",
-    )(norm_t, normed_t, gain, inverse_std, owner_map, bias, stats)
+    )(norm_t, normed_t, gain, inverse_std, owner_map, bias, means)
 
 
 STEPS = 10
 
 
 def finish_kernel(
-    grad_scale, final_hbm, gw2_hbm, gw1_hbm, sum_ref, out_hbm, grad_w2_hbm, grad_w1_hbm, ln_ref, up_ref, down_ref,
-    final, out, gw2, grad_w2, gw1, grad_w1, in_sem, out_sem,
+    grad_scale, final_hbm, weight_hbm, sum_ref, out_hbm, grad_w2_hbm, grad_w1_hbm, ln_ref, up_ref, down_ref,
+    final, out, weight, grad_w2, grad_w1, in_sem, out_sem,
 ):
     wide = final.shape[1] // STEPS
-    small_in = [
-        pltpu.make_async_copy(gw2_hbm, gw2, in_sem.at[STEPS]),
-        pltpu.make_async_copy(gw1_hbm, gw1, in_sem.at[STEPS + 1]),
-    ]
+    small_in = pltpu.make_async_copy(weight_hbm, weight, in_sem.at[STEPS])
     small_out = [
         pltpu.make_async_copy(grad_w2, grad_w2_hbm, out_sem.at[STEPS]),
         pltpu.make_async_copy(grad_w1, grad_w1_hbm, out_sem.at[STEPS + 1]),
@@ -707,8 +678,7 @@
 
     load(0).start()
     load(1).start()
-    for copy in small_in:
-        copy.start()
+    small_in.start()
     for k in range(2, STEPS):
         load(k).start()
     lanes = out.shape[0]
@@ -725,11 +695,16 @@
         return carry
 
     lax.fori_loop(0, STEPS // 2, turn, 0)
-    for copy in small_in:
-        copy.wait()
-    grad_w2[...] = gw2[...].astype(jnp.float32) * grad_scale
+    small_in.wait()
+    channels = grad_w1.shape[0]
+    tall, width = grad_w2.shape
+    for i in range(tall * width // ((weight.shape[0] - channels) * width)):
+        part = weight.shape[0] - channels
+        grad_w2[i * part : (i + 1) * part, :] = (
+            weight[channels:, i * width : (i + 1) * width].astype(jnp.float32) * grad_scale
+        )
     small_out[0].start()
-    grad_w1[...] = gw1[...].astype(jnp.float32) * grad_scale
+    grad_w1[...] = weight[:channels, :].astype(jnp.float32) * grad_scale
     small_out[1].start()
     lax.fori_loop(STEPS // 2, STEPS, turn, 0)
     ln_ref[...] = sum_ref[0:2, 0 : ln_ref.shape[1]]
@@ -741,35 +716,35 @@
         store(k).wait()
 
 
-def finish(final, gw2, gw1_t, sums, width, grad_scale):
-    channels = gw1_t.shape[0]
+def finish(final, weight, sums, width, grad_scale):
+    each = weight.shape[1]
+    channels = weight.shape[0] - width
     vmem = pl.BlockSpec(memory_space=pltpu.VMEM)
     anywhere = pl.BlockSpec(memory_space=pl.ANY)
     return pl.pallas_call(
         functools.partial(finish_kernel, grad_scale),
         out_shape=(
             jax.ShapeDtypeStruct((HALVES * LANES, final.shape[1]), jnp.bfloat16),
-            jax.ShapeDtypeStruct(gw2.shape, jnp.float32),
-            jax.ShapeDtypeStruct(gw1_t.shape, jnp.float32),
+            jax.ShapeDtypeStruct((each, width), jnp.float32),
+            jax.ShapeDtypeStruct((channels, each), jnp.float32),
             jax.ShapeDtypeStruct((2, channels), jnp.float32),
             jax.ShapeDtypeStruct((1, width), jnp.float32),
             jax.ShapeDtypeStruct((1, width), jnp.float32),
         ),
-        in_specs=[anywhere, anywhere, anywhere, vmem],
+        in_specs=[anywhere, anywhere, vmem],
         out_specs=(anywhere, anywhere, anywhere, vmem, vmem, vmem),
         scratch_shapes=[
             pltpu.VMEM(final.shape, jnp.bfloat16),
             pltpu.VMEM((HALVES * LANES, final.shape[1]), jnp.bfloat16),
-            pltpu.VMEM(gw2.shape, jnp.bfloat16),
-            pltpu.VMEM(gw2.shape, jnp.float32),
-            pltpu.VMEM(gw1_t.shape, jnp.bfloat16),
-            pltpu.VMEM(gw1_t.shape, jnp.float32),
-            pltpu.SemaphoreType.DMA((STEPS + 2,)),
+            pltpu.VMEM(weight.shape, jnp.bfloat16),
+            pltpu.VMEM((each, width), jnp.float32),
+            pltpu.VMEM((channels, each), jnp.float32),
+            pltpu.SemaphoreType.DMA((STEPS + 1,)),
             pltpu.SemaphoreType.DMA((STEPS + 2,)),
         ],
         compiler_params=pltpu.CompilerParams(vmem_limit_bytes=VMEM_LIMIT),
         name="finish",
-    )(final, gw2, gw1_t, sums)
+    )(final, weight, sums)
 
 
 def per_device(out_grad, pre_act, normed, inverse_std, w_up, w_down, ln_gain, owner_map):
@@ -777,12 +752,20 @@
     tp_count = lax.axis_size("tp")
     row_count = out_grad.shape[0]
     grad_scale = float(row_count * ctx_count) ** (-0.5)
-    back_part, gw2, bias = down(out_grad, w_down, pre_act)
-    gw2 = lax.psum_scatter(gw2, "ctx", scatter_dimension=0, tiled=True)
+    gain = ln_gain
     normed_t = normed.T
-    gain = ln_gain
-    norm_t, gw1, stats = up(back_part, w_up.T, normed_t, gain, ctx_count, owner_map.shape[1])
-    gw1 = lax.psum_scatter(gw1, "ctx", scatter_dimension=0, tiled=True)
+    norm_t, weight, means, bias = gather(
+        out_grad,
+        pre_act,
+        gain,
+        w_down,
+        w_up.T,
+        normed_t,
+        ctx_count,
+        owner_map.shape[1],
+        float(normed.shape[1] * tp_count),
+    )
+    weight = lax.psum_scatter(weight, "ctx", scatter_dimension=0, tiled=True)
     sums, final = hand_over(
         norm_t,
         normed_t,
@@ -790,13 +773,12 @@
         inverse_std[None, :],
         owner_map,
         bias,
-        stats,
-        float(normed.shape[1] * tp_count),
+        means,
         grad_scale,
         ctx_count,
     )
     vit_grad, grad_w2, grad_w1_t, ln_grads, bias_up, bias_down = finish(
-        final, gw2, gw1[0], sums, bias.shape[1], grad_scale
+        final, weight[0], sums, bias.shape[1], grad_scale
     )
     return (grad_w2, grad_w1_t.T, bias_up[0], bias_down[0], ln_grads, vit_grad)
 

time: 205 us -> 201 us (0.980)
  Pallas kernels: 190 us -> 187 us
    pallas_call x3 -> x2, Pallas kernels: 183 us -> 180 us  [the longest x1 110 us: gather(): pl.pallas_call(functools.partial(gather_kernel, full_width), out_shape=(j...]
  transfers between devices with their start and end apart: 2 -> 1, of which waited for: 0 -> 0; matrix products, arithmetic and copies ran while one was open for 0% -> 0% of each run, Pallas kernels for 63% -> 35%
where the time goes in v6:
time: 201 us
  Pallas kernels  187 us (93%)
  between operations  14.1 us (7%)
    pallas_call x1, Pallas kernels, gather(): pl.pallas_call(functools.partial(gather_kernel, full_width), out_shape=(j...  110 us
    pallas_call x1, Pallas kernels, hand_over(): pl.pallas_call(functools.partial(hand_kernel, grad_scale), out_shape=(jax...  70 us
    pallas_call x1, Pallas kernels, finish(): pl.pallas_call(functools.partial(finish_kernel, grad_scale), out_shape=(j...  7.49 us
  transfers between devices with their start and end apart: 1, of which 0 were waited for; matrix products, arithmetic and copies ran while one was open for 0% of the time, Pallas kernels for 35%

profile of v6, /device:TPU:0, one launch (start us, length us, event | category | flops | bytes accessed | tf_op | source)
XLA Modules:
  0.0 201.2 jit_solution(2764523581983419597)
XLA Ops:
  7.2 0.0 reduce-scatter.2.cloned.1.call-start
  7.2 109.6 %gather.1 = (f32[800,1024]{1,0:T(8,128)}, bf16[8,1056,512]{2,1,0:T(8,128)(2,1)}, f32[8,256]{1,0:T(8,128)}, f32[2,256]{1,0:T(2,128)}) custom-call(bf16[1024,256]{1,0:T(8,128)(2,1)} %grad_ref.1, bf16[1024,256]{1,0:T(8,128)(2,1)} %pre_ref.1, f32[800]{0:T(1024)} %gain_row.1, bf16[4096,256]{1,0:T(8,128)(2,1)} %w_down_hbm.1, bf16[800,4096]{1,0:T(8,128)(2,1)} %bitcast.11, ...), custom_call_target="tpu_custom_call" | custom-call | flops 17716740096 | bytes 31457280 | tf_op jit(solution)/shard_map/gather/pallas_call | solution.py:333
  116.8 0.0 reduce-scatter.2.cloned.1.call-update
  116.8 70.0 %hand_over.1 = (f32[8,1024]{1,0:T(8,128)}, bf16[2,12800,128]{2,1,0:T(8,128)(2,1)}) custom-call(f32[800,1024]{1,0:T(8,128)} %get-tuple-element.18.norm_hbm, bf16[800,1024]{1,0:T(8,128)(2,1)} %bitcast.8, f32[800]{0:T(1024)} %gain_row.1, f32[1,1024]{1,0:T(1,128)} %bitcast.10, s32[1,4]{1,0:T(1,128)} %owner_ref.1, f32[2,256]{1,0:T(2,128)} %get-tuple-element.19.bias_ref, ...), custom_call_target="tpu_custom_call" | custom-call | flops 16384000 | bytes 209715200 | tf_op jit(solution)/shard_map/hand_over/pallas_call | solution.py:612
  186.8 0.0 reduce-scatter.2.cloned.1.call-done
  186.8 7.5 %finish.1 = (bf16[256,12800]{1,0:T(8,128)(2,1)}, f32[512,256]{1,0:T(8,128)}, f32[800,512]{1,0:T(8,128)}, f32[2,800]{1,0:T(2,128)}, f32[1,256]{1,0:T(1,128)}, /*index=5*/f32[1,256]{1,0:T(1,128)}) custom-call(bf16[2,12800,128]{2,1,0:T(8,128)(2,1)} %get-tuple-element.21.final_hbm, bf16[1056,512]{1,0:T(8,128)(2,1)} %bitcast.9, f32[8,1024]{1,0:T(8,128)} %get-tuple-element.23.sum_ref), custom_call_target="tpu_custom_call" | custom-call | tf_op jit(solution)/shard_map/finish/pallas_call | solution.py:724
Async XLA Ops:
  7.2 179.6 %reduce-scatter.2.cloned.1.call-start = ((), (), s32[]{:S(2)}) async-start(), calls=%async_computation.1 | async-start | bytes 9732096 | tf_op jit(solution)/shard_map/reduce_scatter | solution.py:768
Sparse Core Ops, SparseCore 0:
  116.9 55.2 reduce-scatter.1

commit v7 on v6

--- a/solution.py
+++ b/solution.py
@@ -172,7 +172,7 @@
             copy(quarter, (0, 0), k, (1, 0)).wait_send()
         return carry
 
-    lax.fori_loop(0, TP - 1, drain, 0)
+    return lambda: lax.fori_loop(0, TP - 1, drain, 0)
 
 
 def gather_kernel(
@@ -233,7 +233,7 @@
         block_of(short, origin, 0, width)[...] = gw2[features, :].astype(jnp.bfloat16)
         write_down(origin).start()
 
-    tree_gather(prepare_down, me, grads, down_send, down_recv, consume_down, complete_down)
+    drain_down = tree_gather(prepare_down, me, grads, down_send, down_recv, consume_down, complete_down)
     part = (total[...] * slope[...]).astype(jnp.bfloat16)
     parts[me] = part
 
@@ -272,7 +272,7 @@
         lax.fori_loop(0, 5, some, 0)
         write_up(origin).start()
 
-    tree_gather(prepare_up, me, parts, up_send, up_recv, consume_up, complete_up)
+    drain_up = tree_gather(prepare_up, me, parts, up_send, up_recv, consume_up, complete_up)
     store = pltpu.make_async_copy(norm, norm_hbm, load_sem.at[0])
     store.start()
 
@@ -311,6 +311,8 @@
     stats_z[0] = stats_y[0] + stats_y[1] + stats_y[2] + stats_y[3]
     for d in range(1, SIDE):
         stat_copy(1, d).start()
+    drain_down()
+    drain_up()
     store.wait()
     for origin in range(TP):
         write_up(origin).wait()
@@ -654,7 +656,7 @@
     )(norm_t, normed_t, gain, inverse_std, owner_map, bias, means)
 
 
-STEPS = 10
+STEPS = 4
 
 
 def finish_kernel(

time: 201 us -> 201 us (level)
  no operation moved by 1% of the time
where the time goes in v7:
time: 201 us; the launch traced here: 200 us
  Pallas kernels  186 us (93%)
  between operations  14.1 us (7%)
    pallas_call x1, Pallas kernels, gather(): pl.pallas_call(functools.partial(gather_kernel, full_width), out_shape=(j...  109 us
    pallas_call x1, Pallas kernels, hand_over(): pl.pallas_call(functools.partial(hand_kernel, grad_scale), out_shape=(jax...  70 us
    pallas_call x1, Pallas kernels, finish(): pl.pallas_call(functools.partial(finish_kernel, grad_scale), out_shape=(j...  7.08 us
  transfers between devices with their start and end apart: 1, of which 0 were waited for; matrix products, arithmetic and copies ran while one was open for 0% of the time, Pallas kernels for 35%

profile of v7, /device:TPU:0, one launch (start us, length us, event | category | flops | bytes accessed | tf_op | source)
XLA Modules:
  0.0 200.5 jit_solution(5915119137181262624)
XLA Ops:
  7.2 0.0 reduce-scatter.2.cloned.1.call-start
  7.2 109.3 %gather.1 = (f32[800,1024]{1,0:T(8,128)}, bf16[8,1056,512]{2,1,0:T(8,128)(2,1)}, f32[8,256]{1,0:T(8,128)}, f32[2,256]{1,0:T(2,128)}) custom-call(bf16[1024,256]{1,0:T(8,128)(2,1)} %grad_ref.1, bf16[1024,256]{1,0:T(8,128)(2,1)} %pre_ref.1, f32[800]{0:T(1024)} %gain_row.1, bf16[4096,256]{1,0:T(8,128)(2,1)} %w_down_hbm.1, bf16[800,4096]{1,0:T(8,128)(2,1)} %bitcast.11, ...), custom_call_target="tpu_custom_call" | custom-call | flops 17716740096 | bytes 31457280 | tf_op jit(solution)/shard_map/gather/pallas_call | solution.py:335
  116.5 0.0 reduce-scatter.2.cloned.1.call-update
  116.5 70.0 %hand_over.1 = (f32[8,1024]{1,0:T(8,128)}, bf16[2,12800,128]{2,1,0:T(8,128)(2,1)}) custom-call(f32[800,1024]{1,0:T(8,128)} %get-tuple-element.18.norm_hbm, bf16[800,1024]{1,0:T(8,128)(2,1)} %bitcast.8, f32[800]{0:T(1024)} %gain_row.1, f32[1,1024]{1,0:T(1,128)} %bitcast.10, s32[1,4]{1,0:T(1,128)} %owner_ref.1, f32[2,256]{1,0:T(2,128)} %get-tuple-element.19.bias_ref, ...), custom_call_target="tpu_custom_call" | custom-call | flops 16384000 | bytes 209715200 | tf_op jit(solution)/shard_map/hand_over/pallas_call | solution.py:614
  186.5 0.0 reduce-scatter.2.cloned.1.call-done
  186.5 7.1 %finish.1 = (bf16[256,12800]{1,0:T(8,128)(2,1)}, f32[512,256]{1,0:T(8,128)}, f32[800,512]{1,0:T(8,128)}, f32[2,800]{1,0:T(2,128)}, f32[1,256]{1,0:T(1,128)}, /*index=5*/f32[1,256]{1,0:T(1,128)}) custom-call(bf16[2,12800,128]{2,1,0:T(8,128)(2,1)} %get-tuple-element.21.final_hbm, bf16[1056,512]{1,0:T(8,128)(2,1)} %bitcast.9, f32[8,1024]{1,0:T(8,128)} %get-tuple-element.23.sum_ref), custom_call_target="tpu_custom_call" | custom-call | tf_op jit(solution)/shard_map/finish/pallas_call | solution.py:726
Async XLA Ops:
  7.2 179.3 %reduce-scatter.2.cloned.1.call-start = ((), (), s32[]{:S(2)}) async-start(), calls=%async_computation.1 | async-start | bytes 9732096 | tf_op jit(solution)/shard_map/reduce_scatter | solution.py:770
Sparse Core Ops, SparseCore 0:
  116.6 55.2 reduce-scatter.1

commit v8 on v7

--- a/solution.py
+++ b/solution.py
@@ -66,8 +66,8 @@
 
 QUARTERS = 4
 ARRIVALS = (
-    (3, 0), (1, 0), (0, 3), (2, 0), (3, 3), (1, 3), (0, 1), (2, 3),
-    (3, 1), (0, 2), (1, 1), (3, 2), (2, 1), (1, 2), (2, 2),
+    (3, 0), (1, 0), (0, 3), (0, 1), (2, 0), (3, 3), (3, 1), (1, 3),
+    (1, 1), (0, 2), (2, 3), (2, 1), (3, 2), (1, 2), (2, 2),
 )
 
 

time: 201 us -> 200 us (level)
  no operation moved by 1% of the time
where the time goes in v8:
time: 200 us
  Pallas kernels  186 us (93%)
  between operations  14.1 us (7%)
    pallas_call x1, Pallas kernels, gather(): pl.pallas_call(functools.partial(gather_kernel, full_width), out_shape=(j...  109 us
    pallas_call x1, Pallas kernels, hand_over(): pl.pallas_call(functools.partial(hand_kernel, grad_scale), out_shape=(jax...  69.9 us
    pallas_call x1, Pallas kernels, finish(): pl.pallas_call(functools.partial(finish_kernel, grad_scale), out_shape=(j...  7.08 us
  transfers between devices with their start and end apart: 1, of which 0 were waited for; matrix products, arithmetic and copies ran while one was open for 0% of the time, Pallas kernels for 35%

profile of v8, /device:TPU:0, one launch (start us, length us, event | category | flops | bytes accessed | tf_op | source)
XLA Modules:
  0.0 199.8 jit_solution(15578380857826973008)
XLA Ops:
  7.2 0.0 reduce-scatter.2.cloned.1.call-start
  7.2 108.6 %gather.1 = (f32[800,1024]{1,0:T(8,128)}, bf16[8,1056,512]{2,1,0:T(8,128)(2,1)}, f32[8,256]{1,0:T(8,128)}, f32[2,256]{1,0:T(2,128)}) custom-call(bf16[1024,256]{1,0:T(8,128)(2,1)} %grad_ref.1, bf16[1024,256]{1,0:T(8,128)(2,1)} %pre_ref.1, f32[800]{0:T(1024)} %gain_row.1, bf16[4096,256]{1,0:T(8,128)(2,1)} %w_down_hbm.1, bf16[800,4096]{1,0:T(8,128)(2,1)} %bitcast.11, ...), custom_call_target="tpu_custom_call" | custom-call | flops 17716740096 | bytes 31457280 | tf_op jit(solution)/shard_map/gather/pallas_call | solution.py:335
  115.8 0.0 reduce-scatter.2.cloned.1.call-update
  115.8 69.9 %hand_over.1 = (f32[8,1024]{1,0:T(8,128)}, bf16[2,12800,128]{2,1,0:T(8,128)(2,1)}) custom-call(f32[800,1024]{1,0:T(8,128)} %get-tuple-element.18.norm_hbm, bf16[800,1024]{1,0:T(8,128)(2,1)} %bitcast.8, f32[800]{0:T(1024)} %gain_row.1, f32[1,1024]{1,0:T(1,128)} %bitcast.10, s32[1,4]{1,0:T(1,128)} %owner_ref.1, f32[2,256]{1,0:T(2,128)} %get-tuple-element.19.bias_ref, ...), custom_call_target="tpu_custom_call" | custom-call | flops 16384000 | bytes 209715200 | tf_op jit(solution)/shard_map/hand_over/pallas_call | solution.py:614
  185.8 0.0 reduce-scatter.2.cloned.1.call-done
  185.8 7.1 %finish.1 = (bf16[256,12800]{1,0:T(8,128)(2,1)}, f32[512,256]{1,0:T(8,128)}, f32[800,512]{1,0:T(8,128)}, f32[2,800]{1,0:T(2,128)}, f32[1,256]{1,0:T(1,128)}, /*index=5*/f32[1,256]{1,0:T(1,128)}) custom-call(bf16[2,12800,128]{2,1,0:T(8,128)(2,1)} %get-tuple-element.21.final_hbm, bf16[1056,512]{1,0:T(8,128)(2,1)} %bitcast.9, f32[8,1024]{1,0:T(8,128)} %get-tuple-element.23.sum_ref), custom_call_target="tpu_custom_call" | custom-call | tf_op jit(solution)/shard_map/finish/pallas_call | solution.py:726
Async XLA Ops:
  7.2 178.6 %reduce-scatter.2.cloned.1.call-start = ((), (), s32[]{:S(2)}) async-start(), calls=%async_computation.1 | async-start | bytes 9732096 | tf_op jit(solution)/shard_map/reduce_scatter | solution.py:770
Sparse Core Ops, SparseCore 0:
  116.0 55.1 reduce-scatter.1

commit v9 on v8

--- a/solution.py
+++ b/solution.py
@@ -553,6 +553,11 @@
         near(half, 3, 0).wait_recv()
         forward(half, 1)
 
+    for half in range(HALVES):
+        relay(half, 1).wait_recv()
+        relay(half, 3).wait_recv()
+        forward(half, 2)
+
     ones = jnp.ones((8, image_rows), jnp.float32)
     columns = [jnp.zeros((8, channels), jnp.float32)] * 2
     for i in range(images):
@@ -574,11 +579,6 @@
     sums[0, 2:4, 0 : bias_ref.shape[1]] = bias_ref[...]
     for d in range(1, ctx_count):
         sum_copy(d).start()
-
-    for half in range(HALVES):
-        relay(half, 1).wait_recv()
-        relay(half, 3).wait_recv()
-        forward(half, 2)
 
     for d in range(1, ctx_count):
         sum_copy(d).wait_recv()

time: 200 us -> 200 us (level)
  no operation moved by 1% of the time
where the time goes in v9:
time: 200 us
  Pallas kernels  186 us (93%)
  between operations  14.1 us (7%)
    pallas_call x1, Pallas kernels, gather(): pl.pallas_call(functools.partial(gather_kernel, full_width), out_shape=(j...  109 us
    pallas_call x1, Pallas kernels, hand_over(): pl.pallas_call(functools.partial(hand_kernel, grad_scale), out_shape=(jax...  69.9 us
    pallas_call x1, Pallas kernels, finish(): pl.pallas_call(functools.partial(finish_kernel, grad_scale), out_shape=(j...  7.08 us
  transfers between devices with their start and end apart: 1, of which 0 were waited for; matrix products, arithmetic and copies ran while one was open for 0% of the time, Pallas kernels for 35%

profile of v9, /device:TPU:0, one launch (start us, length us, event | category | flops | bytes accessed | tf_op | source)
XLA Modules:
  0.0 199.8 jit_solution(10902444979399664121)
XLA Ops:
  7.2 0.0 reduce-scatter.2.cloned.1.call-start
  7.2 108.6 %gather.1 = (f32[800,1024]{1,0:T(8,128)}, bf16[8,1056,512]{2,1,0:T(8,128)(2,1)}, f32[8,256]{1,0:T(8,128)}, f32[2,256]{1,0:T(2,128)}) custom-call(bf16[1024,256]{1,0:T(8,128)(2,1)} %grad_ref.1, bf16[1024,256]{1,0:T(8,128)(2,1)} %pre_ref.1, f32[800]{0:T(1024)} %gain_row.1, bf16[4096,256]{1,0:T(8,128)(2,1)} %w_down_hbm.1, bf16[800,4096]{1,0:T(8,128)(2,1)} %bitcast.11, ...), custom_call_target="tpu_custom_call" | custom-call | flops 17716740096 | bytes 31457280 | tf_op jit(solution)/shard_map/gather/pallas_call | solution.py:335
  115.8 0.0 reduce-scatter.2.cloned.1.call-update
  115.8 69.9 %hand_over.1 = (f32[8,1024]{1,0:T(8,128)}, bf16[2,12800,128]{2,1,0:T(8,128)(2,1)}) custom-call(f32[800,1024]{1,0:T(8,128)} %get-tuple-element.18.norm_hbm, bf16[800,1024]{1,0:T(8,128)(2,1)} %bitcast.8, f32[800]{0:T(1024)} %gain_row.1, f32[1,1024]{1,0:T(1,128)} %bitcast.10, s32[1,4]{1,0:T(1,128)} %owner_ref.1, f32[2,256]{1,0:T(2,128)} %get-tuple-element.19.bias_ref, ...), custom_call_target="tpu_custom_call" | custom-call | flops 16384000 | bytes 209715200 | tf_op jit(solution)/shard_map/hand_over/pallas_call | solution.py:614
  185.8 0.0 reduce-scatter.2.cloned.1.call-done
  185.8 7.1 %finish.1 = (bf16[256,12800]{1,0:T(8,128)(2,1)}, f32[512,256]{1,0:T(8,128)}, f32[800,512]{1,0:T(8,128)}, f32[2,800]{1,0:T(2,128)}, f32[1,256]{1,0:T(1,128)}, /*index=5*/f32[1,256]{1,0:T(1,128)}) custom-call(bf16[2,12800,128]{2,1,0:T(8,128)(2,1)} %get-tuple-element.21.final_hbm, bf16[1056,512]{1,0:T(8,128)(2,1)} %bitcast.9, f32[8,1024]{1,0:T(8,128)} %get-tuple-element.23.sum_ref), custom_call_target="tpu_custom_call" | custom-call | tf_op jit(solution)/shard_map/finish/pallas_call | solution.py:726
Async XLA Ops:
  7.2 178.6 %reduce-scatter.2.cloned.1.call-start = ((), (), s32[]{:S(2)}) async-start(), calls=%async_computation.1 | async-start | bytes 9732096 | tf_op jit(solution)/shard_map/reduce_scatter | solution.py:770
Sparse Core Ops, SparseCore 0:
  116.0 53.7 reduce-scatter.1
